TPU v7x, 32 devices: a whole 2x2x4 slice. The times are simulated.
32 devices in a mesh: groups: 2 (over y), atoms: 8 (over z, x), waves: 2 (over core).
Axes of the slice: x: 2, y: 2, z: 4, core: 2. Of those that a mesh axis runs over, the one named last changes fastest.
Arguments:
- features: bfloat16 [8192, 256], P(('groups', 'atoms', 'waves')), parts along dimension 0, may hold values from -6 to 6
- positions: float32 [3, 8192], P(None, ('groups', 'atoms', 'waves')), parts along dimension 1, may hold values from 0 to 1, as said below
- distances: float32 [8192, 768], P(('groups', 'atoms', 'waves')), parts along dimension 0, may hold values from 0.5 to 5
- pair_mask: int32 [8192, 768], P(('groups', 'atoms', 'waves')), parts along dimension 0, may hold values 0 or 1
- counts: int32 [32], P(('groups', 'atoms', 'waves')), parts along dimension 0, may hold values from 128 to 256, as said below
- wave_index: int32 [3, 2048], P(None, ('groups', 'waves')), parts along dimension 1, may hold values from -6 to 6
- w_value: bfloat16 [256, 256], replicated, may hold values from -0.375 to 0.375
- filter_short: float32 [16, 256], replicated, may hold values from -1 to 1
- filter_long: float32 [16, 256], replicated, may hold values from -6 to 6
- gain: float32 [256], replicated, may hold values from 0.1 to 1.9
- w_inner: bfloat16 [256, 256], replicated, may hold values from -0.375 to 0.375
- w_outer: bfloat16 [256, 256], replicated, may hold values from -0.375 to 0.375
Outputs:
- updated: bfloat16 [8192, 256], P(('groups', 'atoms', 'waves')), parts along dimension 0
There are 2 independent parts, one for each index of `groups`. A program takes and returns all parts, laid end to end along the dimension named above; an argument that names none is the same for every part. Nothing has to cross between parts.
Inputs may be any that keep to these rules, and one draw needn't show every extreme that they name: The atoms of box b are its first counts[b] slots; in every draw some box is full. `positions`: fractional coordinates; the first coordinate of every slot of box b lies in [b / 16, (b + 1) / 16).
All inputs are finite; a program needn't handle non-finite values. No bound on the sum of `pair_mask` on one device may be relied on, other than what follows from the above.
Results may differ from a plain program's by a relative error of at most 0.015.
Values may be sent and summed in bfloat16 or wider, within the bound.
No kernel may reach another device: no remote copies, remote signals or barrier semaphores. Data moves between devices by JAX's collectives and lax.ppermute only.
A program may use at most 64 MiB of HBM per device.

v0:
```python
import jax
import jax.numpy as jnp
from jax import lax
from jax.sharding import PartitionSpec as P

radius_cut = 5.0
wave_top = 6.0 * 3.0**0.5


def padded(block, sides, width):
    for axis, dim in sides:
        count = lax.axis_size(axis)
        forward = [(i, i + 1) for i in range(count - 1)]
        forward.append((count - 1, 0))
        backward = [(target, source) for source, target in forward]
        low = lax.ppermute(
            lax.slice_in_dim(block, block.shape[dim] - width, None, axis=dim), axis, forward
        )
        high = lax.ppermute(lax.slice_in_dim(block, 0, width, axis=dim), axis, backward)
        block = jnp.concatenate([low, block, high], axis=dim)
    return block


def radial_tiles(distances, pair_mask, radial_count):
    centres = radius_cut * jnp.arange(radial_count, dtype=jnp.float32) / (radial_count - 1)
    spacing = radius_cut / (radial_count - 1)
    envelope = (
        0.5 * (jnp.cos(jnp.pi * distances / radius_cut) + 1.0) * pair_mask.astype(jnp.float32)
    )
    offsets = (distances[None] - centres[:, None, None]) / spacing
    tiles = jnp.exp(-0.5 * offsets * offsets) * envelope[None]
    return tiles.astype(jnp.bfloat16)


def phase_tiles(points, wave_index):
    waves = wave_index.astype(jnp.float32)
    theta = points[0][:, None] * waves[0][None, :] + points[1][:, None] * waves[1][None, :]
    theta = 2.0 * jnp.pi * (theta + points[2][:, None] * waves[2][None, :])
    return (jnp.cos(theta).astype(jnp.bfloat16), jnp.sin(theta).astype(jnp.bfloat16))


def wave_filter(wave_index, filter_long):
    waves = wave_index.astype(jnp.float32)
    radial_count = filter_long.shape[0]
    magnitude = jnp.sqrt(waves[0] * waves[0] + waves[1] * waves[1] + waves[2] * waves[2])
    centres = wave_top * jnp.arange(radial_count, dtype=jnp.float32) / (radial_count - 1)
    spacing = wave_top / (radial_count - 1)
    offsets = (magnitude[None, :] - centres[:, None]) / spacing
    k_basis = jnp.exp(-0.5 * offsets * offsets)
    return jnp.dot(k_basis.T, filter_long, precision=lax.Precision.HIGHEST)


def body(
    features,
    positions,
    distances,
    pair_mask,
    counts,
    wave_index,
    w_value,
    filter_short,
    filter_long,
    gain,
    w_inner,
    w_outer,
):
    row_count = features.shape[0]
    width = features.shape[1]
    radial_count = filter_short.shape[0]
    occupied = (lax.iota(jnp.int32, row_count) < counts[0]).astype(jnp.float32)
    values = (
        jnp.dot(features, w_value, preferred_element_type=jnp.float32) * occupied[:, None]
    ).astype(jnp.bfloat16)
    beside_all = padded(values, ((("atoms", "waves"), 0),), row_count)
    tiles = radial_tiles(distances, pair_mask, radial_count).reshape(
        radial_count * row_count, 3 * row_count
    )
    products = jnp.dot(tiles, beside_all, preferred_element_type=jnp.float32).reshape(
        radial_count, row_count, width
    )
    near_field = jnp.sum(products * filter_short[:, None, :], axis=0)
    wide_values, block_points = (
        lax.all_gather(values.astype(jnp.float32), "waves", axis=0, tiled=True),
        lax.all_gather(positions, "waves", axis=1, tiled=True),
    )
    block_values = wide_values.astype(jnp.bfloat16)
    cosine, sine = phase_tiles(block_points, wave_index)
    cos_sum = jnp.einsum("ak,af->kf", cosine, block_values, preferred_element_type=jnp.float32)
    sin_sum = jnp.einsum("ak,af->kf", sine, block_values, preferred_element_type=jnp.float32)
    atom_total = row_count * lax.axis_size(("atoms", "waves"))
    wave_total = wave_index.shape[1] * lax.axis_size("waves")
    factor_scale = float(atom_total) ** (-0.5)
    cos_total, sin_total = lax.psum((cos_sum, sin_sum), "atoms")
    block_filter = wave_filter(wave_index, filter_long)
    cos_filtered = (cos_total * block_filter * factor_scale).astype(jnp.bfloat16)
    sin_filtered = (sin_total * block_filter * factor_scale).astype(jnp.bfloat16)
    far_field = lax.psum_scatter(
        (
            jnp.dot(cosine, cos_filtered, preferred_element_type=jnp.float32)
            + jnp.dot(sine, sin_filtered, preferred_element_type=jnp.float32)
        ).astype(jnp.bfloat16),
        "waves",
        scatter_dimension=0,
        tiled=True,
    ).astype(jnp.float32) * float(wave_total) ** (-0.5)
    combined = features.astype(jnp.float32) + near_field + far_field
    normed = (
        combined * lax.rsqrt(jnp.mean(combined * combined, axis=-1, keepdims=True) + 1e-06) * gain
    ).astype(jnp.bfloat16)
    inner = jax.nn.silu(jnp.dot(normed, w_inner, preferred_element_type=jnp.float32)).astype(
        jnp.bfloat16
    )
    result = jnp.dot(inner, w_outer, preferred_element_type=jnp.float32) * occupied[:, None]
    return result.astype(jnp.bfloat16)


def solution(mesh):
    placed = (
        P(("groups", "atoms", "waves"), None),
        P(None, ("groups", "atoms", "waves")),
        P(("groups", "atoms", "waves"), None),
        P(("groups", "atoms", "waves"), None),
        P(("groups", "atoms", "waves")),
        P(None, ("groups", "waves")),
        P(),
        P(),
        P(),
        P(),
        P(),
        P(),
    )
    return jax.shard_map(
        body,
        mesh=mesh,
        in_specs=placed,
        out_specs=P(("groups", "atoms", "waves"), None),
        check_vma=False,
    )
```

profile of v0, /device:TPU:0, one launch (start us, length us, event | category | flops | bytes accessed | tf_op | source)
XLA Modules:
  0.0 131.1 jit_solution(18217226336184944433)
XLA Ops:
  6.5 0.0 copy-start
  6.5 0.0 copy-start.5
  6.5 0.0 all-reduce.3.cloned.1.call-start
  6.5 0.7 convert_element_type.63
  8.0 0.0 copy-done
  8.0 1.1 fusion.14
  9.1 2.1 %all_gather.7 = bf16[512,256]{1,0:T(8,128)(2,1)S(1)} all-gather(bf16[256,256]{1,0:T(8,128)(2,1)S(1)} %fusion.14), channel_id=1, replica_groups=mesh['groups'=2,'atoms'=8,'waves'=2] {'waves'}, dimensions={0}, use_global_device_ids=true | all-gather | bytes 393216 | tf_op jit(solution)/shard_map/all_gather | solution.py:83
  11.2 0.0 copy-done.5
  11.2 1.8 %all_gather.6 = f32[3,512]{1,0:T(4,128)S(1)} all-gather(f32[3,256]{1,0:T(4,128)S(1)} %copy-done.5), channel_id=1, replica_groups=mesh['groups'=2,'atoms'=8,'waves'=2] {'waves'}, dimensions={1}, use_global_device_ids=true | all-gather | bytes 9216 | tf_op jit(solution)/shard_map/all_gather | solution.py:84
  13.0 4.8 %fusion.20 = f32[512,256]{1,0:T(8,128)} fusion(f32[512]{0:T(512)S(1)} %bitcast.20, f32[512]{0:T(512)S(1)} %bitcast.36, f32[512]{0:T(512)S(1)} %bitcast.24, f32[512]{0:T(512)S(1)} %bitcast.40, f32[512]{0:T(512)S(1)} %bitcast.28, f32[512]{0:T(512)S(1)} %bitcast.32, bf16[512,256]{1,0:T(8,128)(2,1)S(1)} %all_gather.7), kind=kOutput, calls=%fused_computation.30 | convolution fusion | flops 136052736 | bytes 798720 | tf_op jit(solution)/shard_map/ak,af->kf/dot_general | solution.py:89
  17.9 4.8 %fusion.22 = f32[512,256]{1,0:T(8,128)} fusion(f32[512]{0:T(512)S(1)} %bitcast.21, f32[512]{0:T(512)S(1)} %bitcast.37, f32[512]{0:T(512)S(1)} %bitcast.25, f32[512]{0:T(512)S(1)} %bitcast.41, f32[512]{0:T(512)S(1)} %bitcast.29, f32[512]{0:T(512)S(1)} %bitcast.33, bf16[512,256]{1,0:T(8,128)(2,1)S(1)} %all_gather.7), kind=kOutput, calls=%fused_computation.32 | convolution fusion | flops 136052736 | bytes 798720 | tf_op jit(solution)/shard_map/ak,af->kf/dot_general | solution.py:88
  22.7 0.0 copy-start.4
  22.7 0.0 copy-start.1
  22.7 0.0 copy-start.2
  22.7 0.0 all-reduce.3.cloned.1.call-update
  22.7 0.0 reduce-scatter.2.cloned.1.call-start
  22.8 0.4 collective-permute-start
  23.2 5.5 %collective-permute-start.1 = (bf16[256,256]{1,0:T(8,128)(2,1)S(1)}, bf16[256,256]{1,0:T(8,128)(2,1)S(1)}, u32[]{:S(2)}, u32[]{:S(2)}) collective-permute-start(bf16[256,256]{1,0:T(8,128)(2,1)S(1)} %fusion.14), channel_id=1, source_target_pairs={{1,0},{2,1},{3,2},{4,3},{5,4},{6,5},{7,6},{8,7},{9,8},{10,9},{11,1... | collective-permute-start | bytes 393224 | tf_op jit(solution)/shard_map/ppermute | solution.py:19
  28.7 0.0 copy-done.4
  28.7 0.7 fusion.35
  29.4 0.0 copy-done.1
  29.4 0.0 copy-done.2
  29.4 2.7 %convert_multiply_fusion = f32[256,768]{1,0:T(8,128)S(1)} fusion(s32[256,768]{1,0:T(8,128)S(1)} %copy-done.1, f32[256,768]{1,0:T(8,128)S(1)} %copy-done.2), kind=kLoop, calls=%fused_computation.22 | loop fusion | flops 983040 | bytes 2359296 | tf_op jit(solution)/shard_map/mul | solution.py:28
  32.1 71.6 %all-reduce.3.cloned.1.call-done = (f32[512,256]{1,0:T(8,128)}, f32[512,256]{1,0:T(8,128)}) async-done(((f32[512,256]{1,0:T(8,128)}, f32[512,256]{1,0:T(8,128)}), (f32[512,256]{1,0:T(8,128)}, f32[512,256]{1,0:T(8,128)})) %all-reduce.3.cloned.1.call-update) | async-done | bytes 1048592 | tf_op jit(solution)/shard_map/psum | solution.py:93
  103.7 0.0 copy-start.6
  103.7 5.0 %fusion.21 = f32[512,256]{1,0:T(8,128)S(1)} fusion(f32[512]{0:T(512)S(1)} %bitcast.22, f32[512]{0:T(512)S(1)} %bitcast.38, f32[512]{0:T(512)S(1)} %bitcast.26, f32[512]{0:T(512)S(1)} %bitcast.42, f32[512]{0:T(512)S(1)} %bitcast.30, f32[512]{0:T(512)S(1)} %bitcast.34, f32[512,256]{1,0:T(8,128)} %get-tuple-element.5, f32[512,256]{1,0:T(8,128)S(1)} %fusion.35), kind=kOutput, calls=%fused_computation.31 | convolution fusion | flops 136445952 | bytes 1585152 | tf_op jit(solution)/shard_map/dot_general | solution.py:99
  108.7 0.0 copy-done.6
  108.7 0.0 copy-start.9
  108.7 4.9 %fusion.13 = bf16[512,256]{1,0:T(8,128)(2,1)} fusion(f32[512,256]{1,0:T(8,128)S(1)} %fusion.21, f32[512]{0:T(512)S(1)} %bitcast.23, f32[512]{0:T(512)S(1)} %bitcast.39, f32[512]{0:T(512)S(1)} %bitcast.27, f32[512]{0:T(512)S(1)} %bitcast.43, f32[512]{0:T(512)S(1)} %bitcast.31, f32[512]{0:T(512)S(1)} %bitcast.35, f32[512,256]{1,0:T(8,128)S(1)} %copy-done.6, ...), kind=kOutput, calls=%fused_computation.14 | convolution fusion | flops 136708096 | bytes 1847296 | tf_op jit(solution)/shard_map/dot_general | solution.py:100
  113.6 0.0 reduce-scatter.2.cloned.1.call-update
  113.7 0.0 copy-start.3
  113.7 0.0 copy-start.7
  113.7 0.0 copy-start.8
  113.7 0.0 copy-start.10
  113.7 0.0 collective-permute-done
  113.7 0.0 collective-permute-done.1
  113.7 0.0 copy-done.9
  113.7 3.9 %multiply_reduce_fusion = f32[256,256]{1,0:T(8,128)S(1)} fusion(f32[16,256]{1,0:T(8,128)S(1)} %copy-done.9, f32[256,768]{1,0:T(8,128)S(1)} %convert_multiply_fusion, f32[16]{0:T(128)S(1)} %iota_multiply_fusion.1, f32[256,768]{1,0:T(8,128)S(1)} %copy-done.2, bf16[256,256]{1,0:T(8,128)(2,1)S(1)} %collective-permute-done.1, bf16[256,256]{1,0:T(8,128)(2,1)S(1)} %fusion.14, ...), kind=kOutput, calls=%fused_computation.12 | convolution fusion | flops 1632698368 | bytes 2244672 | tf_op jit(solution)/shard_map/dot_general | solution.py:78
  117.6 3.6 %reduce-scatter.2.cloned.1.call-done = bf16[256,256]{1,0:T(8,128)(2,1)} async-done(((bf16[512,256]{1,0:T(8,128)(2,1)}), bf16[256,256]{1,0:T(8,128)(2,1)}) %reduce-scatter.2.cloned.1.call-update) | async-done | bytes 131088 | tf_op jit(solution)/shard_map/reduce_scatter | solution.py:97
  121.2 0.0 copy-done.3
  121.2 1.0 multiply_reduce_fusion.1
  122.3 0.0 copy-done.7
  122.3 0.0 copy-done.8
  122.3 0.0 copy-done.10
  122.3 2.0 %fusion.15 = bf16[256,256]{1,0:T(8,128)(2,1)} fusion(bf16[256,256]{1,0:T(8,128)(2,1)S(1)} %copy-done.7, bf16[256,256]{1,0:T(8,128)(2,1)S(1)} %copy-done.8, f32[256]{0:T(256)S(1)} %copy-done.10, f32[256]{0:T(256)S(1)} %add_rsqrt_fusion, f32[256]{0:T(256)S(1)} %compare_convert_fusion, bf16[256,256]{1,0:T(8,128)(2,1)} %reduce-scatter.2.cloned.1.call-done, ...), kind=kOutput, calls=%fused_computation.18 | convolution fusion | flops 68091904 | bytes 920576 | tf_op jit(solution)/shard_map/dot_general | solution.py:113
  (6 shorter events, 0.0 us)
Async XLA Ops:
  6.5 1.4 %copy-start = (bf16[256,256]{1,0:T(8,128)(2,1)S(1)}, bf16[256,256]{1,0:T(8,128)(2,1)}, u32[]{:S(2)}) copy-start(bf16[256,256]{1,0:T(8,128)(2,1)} %param.18) | copy-start | bytes 393220
  6.5 4.7 %copy-start.5 = (f32[3,256]{1,0:T(4,128)S(1)}, f32[3,256]{1,0:T(4,128)}, u32[]{:S(2)}) copy-start(f32[3,256]{1,0:T(4,128)} %param.13) | copy-start | bytes 9220
  6.5 97.2 %all-reduce.3.cloned.1.call-start = ((), (), s32[]{:S(2)}) async-start(), calls=%async_computation.2 | async-start | bytes 2097152 | tf_op jit(solution)/shard_map/psum | solution.py:93
  22.7 6.0 %copy-start.4 = (f32[16,256]{1,0:T(8,128)S(1)}, f32[16,256]{1,0:T(8,128)}, u32[]{:S(2)}) copy-start(f32[16,256]{1,0:T(8,128)} %param.20) | copy-start | bytes 49156
  22.7 6.7 %copy-start.1 = (s32[256,768]{1,0:T(8,128)S(1)}, s32[256,768]{1,0:T(8,128)}, u32[]{:S(2)}) copy-start(s32[256,768]{1,0:T(8,128)} %param.15) | copy-start | bytes 2359300
  22.7 6.7 %copy-start.2 = (f32[256,768]{1,0:T(8,128)S(1)}, f32[256,768]{1,0:T(8,128)}, u32[]{:S(2)}) copy-start(f32[256,768]{1,0:T(8,128)} %param.14) | copy-start | bytes 2359300
  22.7 98.5 %reduce-scatter.2.cloned.1.call-start = ((), (), s32[]{:S(2)}) async-start(), calls=%async_computation.1 | async-start | bytes 393216 | tf_op jit(solution)/shard_map/reduce_scatter | solution.py:97
  22.8 91.0 %collective-permute-start = (bf16[256,256]{1,0:T(8,128)(2,1)S(1)}, bf16[256,256]{1,0:T(8,128)(2,1)S(1)}, u32[]{:S(2)}, u32[]{:S(2)}) collective-permute-start(bf16[256,256]{1,0:T(8,128)(2,1)S(1)} %fusion.14), channel_id=1, source_target_pairs={{0,1},{1,2},{2,3},{3,4},{4,5},{5,6},{6,7},{7,8},{8,9},{9,10},{10,1... | collective-permute-start | bytes 393224 | tf_op jit(solution)/shard_map/ppermute | solution.py:16
  23.2 90.6 %collective-permute-start.1 = (bf16[256,256]{1,0:T(8,128)(2,1)S(1)}, bf16[256,256]{1,0:T(8,128)(2,1)S(1)}, u32[]{:S(2)}, u32[]{:S(2)}) collective-permute-start(bf16[256,256]{1,0:T(8,128)(2,1)S(1)} %fusion.14), channel_id=1, source_target_pairs={{1,0},{2,1},{3,2},{4,3},{5,4},{6,5},{7,6},{8,7},{9,8},{10,9},{11,1... | collective-permute-start | bytes 393224 | tf_op jit(solution)/shard_map/ppermute | solution.py:19
  103.7 5.0 %copy-start.6 = (f32[512,256]{1,0:T(8,128)S(1)}, f32[512,256]{1,0:T(8,128)}, u32[]{:S(2)}) copy-start(f32[512,256]{1,0:T(8,128)} %get-tuple-element.6) | copy-start | bytes 1572868
  108.7 5.0 %copy-start.9 = (f32[16,256]{1,0:T(8,128)S(1)}, f32[16,256]{1,0:T(8,128)}, u32[]{:S(2)}) copy-start(f32[16,256]{1,0:T(8,128)} %param.19) | copy-start | bytes 49156
  113.7 7.5 %copy-start.3 = (bf16[256,256]{1,0:T(8,128)(2,1)S(1)}, bf16[256,256]{1,0:T(8,128)(2,1)}, u32[]{:S(2)}) copy-start(bf16[256,256]{1,0:T(8,128)(2,1)} %param.12) | copy-start | bytes 393220
  113.7 8.6 %copy-start.7 = (bf16[256,256]{1,0:T(8,128)(2,1)S(1)}, bf16[256,256]{1,0:T(8,128)(2,1)}, u32[]{:S(2)}) copy-start(bf16[256,256]{1,0:T(8,128)(2,1)} %param.23) | copy-start | bytes 393220
  113.7 8.6 %copy-start.8 = (bf16[256,256]{1,0:T(8,128)(2,1)S(1)}, bf16[256,256]{1,0:T(8,128)(2,1)}, u32[]{:S(2)}) copy-start(bf16[256,256]{1,0:T(8,128)(2,1)} %param.22) | copy-start | bytes 393220
  113.7 8.6 %copy-start.10 = (f32[256]{0:T(256)S(1)}, f32[256]{0:T(256)}, u32[]{:S(2)}) copy-start(f32[256]{0:T(256)} %param.21) | copy-start | bytes 3076
Sparse Core Ops, SparseCore 0:
  22.8 80.8 all-reduce.2
  113.8 7.3 reduce-scatter.1
where the time goes:
time: 131 us
  waiting for transfers between devices  75.2 us (57%)
  matrix products  27.2 us (21%)
  between operations  14.2 us (11%)
  starting transfers between devices  5.96 us (5%)
  other arithmetic  4.51 us (3%)
  blocking collectives  3.94 us (3%)
    psum x1, waiting for transfers between devices, body(): cos_total, sin_total = lax.psum((cos_sum, sin_sum), 'atoms')  71.6 us
    ppermute x1, starting transfers between devices, padded(): lax.ppermute(lax.slice_in_dim(block, 0, width, axis=dim), axis, backward)  5.52 us
    dot_general x1, matrix products, body(): jnp.dot(cosine, cos_filtered, preferred_element_type=jnp.float32)  4.99 us
    dot_general x1, matrix products, body(): jnp.dot(sine, sin_filtered, preferred_element_type=jnp.float32)  4.93 us
    dot_general x1, matrix products, body(): jnp.einsum('ak,af->kf', sine, block_values, preferred_element_type=jnp.fl...  4.84 us
    dot_general x1, matrix products, body(): jnp.einsum('ak,af->kf', cosine, block_values, preferred_element_type=jnp....  4.82 us
    dot_general x1, matrix products, body(): jnp.dot(tiles, beside_all, preferred_element_type=jnp.float32)  3.85 us
    reduce_scatter x1, waiting for transfers between devices, body(): lax.psum_scatter((jnp.dot(cosine, cos_filtered, preferred_element_type=jn...  3.59 us
  transfers between devices with their start and end apart: 4, of which 2 were waited for; matrix products, arithmetic and copies ran while one was open for 13% of the time, Pallas kernels for 0%

commit v1 on v0

--- a/solution.py
+++ b/solution.py
@@ -1,10 +1,25 @@
+import functools
+import math
+
 import jax
 import jax.numpy as jnp
 from jax import lax
+from jax.experimental import pallas as pl
+from jax.experimental.pallas import tpu as pltpu
 from jax.sharding import PartitionSpec as P
 
 radius_cut = 5.0
 wave_top = 6.0 * 3.0**0.5
+both = ("atoms", "waves")
+gather_limit = 8
+extra_rows = 16
+
+sin_terms = (
+    2.641753992459813,
+    -1.08637674632807,
+    0.134005627536115,
+    -0.007739884914760742,
+)
 
 
 def padded(block, sides, width):
@@ -50,7 +65,7 @@
     return jnp.dot(k_basis.T, filter_long, precision=lax.Precision.HIGHEST)
 
 
-def body(
+def summed_body(
     features,
     positions,
     distances,
@@ -114,6 +129,443 @@
     return result.astype(jnp.bfloat16)
 
 
+def horner(terms, w):
+    total = jnp.full_like(w, terms[-1])
+    for term in terms[-2::-1]:
+        total = total * w + term
+    return total
+
+
+def phases(turns):
+    r = turns - jnp.round(turns)
+    quarter = r * horner(sin_terms, r * r)
+    square = quarter * quarter
+    rest = 2.0**1.5 - square
+    half_sin = quarter * (rest * lax.rsqrt(rest))
+    half_cos = 2.0**0.5 - square
+    return 1.0 - half_sin * half_sin, half_sin * half_cos
+
+
+def fill_phases(phase_ref, column, wave_ref, point_rows, step=64):
+    wave_count = wave_ref.shape[0]
+    width = point_rows.shape[1]
+    for low in range(0, wave_count, step):
+        turns = jnp.dot(
+            wave_ref[low : low + step, :], point_rows, preferred_element_type=jnp.float32
+        )
+        cosine, sine = phases(turns)
+        phase_ref[low : low + step, column : column + width] = cosine.astype(jnp.bfloat16)
+        phase_ref[wave_count + low : wave_count + low + step, column : column + width] = (
+            sine.astype(jnp.bfloat16)
+        )
+
+
+def add_sums(sums, chunks, wave_ref, phase_ref):
+    rows = chunks[0].shape[0] - extra_rows
+    for i in range(len(chunks) // 2):
+        first, second = chunks[2 * i], chunks[2 * i + 1]
+        slot = phase_ref.at[i % 2]
+        fill_phases(slot, 0, wave_ref, first[rows:, :])
+        fill_phases(slot, rows, wave_ref, second[rows:, :])
+        block_values = jnp.concatenate([first[:rows, :], second[:rows, :]], axis=0)
+        found = jnp.dot(slot[...], block_values, preferred_element_type=jnp.float32)
+        sums = found if sums is None else sums + found
+    return sums
+
+
+def fetch(sources, targets, semaphores):
+    copies = [
+        pltpu.make_async_copy(source, target, semaphores.at[i])
+        for i, (source, target) in enumerate(zip(sources, targets))
+    ]
+    for copy in copies:
+        copy.start()
+    for copy in copies:
+        copy.wait()
+
+
+def prepare_kernel(
+    features_hbm,
+    w_value_hbm,
+    positions_hbm,
+    count_hbm,
+    chunk_ref,
+    features,
+    w_value,
+    positions,
+    count_ref,
+    sems,
+):
+    fetch(
+        (features_hbm, w_value_hbm, positions_hbm, count_hbm),
+        (features, w_value, positions, count_ref),
+        sems,
+    )
+    rows = features.shape[0]
+    values = jnp.dot(features[...], w_value[...], preferred_element_type=jnp.float32)
+    row = lax.broadcasted_iota(jnp.int32, values.shape, 0)
+    chunk_ref[:rows, :] = jnp.where(row < count_ref[0], values, 0.0).astype(jnp.bfloat16)
+    points = positions[...]
+    high = points.astype(jnp.bfloat16).astype(jnp.float32)
+    middle = (points - high).astype(jnp.bfloat16).astype(jnp.float32)
+    low = points - high - middle
+    spare = jnp.zeros((extra_rows - 9, rows), jnp.float32)
+    chunk_ref[rows:, :] = jnp.concatenate([high, middle, low, spare], axis=0).astype(jnp.bfloat16)
+
+
+def waves_kernel(
+    scale, wave_hbm, filter_long_hbm, waves_ref, weights_ref, wave_ref, filter_long_ref, sems
+):
+    fetch((wave_hbm, filter_long_hbm), (wave_ref, filter_long_ref), sems)
+    waves = wave_ref[...].astype(jnp.float32)
+    spare = jnp.zeros((extra_rows - 9, waves.shape[1]), jnp.float32)
+    waves_ref[...] = jnp.concatenate([waves, waves, waves, spare], axis=0).T.astype(jnp.bfloat16)
+    radial_count = filter_long_ref.shape[0]
+    magnitude = jnp.sqrt(
+        waves[0:1] * waves[0:1] + waves[1:2] * waves[1:2] + waves[2:3] * waves[2:3]
+    )
+    spacing = wave_top / (radial_count - 1)
+    index = lax.broadcasted_iota(jnp.int32, (radial_count, waves.shape[1]), 0)
+    offsets = magnitude / spacing - index.astype(jnp.float32)
+    basis = jnp.exp(-0.5 * offsets * offsets)
+    weights_ref[...] = scale * jnp.dot(
+        basis.T,
+        filter_long_ref[...],
+        precision=lax.Precision.HIGHEST,
+        preferred_element_type=jnp.float32,
+    )
+
+
+def own_kernel(wave_ref, first_ref, second_ref, sums_ref, turned_ref, phase_ref):
+    sums_ref[...] = add_sums(None, (first_ref, second_ref), wave_ref, phase_ref)
+    turned_ref[...] = phase_ref[0].T
+
+
+def more_kernel(wave_ref, sums_in_ref, *refs):
+    chunks, (sums_ref, phase_ref) = refs[:-2], refs[-2:]
+    sums_ref[...] = add_sums(sums_in_ref[...], chunks, wave_ref, phase_ref)
+
+
+def weighted(products, rows, filter_ref):
+    radial_count = filter_ref.shape[0]
+    total = None
+    for k in range(radial_count):
+        m = k - radial_count // 2
+        term = products[k * rows : (k + 1) * rows, :] * (
+            filter_ref[k : k + 1, :] * math.exp(-0.5 * m * m)
+        )
+        total = term if total is None else total + term
+    return total
+
+
+def near_kernel(
+    distances_ref,
+    mask_ref,
+    filter_ref,
+    own_ref,
+    sibling_ref,
+    near_ref,
+    far_tiles_ref,
+    tiles_ref,
+    *,
+    step,
+    part=32,
+):
+    rows = distances_ref.shape[0]
+    radial_count = filter_ref.shape[0]
+    middle = radial_count // 2
+    sibling = 2 - 2 * lax.axis_index("waves")
+
+    def make(low, block, put):
+        start = block * rows if isinstance(block, int) else pl.multiple_of(block * rows, rows)
+        d = distances_ref[low : low + part, pl.ds(start, rows)]
+        mask = mask_ref[low : low + part, pl.ds(start, rows)].astype(jnp.float32)
+        u = d * (0.5 / radius_cut)
+        quarter = u * horner(sin_terms, u * u)
+        half = 1.0 - 0.5**0.5 * quarter * quarter
+        y = d * ((radial_count - 1) / radius_cut) - float(middle)
+        centre = half * half * mask * jnp.exp(-0.5 * y * y)
+        ratio = jnp.exp(y)
+        back = jnp.exp(-y)
+        put(middle, centre.astype(jnp.bfloat16))
+        value = centre
+        for k in range(middle + 1, radial_count):
+            value = value * ratio
+            put(k, value.astype(jnp.bfloat16))
+        value = centre
+        for k in range(middle - 1, -1, -1):
+            value = value * back
+            put(k, value.astype(jnp.bfloat16))
+
+    block_values = jnp.concatenate([own_ref[:rows, :], sibling_ref[:rows, :]], axis=0)
+
+    def products(i):
+        found = jnp.dot(tiles_ref[i % 2], block_values, preferred_element_type=jnp.float32)
+        near_ref[i * step : (i + 1) * step, :] = weighted(found, step, filter_ref)
+
+    for i in range(rows // step):
+        for low in range(i * step, (i + 1) * step, part):
+            inner = low - i * step
+
+            def put(column):
+                def store(k, value):
+                    at = k * step + inner
+                    tiles_ref[i % 2, at : at + part, column : column + rows] = value
+
+                return store
+
+            def put_far(k, value):
+                at = k * rows + low
+                far_tiles_ref[at : at + part, :] = value
+
+            make(low, 1, put(0))
+            make(low, sibling, put(rows))
+            make(low, 2 - sibling, put_far)
+        if i:
+            products(i - 1)
+    products(rows // step - 1)
+
+
+def beyond_kernel(nearby, near_in_ref, far_tiles_ref, filter_ref, *refs):
+    near_chunks, (near_ref, side_ref) = refs[:nearby], refs[nearby:]
+    rows = near_ref.shape[0]
+    blocks, block = lax.axis_size("atoms"), lax.axis_index("atoms")
+    side = lax.rem(block + 2 * lax.axis_index("waves") - 1 + blocks, blocks)
+    for mask, chunk in zip(near_masks(blocks), near_chunks):
+
+        @pl.when((block ^ side) == mask)
+        def _():
+            side_ref[...] = chunk[:rows, :]
+
+    found = jnp.dot(far_tiles_ref[...], side_ref[...], preferred_element_type=jnp.float32)
+    near_ref[...] = near_in_ref[...] + weighted(found, rows, filter_ref)
+
+
+def near_masks(blocks):
+    return sorted({a ^ ((a + 1) % blocks) for a in range(blocks)})
+
+
+def last_kernel(
+    wave_ref,
+    sums_in_ref,
+    weights_ref,
+    turned_ref,
+    *refs,
+):
+    chunks, (own_far_ref, message_ref, phase_ref) = refs[:-3], refs[-3:]
+    rows = own_far_ref.shape[0]
+    wave_count = wave_ref.shape[0]
+    sums = add_sums(sums_in_ref[...], chunks, wave_ref, phase_ref)
+    weights = weights_ref[...]
+    filtered = jnp.concatenate(
+        [
+            (sums[:wave_count, :] * weights).astype(jnp.bfloat16),
+            (sums[wave_count:, :] * weights).astype(jnp.bfloat16),
+        ],
+        axis=0,
+    )
+    far = jnp.dot(turned_ref[...], filtered, preferred_element_type=jnp.float32)
+    own_far_ref[...] = far[:rows, :]
+    message_ref[...] = far[rows:, :].astype(jnp.bfloat16)
+
+
+def update_kernel(
+    scale,
+    count_hbm,
+    features_ref,
+    near_ref,
+    own_far_ref,
+    message_ref,
+    gain_ref,
+    w_inner_ref,
+    w_outer_ref,
+    out_ref,
+    count_ref,
+    sem,
+):
+    copy = pltpu.make_async_copy(count_hbm, count_ref, sem)
+    copy.start()
+    far = (own_far_ref[...] + message_ref[...].astype(jnp.float32)) * scale
+    combined = features_ref[...].astype(jnp.float32) + near_ref[...] + far
+    spread = lax.rsqrt(jnp.mean(combined * combined, axis=-1, keepdims=True) + 1e-06)
+    normed = (combined * spread * gain_ref[...]).astype(jnp.bfloat16)
+    inner = jnp.dot(normed, w_inner_ref[...], preferred_element_type=jnp.float32)
+    inner = (inner / (1.0 + jnp.exp(-inner))).astype(jnp.bfloat16)
+    result = jnp.dot(inner, w_outer_ref[...], preferred_element_type=jnp.float32)
+    row = lax.broadcasted_iota(jnp.int32, result.shape, 0)
+    copy.wait()
+    out_ref[...] = jnp.where(row < count_ref[0], result, 0.0).astype(jnp.bfloat16)
+
+
+hbm = pl.BlockSpec(memory_space=pltpu.HBM)
+vmem = pl.BlockSpec(memory_space=pltpu.VMEM)
+
+
+def call(kernel, specs, outs, scratch=(), micros=1.0, mib=8):
+    shapes = tuple(jax.ShapeDtypeStruct(shape, dtype) for shape, dtype in outs)
+    return pl.pallas_call(
+        kernel,
+        in_specs=specs,
+        out_specs=tuple(vmem for _ in outs),
+        out_shape=shapes,
+        scratch_shapes=list(scratch),
+        cost_estimate=pl.CostEstimate(
+            flops=int(micros * 1.1e9), bytes_accessed=int(micros * 1e6), transcendentals=0
+        ),
+        compiler_params=pltpu.CompilerParams(vmem_limit_bytes=mib * 1024 * 1024),
+    )
+
+
+def gathered_parts(
+    features,
+    positions,
+    distances,
+    pair_mask,
+    counts,
+    wave_index,
+    w_value,
+    filter_short,
+    filter_long,
+    gain,
+    w_inner,
+    w_outer,
+):
+    rows, width = features.shape
+    radial_count = filter_short.shape[0]
+    wave_count = wave_index.shape[1]
+    blocks, cores = lax.axis_size("atoms"), lax.axis_size("waves")
+    bf16, f32 = jnp.bfloat16, jnp.float32
+
+    def across(mask):
+        return [
+            (a * cores + c, (a ^ mask) * cores + c) for a in range(blocks) for c in range(cores)
+        ]
+
+    over = [(a * cores + c, a * cores + 1 - c) for a in range(blocks) for c in range(cores)]
+
+    chunk_rows = rows + extra_rows
+    (chunk,) = call(
+        prepare_kernel,
+        [hbm, hbm, hbm, hbm],
+        [((chunk_rows, width), bf16)],
+        [
+            pltpu.VMEM(features.shape, features.dtype),
+            pltpu.VMEM(w_value.shape, w_value.dtype),
+            pltpu.VMEM(positions.shape, positions.dtype),
+            pltpu.SMEM(counts.shape, counts.dtype),
+            pltpu.SemaphoreType.DMA((4,)),
+        ],
+        micros=1.0,
+        mib=60,
+    )(features, w_value, positions, counts)
+    waves, wave_weights = call(
+        functools.partial(waves_kernel, float(rows * blocks * cores) ** -0.5),
+        [hbm, hbm],
+        [((wave_count, extra_rows), bf16), ((wave_count, width), f32)],
+        [
+            pltpu.VMEM(wave_index.shape, wave_index.dtype),
+            pltpu.VMEM(filter_long.shape, filter_long.dtype),
+            pltpu.SemaphoreType.DMA((2,)),
+        ],
+        micros=1.3,
+    )(wave_index, filter_long)
+
+    half = blocks // 2
+
+    def move(value, mask):
+        return lax.ppermute(value, both, across(mask))
+
+    got = {0: chunk, half: move(chunk, half)}
+    for mask in range(half - 1, 0, -1):
+        got[mask] = move(chunk, mask)
+    for mask in range(half - 1, 0, -1):
+        got[half ^ mask] = move(got[half], mask)
+    other = {}
+    for mask, value in got.items():
+        other[mask] = lax.ppermute(value, both, over)
+
+    sums_shape = ((2 * wave_count, width), f32)
+    phase_shape = (2 * wave_count, 2 * rows)
+    sums, turned = call(
+        own_kernel,
+        [vmem] * 3,
+        [sums_shape, (phase_shape[::-1], bf16)],
+        [pltpu.VMEM((1,) + phase_shape, bf16)],
+        micros=1.0,
+    )(waves, chunk, other[0])
+
+    step = rows // 4
+    near, far_tiles = call(
+        functools.partial(near_kernel, step=step),
+        [vmem] * 5,
+        [((rows, width), f32), ((radial_count * rows, rows), bf16)],
+        [pltpu.VMEM((2, radial_count * step, 2 * rows), bf16)],
+        micros=2.5,
+        mib=16,
+    )(distances, pair_mask, filter_short, chunk, other[0])
+
+    def pairs(masks):
+        return [c for mask in masks for c in (got[mask], other[mask])]
+
+    groups = sum_groups(blocks)
+    for masks in groups[:-1]:
+        (sums,) = call(
+            more_kernel,
+            [vmem] * (2 + 2 * len(masks)),
+            [sums_shape],
+            [pltpu.VMEM((min(2, len(masks)),) + phase_shape, bf16)],
+            micros=0.8 * len(masks) + 0.3,
+            mib=12,
+        )(waves, sums, *pairs(masks))
+    own_far, message = call(
+        last_kernel,
+        [vmem] * (4 + 2 * len(groups[-1])),
+        [((rows, width), f32), ((rows, width), bf16)],
+        [pltpu.VMEM((min(2, len(groups[-1])),) + phase_shape, bf16)],
+        micros=1.5,
+        mib=12,
+    )(waves, sums, wave_weights, turned, *pairs(groups[-1]))
+    message = lax.ppermute(message, both, over)
+    near_chunks = [other[m] for m in near_masks(blocks)]
+    (near,) = call(
+        functools.partial(beyond_kernel, len(near_chunks)),
+        [vmem] * (3 + len(near_chunks)),
+        [((rows, width), f32)],
+        [pltpu.VMEM((rows, width), bf16)],
+        micros=1.0,
+        mib=12,
+    )(near, far_tiles, filter_short, *near_chunks)
+    return call(
+        functools.partial(update_kernel, float(wave_count * cores) ** -0.5),
+        [hbm] + [vmem] * 7,
+        [((rows, width), bf16)],
+        [pltpu.SMEM(counts.shape, counts.dtype), pltpu.SemaphoreType.DMA],
+        micros=1.0,
+    )(counts, features, near, own_far, message, jnp.reshape(gain, (1, width)), w_inner, w_outer)[0]
+
+
+def gathered_body(*args):
+    return gathered_parts(*args)
+
+
+def move_masks(blocks):
+    half = blocks // 2
+    direct = list(range(half - 1, 0, -1))
+    return [half] + direct, [half ^ mask for mask in direct]
+
+
+def sum_groups(blocks):
+    starts, passed = move_masks(blocks)
+    order = starts[:1] + passed
+    groups = [starts[1:], order[:2]] + [[mask] for mask in order[2:]]
+    return [group for group in groups if group]
+
+
+def gathers(mesh):
+    blocks, cores = mesh.shape["atoms"], mesh.shape["waves"]
+    return cores == 2 and 2 <= blocks <= gather_limit and blocks & (blocks - 1) == 0
+
+
 def solution(mesh):
     placed = (
         P(("groups", "atoms", "waves"), None),
@@ -130,7 +582,7 @@
         P(),
     )
     return jax.shard_map(
-        body,
+        gathered_body if gathers(mesh) else summed_body,
         mesh=mesh,
         in_specs=placed,
         out_specs=P(("groups", "atoms", "waves"), None),

time: 131 us -> 38.8 us (0.30)
  waiting for transfers between devices: 75.2 us -> 9.88 us
  matrix products: 27.2 us -> 0 us
  Pallas kernels: 0 us -> 15.9 us
  between operations: 14.2 us -> 0.88 us
  starting transfers between devices: 5.96 us -> 11.8 us
  other arithmetic: 4.51 us -> 0 us
  blocking collectives: 3.94 us -> 0 us
    psum x1 -> x0, waiting for transfers between devices: 71.6 us -> none  [body(): cos_total, sin_total = lax.psum((cos_sum, sin_sum), 'atoms')]
    dot_general x8 -> x0, matrix products: 27.2 us -> none  [the longest x1 4.99 us: body(): jnp.dot(cosine, cos_filtered, preferred_element_type=jnp.float32)]
    pallas_call x0 -> x10, Pallas kernels: none -> 15.9 us  [the longest x3 6.15 us: gathered_parts(): call(more_kernel, [vmem] * (2 + 2 * len(masks)), [sums_shape], [pltpu.VME...]
    ppermute x2 -> x16, waiting for transfers between devices: 0.01 us -> 9.88 us  [the longest x7 9.85 us: move(): return lax.ppermute(value, both, across(mask))]
    ppermute x2 -> x16, starting transfers between devices: 5.92 us -> 11.8 us  [the longest x7 10.6 us: move(): return lax.ppermute(value, both, across(mask))]
    all_gather x2 -> x0, blocking collectives: 3.94 us -> none  [the longest x1 2.12 us: body(): lax.all_gather(values.astype(jnp.float32), 'waves', axis=0, tiled=True)]
    reduce_scatter x1 -> x0, waiting for transfers between devices: 3.59 us -> none  [body(): lax.psum_scatter((jnp.dot(cosine, cos_filtered, preferred_element_type=jn...]
    mul x1 -> x0, other arithmetic: 2.69 us -> none  [radial_tiles(): 0.5 * (jnp.cos(jnp.pi * distances / radius_cut) + 1.0)]
  transfers between devices with their start and end apart: 4 -> 16, of which waited for: 2 -> 6; matrix products, arithmetic and copies ran while one was open for 13% -> 0% of each run, Pallas kernels for 0% -> 29%
where the time goes in v1:
time: 38.8 us; the launch traced here: 38.7 us
  Pallas kernels  15.9 us (41%)
  starting transfers between devices  11.8 us (30%)
  waiting for transfers between devices  9.88 us (25%)
  between operations  0.88 us (2%)
    ppermute x7, starting transfers between devices, move(): return lax.ppermute(value, both, across(mask))  10.6 us
    ppermute x7, waiting for transfers between devices, move(): return lax.ppermute(value, both, across(mask))  9.85 us
    pallas_call x3, Pallas kernels, gathered_parts(): call(more_kernel, [vmem] * (2 + 2 * len(masks)), [sums_shape], [pltpu.VME...  6.15 us
    pallas_call x1, Pallas kernels, gathered_parts(): call(functools.partial(near_kernel, step=step), [vmem] * 5, [((rows, widt...  2.22 us
    pallas_call x1, Pallas kernels, gathered_parts(): call(prepare_kernel, [hbm, hbm, hbm, hbm], [((chunk_rows, width), bf16)],...  1.85 us
    pallas_call x1, Pallas kernels, gathered_parts(): call(last_kernel, [vmem] * (4 + 2 * len(groups[-1])), [((rows, width), f3...  1.56 us
    pallas_call x1, Pallas kernels, gathered_parts(): call(functools.partial(update_kernel, float(wave_count * cores) ** (-0.5)...  1.39 us
    pallas_call x1, Pallas kernels, gathered_parts(): call(own_kernel, [vmem] * 3, [sums_shape, (phase_shape[::-1], bf16)], [pl...  1.2 us
  transfers between devices with their start and end apart: 16, of which 6 were waited for; matrix products, arithmetic and copies ran while one was open for 0% of the time, Pallas kernels for 29%

profile of v1, /device:TPU:0, one launch (start us, length us, event | category | flops | bytes accessed | tf_op | source)
XLA Modules:
  0.0 38.7 jit_solution(3048143986822655045)
XLA Ops:
  0.7 1.9 %shard_map.118.own_ref.first_ref = bf16[272,256]{1,0:T(8,128)(2,1)} custom-call(bf16[256,256]{1,0:T(8,128)(2,1)} %features_ref.1, bf16[256,256]{1,0:T(8,128)(2,1)} %w_value_hbm.1, f32[3,256]{1,0:T(4,128)} %positions_hbm.1, s32[1]{0:T(128)S(6)} %copy.13.count_hbm), custom_call_target="tpu_custom_call" | custom-call | flops 1100000000 | bytes 1000000 | tf_op jit(solution)/shard_map/pallas_call | solution.py:447
  2.5 3.0 %collective-permute-start.1 = (bf16[272,256]{1,0:T(8,128)(2,1)}, bf16[272,256]{1,0:T(8,128)(2,1)S(1)}, u32[]{:S(2)}, u32[]{:S(2)}) collective-permute-start(bf16[272,256]{1,0:T(8,128)(2,1)} %shard_map.118.own_ref.first_ref), channel_id=1, source_target_pairs={{0,2},{1,3},{2,0},{3,1},{4,6},{5,7},{6,4},{7,5},{8,10},{9,11},{10,... | collective-permute-start | bytes 417800 | tf_op jit(solution)/shard_map/ppermute | solution.py:476
  5.6 2.6 %collective-permute-start.5 = (bf16[272,256]{1,0:T(8,128)(2,1)}, bf16[272,256]{1,0:T(8,128)(2,1)S(1)}, u32[]{:S(2)}, u32[]{:S(2)}) collective-permute-start(bf16[272,256]{1,0:T(8,128)(2,1)} %shard_map.118.own_ref.first_ref), channel_id=1, source_target_pairs={{0,8},{1,9},{2,10},{3,11},{4,12},{5,13},{6,14},{7,15},{8,0},{9,1},... | collective-permute-start | bytes 417800 | tf_op jit(solution)/shard_map/ppermute | solution.py:476
  8.2 0.0 collective-permute-start
  8.2 1.5 %collective-permute-start.3 = (bf16[272,256]{1,0:T(8,128)(2,1)}, bf16[272,256]{1,0:T(8,128)(2,1)S(1)}, u32[]{:S(2)}, u32[]{:S(2)}) collective-permute-start(bf16[272,256]{1,0:T(8,128)(2,1)} %shard_map.118.own_ref.first_ref), channel_id=1, source_target_pairs={{0,6},{1,7},{2,4},{3,5},{4,2},{5,3},{6,0},{7,1},{8,14},{9,15},{10,... | collective-permute-start | bytes 417800 | tf_op jit(solution)/shard_map/ppermute | solution.py:476
  9.7 0.4 %collective-permute-start.8 = (bf16[272,256]{1,0:T(8,128)(2,1)}, bf16[272,256]{1,0:T(8,128)(2,1)S(1)}, u32[]{:S(2)}, u32[]{:S(2)}) collective-permute-start(bf16[272,256]{1,0:T(8,128)(2,1)} %shard_map.118.own_ref.first_ref), channel_id=1, source_target_pairs={{0,4},{1,5},{2,6},{3,7},{4,0},{5,1},{6,2},{7,3},{8,12},{9,13},{10,... | collective-permute-start | bytes 417800 | tf_op jit(solution)/shard_map/ppermute | solution.py:476
  10.2 0.0 collective-permute-done.1.refs_4_
  10.2 0.0 collective-permute-start.2
  10.2 4.8 %collective-permute-done.5.refs_0_ = bf16[272,256]{1,0:T(8,128)(2,1)S(1)} collective-permute-done((bf16[272,256]{1,0:T(8,128)(2,1)}, bf16[272,256]{1,0:T(8,128)(2,1)S(1)}, u32[]{:S(2)}, u32[]{:S(2)}) %collective-permute-start.5) | collective-permute-done | bytes 139296 | tf_op jit(solution)/shard_map/ppermute | solution.py:476
  14.9 0.7 %collective-permute-start.6 = (bf16[272,256]{1,0:T(8,128)(2,1)S(1)}, bf16[272,256]{1,0:T(8,128)(2,1)S(1)}, u32[]{:S(2)}, u32[]{:S(2)}) collective-permute-start(bf16[272,256]{1,0:T(8,128)(2,1)S(1)} %collective-permute-done.5.refs_0_), channel_id=1, source_target_pairs={{0,6},{1,7},{2,4},{3,5},{4,2},{5,3},{6,0},{7,1},{8,14},{9,15},{10,... | collective-permute-start | bytes 417800 | tf_op jit(solution)/shard_map/ppermute | solution.py:476
  15.6 0.0 collective-permute-done.sibling_ref.second_ref
  15.6 1.3 %collective-permute-start.11 = (bf16[272,256]{1,0:T(8,128)(2,1)S(1)}, bf16[272,256]{1,0:T(8,128)(2,1)S(1)}, u32[]{:S(2)}, u32[]{:S(2)}) collective-permute-start(bf16[272,256]{1,0:T(8,128)(2,1)S(1)} %collective-permute-done.5.refs_0_), channel_id=1, source_target_pairs={{0,4},{1,5},{2,6},{3,7},{4,0},{5,1},{6,2},{7,3},{8,12},{9,13},{10,... | collective-permute-start | bytes 417800 | tf_op jit(solution)/shard_map/ppermute | solution.py:476
  16.9 0.5 %collective-permute-done.3.refs_0_ = bf16[272,256]{1,0:T(8,128)(2,1)S(1)} collective-permute-done((bf16[272,256]{1,0:T(8,128)(2,1)}, bf16[272,256]{1,0:T(8,128)(2,1)S(1)}, u32[]{:S(2)}, u32[]{:S(2)}) %collective-permute-start.3) | collective-permute-done | bytes 139296 | tf_op jit(solution)/shard_map/ppermute | solution.py:476
  17.4 1.1 %collective-permute-start.13 = (bf16[272,256]{1,0:T(8,128)(2,1)S(1)}, bf16[272,256]{1,0:T(8,128)(2,1)S(1)}, u32[]{:S(2)}, u32[]{:S(2)}) collective-permute-start(bf16[272,256]{1,0:T(8,128)(2,1)S(1)} %collective-permute-done.5.refs_0_), channel_id=1, source_target_pairs={{0,2},{1,3},{2,0},{3,1},{4,6},{5,7},{6,4},{7,5},{8,10},{9,11},{10,... | collective-permute-start | bytes 417800 | tf_op jit(solution)/shard_map/ppermute | solution.py:476
  18.4 1.2 %collective-permute-done.8.refs_2_ = bf16[272,256]{1,0:T(8,128)(2,1)S(1)} collective-permute-done((bf16[272,256]{1,0:T(8,128)(2,1)}, bf16[272,256]{1,0:T(8,128)(2,1)S(1)}, u32[]{:S(2)}, u32[]{:S(2)}) %collective-permute-start.8) | collective-permute-done | bytes 139296 | tf_op jit(solution)/shard_map/ppermute | solution.py:476
  19.6 0.0 collective-permute-start.4
  19.6 0.0 collective-permute-done.2.refs_0_.refs_5_
  19.6 0.5 %collective-permute-start.9 = (bf16[272,256]{1,0:T(8,128)(2,1)S(1)}, bf16[272,256]{1,0:T(8,128)(2,1)S(1)}, u32[]{:S(2)}, u32[]{:S(2)}) collective-permute-start(bf16[272,256]{1,0:T(8,128)(2,1)S(1)} %collective-permute-done.8.refs_2_), channel_id=1, source_target_pairs={{0,1},{1,0},{2,3},{3,2},{4,5},{5,4},{6,7},{7,6},{8,9},{9,8},{10,11... | collective-permute-start | bytes 417800 | tf_op jit(solution)/shard_map/ppermute | solution.py:485
  20.1 0.7 %shard_map.121 = (bf16[512,16]{1,0:T(8,128)(2,1)S(1)}, f32[512,256]{1,0:T(8,128)S(1)}) custom-call(s32[3,512]{1,0:T(4,128)S(1)} %copy-done.8, f32[16,256]{1,0:T(8,128)S(1)} %copy-done.6), custom_call_target="tpu_custom_call" | custom-call | flops 1430000000 | bytes 1300000 | tf_op jit(solution)/shard_map/pallas_call | solution.py:461
  20.9 1.2 %shard_map.122 = (f32[1024,256]{1,0:T(8,128)S(1)}, bf16[512,1024]{1,0:T(8,128)(2,1)S(1)}) custom-call(bf16[512,16]{1,0:T(8,128)(2,1)S(1)} %get-tuple-element.15.wave_ref, bf16[272,256]{1,0:T(8,128)(2,1)S(1)} %copy-done.2, bf16[272,256]{1,0:T(8,128)(2,1)S(1)} %collective-permute-done.sibling_ref.second_ref), custom_call_target="tpu_custom_call" | custom-call | flops 1100000000 | bytes 1000000 | tf_op jit(solution)/shard_map/pallas_call | solution.py:489
  22.1 0.0 collective-permute-done.4.refs_1_
  22.1 0.1 collective-permute-start.10
  22.2 1.2 %collective-permute-done.6.refs_2_ = bf16[272,256]{1,0:T(8,128)(2,1)S(1)} collective-permute-done((bf16[272,256]{1,0:T(8,128)(2,1)S(1)}, bf16[272,256]{1,0:T(8,128)(2,1)S(1)}, u32[]{:S(2)}, u32[]{:S(2)}) %collective-permute-start.6) | collective-permute-done | bytes 139296 | tf_op jit(solution)/shard_map/ppermute | solution.py:476
  23.4 0.0 collective-permute-start.7
  23.4 1.9 %collective-permute-done.11.refs_0_ = bf16[272,256]{1,0:T(8,128)(2,1)S(1)} collective-permute-done((bf16[272,256]{1,0:T(8,128)(2,1)S(1)}, bf16[272,256]{1,0:T(8,128)(2,1)S(1)}, u32[]{:S(2)}, u32[]{:S(2)}) %collective-permute-start.11) | collective-permute-done | bytes 139296 | tf_op jit(solution)/shard_map/ppermute | solution.py:476
  25.3 0.0 collective-permute-start.12
  25.3 0.3 collective-permute-done.13.refs_0_
  25.6 0.2 collective-permute-start.14
  25.8 2.9 %shard_map.123.sums_in_ref = f32[1024,256]{1,0:T(8,128)S(1)} custom-call(bf16[512,16]{1,0:T(8,128)(2,1)S(1)} %get-tuple-element.15.wave_ref, f32[1024,256]{1,0:T(8,128)S(1)} %get-tuple-element.16.sums_in_ref, bf16[272,256]{1,0:T(8,128)(2,1)S(1)} %collective-permute-done.3.refs_0_, bf16[272,256]{1,0:T(8,128)(2,1)S(1)} %collective-permute-done.4.refs_1_, ...), custom_call_target="tpu_custom_call" | custom-call | flops 2969999872 | bytes 2700000 | tf_op jit(solution)/shard_map/pallas_call | solution.py:512
  28.7 0.0 collective-permute-done.10.refs_1_
  28.8 2.1 %shard_map.124.sums_in_ref = f32[1024,256]{1,0:T(8,128)S(1)} custom-call(bf16[512,16]{1,0:T(8,128)(2,1)S(1)} %get-tuple-element.15.wave_ref, f32[1024,256]{1,0:T(8,128)S(1)} %shard_map.123.sums_in_ref, bf16[272,256]{1,0:T(8,128)(2,1)S(1)} %collective-permute-done.5.refs_0_, bf16[272,256]{1,0:T(8,128)(2,1)S(1)} %collective-permute-done.10.refs_1_, ...), custom_call_target="tpu_custom_call" | custom-call | flops 2090000000 | bytes 1900000 | tf_op jit(solution)/shard_map/pallas_call | solution.py:512
  30.9 0.0 collective-permute-done.12.refs_1_
  30.9 1.1 %shard_map.125.sums_in_ref = f32[1024,256]{1,0:T(8,128)S(1)} custom-call(bf16[512,16]{1,0:T(8,128)(2,1)S(1)} %get-tuple-element.15.wave_ref, f32[1024,256]{1,0:T(8,128)S(1)} %shard_map.124.sums_in_ref, bf16[272,256]{1,0:T(8,128)(2,1)S(1)} %collective-permute-done.11.refs_0_, bf16[272,256]{1,0:T(8,128)(2,1)S(1)} %collective-permute-done.12.refs_1_), custom_call_target="tpu_custom_call" | custom-call | flops 1210000000 | bytes 1100000 | tf_op jit(solution)/shard_map/pallas_call | solution.py:512
  32.0 0.0 copy-start
  32.1 0.0 copy-start.1
  32.1 0.0 copy-start.7
  32.1 1.6 %shard_map.126 = (f32[256,256]{1,0:T(8,128)S(1)}, bf16[256,256]{1,0:T(8,128)(2,1)S(1)}) custom-call(bf16[512,16]{1,0:T(8,128)(2,1)S(1)} %get-tuple-element.15.wave_ref, f32[1024,256]{1,0:T(8,128)S(1)} %shard_map.125.sums_in_ref, f32[512,256]{1,0:T(8,128)S(1)} %get-tuple-element.17.weights_ref, bf16[512,1024]{1,0:T(8,128)(2,1)S(1)} %get-tuple-element.18.turned_ref, ...), custom_call_target="tpu_custom_call" | custom-call | flops 1650000000 | bytes 1500000 | tf_op jit(solution)/shard_map/pallas_call | solution.py:520
  33.6 0.3 collective-permute-start.15
  34.0 2.2 %shard_map.119 = (f32[256,256]{1,0:T(8,128)S(1)}, bf16[4096,256]{1,0:T(8,128)(2,1)S(1)}) custom-call(f32[256,768]{1,0:T(8,128)S(1)} %copy-done, s32[256,768]{1,0:T(8,128)S(1)} %copy-done.1, f32[16,256]{1,0:T(8,128)S(1)} %copy-done.7, bf16[272,256]{1,0:T(8,128)(2,1)S(1)} %copy-done.2, bf16[272,256]{1,0:T(8,128)(2,1)S(1)} %collective-permute-done.sibling_ref.second_ref), custom_call_target="tpu_custom_call" | custom-call | flops 2750000128 | bytes 2500000 | tf_op jit(solution)/shard_map/pallas_call | solution.py:498
  36.2 0.0 copy-start.3
  36.2 0.0 copy-start.4
  36.2 0.0 copy-start.5
  36.3 0.0 copy-start.9
  36.3 0.9 %shard_map.120.near_ref = f32[256,256]{1,0:T(8,128)S(1)} custom-call(f32[256,256]{1,0:T(8,128)S(1)} %get-tuple-element.13.near_in_ref, bf16[4096,256]{1,0:T(8,128)(2,1)S(1)} %get-tuple-element.14.far_tiles_ref, f32[16,256]{1,0:T(8,128)S(1)} %copy-done.7, bf16[272,256]{1,0:T(8,128)(2,1)S(1)} %collective-permute-done.2.refs_0_.refs_5_, ...), custom_call_target="tpu_custom_call" | custom-call | flops 1100000000 | bytes 1000000 | tf_op jit(solution)/shard_map/pallas_call | solution.py:530
  37.1 0.0 collective-permute-done.15.message_ref
  37.1 0.0 copy-done.4
  37.2 0.1 copy-done.5
  37.3 1.4 %shard_map.127 = bf16[256,256]{1,0:T(8,128)(2,1)} custom-call(s32[1]{0:T(128)S(6)} %copy.13.count_hbm, bf16[256,256]{1,0:T(8,128)(2,1)S(1)} %copy-done.3, f32[256,256]{1,0:T(8,128)S(1)} %shard_map.120.near_ref, f32[256,256]{1,0:T(8,128)S(1)} %get-tuple-element.19.own_far_ref, bf16[256,256]{1,0:T(8,128)(2,1)S(1)} %collective-permute-done.15.message_ref, ...), custom_call_target="tpu_custom_call" | custom-call | flops 1100000000 | bytes 1000000 | tf_op jit(solution)/shard_map/pallas_call | solution.py:538
  (14 shorter events, 0.0 us)
Async XLA Ops:
  0.0 20.1 %copy-start.8 = (s32[3,512]{1,0:T(4,128)S(1)}, s32[3,512]{1,0:T(4,128)}, u32[]{:S(2)}) copy-start(s32[3,512]{1,0:T(4,128)} %wave_hbm.1) | copy-start | bytes 18436
  0.0 20.1 %copy-start.6 = (f32[16,256]{1,0:T(8,128)S(1)}, f32[16,256]{1,0:T(8,128)}, u32[]{:S(2)}) copy-start(f32[16,256]{1,0:T(8,128)} %filter_long_hbm.1) | copy-start | bytes 49156
  2.5 18.3 %copy-start.2 = (bf16[272,256]{1,0:T(8,128)(2,1)S(1)}, bf16[272,256]{1,0:T(8,128)(2,1)}, u32[]{:S(2)}) copy-start(bf16[272,256]{1,0:T(8,128)(2,1)} %shard_map.118.own_ref.first_ref) | copy-start | bytes 417796
  2.5 7.6 %collective-permute-start.1 = (bf16[272,256]{1,0:T(8,128)(2,1)}, bf16[272,256]{1,0:T(8,128)(2,1)S(1)}, u32[]{:S(2)}, u32[]{:S(2)}) collective-permute-start(bf16[272,256]{1,0:T(8,128)(2,1)} %shard_map.118.own_ref.first_ref), channel_id=1, source_target_pairs={{0,2},{1,3},{2,0},{3,1},{4,6},{5,7},{6,4},{7,5},{8,10},{9,11},{10,... | collective-permute-start | bytes 417800 | tf_op jit(solution)/shard_map/ppermute | solution.py:476
  5.6 9.3 %collective-permute-start.5 = (bf16[272,256]{1,0:T(8,128)(2,1)}, bf16[272,256]{1,0:T(8,128)(2,1)S(1)}, u32[]{:S(2)}, u32[]{:S(2)}) collective-permute-start(bf16[272,256]{1,0:T(8,128)(2,1)} %shard_map.118.own_ref.first_ref), channel_id=1, source_target_pairs={{0,8},{1,9},{2,10},{3,11},{4,12},{5,13},{6,14},{7,15},{8,0},{9,1},... | collective-permute-start | bytes 417800 | tf_op jit(solution)/shard_map/ppermute | solution.py:476
  8.2 7.4 %collective-permute-start = (bf16[272,256]{1,0:T(8,128)(2,1)}, bf16[272,256]{1,0:T(8,128)(2,1)S(1)}, u32[]{:S(2)}, u32[]{:S(2)}) collective-permute-start(bf16[272,256]{1,0:T(8,128)(2,1)} %shard_map.118.own_ref.first_ref), channel_id=1, source_target_pairs={{0,1},{1,0},{2,3},{3,2},{4,5},{5,4},{6,7},{7,6},{8,9},{9,8},{10,11... | collective-permute-start | bytes 417800 | tf_op jit(solution)/shard_map/ppermute | solution.py:485
  8.2 9.2 %collective-permute-start.3 = (bf16[272,256]{1,0:T(8,128)(2,1)}, bf16[272,256]{1,0:T(8,128)(2,1)S(1)}, u32[]{:S(2)}, u32[]{:S(2)}) collective-permute-start(bf16[272,256]{1,0:T(8,128)(2,1)} %shard_map.118.own_ref.first_ref), channel_id=1, source_target_pairs={{0,6},{1,7},{2,4},{3,5},{4,2},{5,3},{6,0},{7,1},{8,14},{9,15},{10,... | collective-permute-start | bytes 417800 | tf_op jit(solution)/shard_map/ppermute | solution.py:476
  9.7 9.9 %collective-permute-start.8 = (bf16[272,256]{1,0:T(8,128)(2,1)}, bf16[272,256]{1,0:T(8,128)(2,1)S(1)}, u32[]{:S(2)}, u32[]{:S(2)}) collective-permute-start(bf16[272,256]{1,0:T(8,128)(2,1)} %shard_map.118.own_ref.first_ref), channel_id=1, source_target_pairs={{0,4},{1,5},{2,6},{3,7},{4,0},{5,1},{6,2},{7,3},{8,12},{9,13},{10,... | collective-permute-start | bytes 417800 | tf_op jit(solution)/shard_map/ppermute | solution.py:476
  10.2 9.5 %collective-permute-start.2 = (bf16[272,256]{1,0:T(8,128)(2,1)S(1)}, bf16[272,256]{1,0:T(8,128)(2,1)S(1)}, u32[]{:S(2)}, u32[]{:S(2)}) collective-permute-start(bf16[272,256]{1,0:T(8,128)(2,1)S(1)} %collective-permute-done.1.refs_4_), channel_id=1, source_target_pairs={{0,1},{1,0},{2,3},{3,2},{4,5},{5,4},{6,7},{7,6},{8,9},{9,8},{10,11... | collective-permute-start | bytes 417800 | tf_op jit(solution)/shard_map/ppermute | solution.py:485
  14.9 8.5 %collective-permute-start.6 = (bf16[272,256]{1,0:T(8,128)(2,1)S(1)}, bf16[272,256]{1,0:T(8,128)(2,1)S(1)}, u32[]{:S(2)}, u32[]{:S(2)}) collective-permute-start(bf16[272,256]{1,0:T(8,128)(2,1)S(1)} %collective-permute-done.5.refs_0_), channel_id=1, source_target_pairs={{0,6},{1,7},{2,4},{3,5},{4,2},{5,3},{6,0},{7,1},{8,14},{9,15},{10,... | collective-permute-start | bytes 417800 | tf_op jit(solution)/shard_map/ppermute | solution.py:476
  15.6 9.7 %collective-permute-start.11 = (bf16[272,256]{1,0:T(8,128)(2,1)S(1)}, bf16[272,256]{1,0:T(8,128)(2,1)S(1)}, u32[]{:S(2)}, u32[]{:S(2)}) collective-permute-start(bf16[272,256]{1,0:T(8,128)(2,1)S(1)} %collective-permute-done.5.refs_0_), channel_id=1, source_target_pairs={{0,4},{1,5},{2,6},{3,7},{4,0},{5,1},{6,2},{7,3},{8,12},{9,13},{10,... | collective-permute-start | bytes 417800 | tf_op jit(solution)/shard_map/ppermute | solution.py:476
  17.4 8.2 %collective-permute-start.13 = (bf16[272,256]{1,0:T(8,128)(2,1)S(1)}, bf16[272,256]{1,0:T(8,128)(2,1)S(1)}, u32[]{:S(2)}, u32[]{:S(2)}) collective-permute-start(bf16[272,256]{1,0:T(8,128)(2,1)S(1)} %collective-permute-done.5.refs_0_), channel_id=1, source_target_pairs={{0,2},{1,3},{2,0},{3,1},{4,6},{5,7},{6,4},{7,5},{8,10},{9,11},{10,... | collective-permute-start | bytes 417800 | tf_op jit(solution)/shard_map/ppermute | solution.py:476
  19.6 2.4 %collective-permute-start.4 = (bf16[272,256]{1,0:T(8,128)(2,1)S(1)}, bf16[272,256]{1,0:T(8,128)(2,1)S(1)}, u32[]{:S(2)}, u32[]{:S(2)}) collective-permute-start(bf16[272,256]{1,0:T(8,128)(2,1)S(1)} %collective-permute-done.3.refs_0_), channel_id=1, source_target_pairs={{0,1},{1,0},{2,3},{3,2},{4,5},{5,4},{6,7},{7,6},{8,9},{9,8},{10,11... | collective-permute-start | bytes 417800 | tf_op jit(solution)/shard_map/ppermute | solution.py:485
  19.6 6.2 %collective-permute-start.9 = (bf16[272,256]{1,0:T(8,128)(2,1)S(1)}, bf16[272,256]{1,0:T(8,128)(2,1)S(1)}, u32[]{:S(2)}, u32[]{:S(2)}) collective-permute-start(bf16[272,256]{1,0:T(8,128)(2,1)S(1)} %collective-permute-done.8.refs_2_), channel_id=1, source_target_pairs={{0,1},{1,0},{2,3},{3,2},{4,5},{5,4},{6,7},{7,6},{8,9},{9,8},{10,11... | collective-permute-start | bytes 417800 | tf_op jit(solution)/shard_map/ppermute | solution.py:485
  22.1 6.7 %collective-permute-start.10 = (bf16[272,256]{1,0:T(8,128)(2,1)S(1)}, bf16[272,256]{1,0:T(8,128)(2,1)S(1)}, u32[]{:S(2)}, u32[]{:S(2)}) collective-permute-start(bf16[272,256]{1,0:T(8,128)(2,1)S(1)} %collective-permute-done.5.refs_0_), channel_id=1, source_target_pairs={{0,1},{1,0},{2,3},{3,2},{4,5},{5,4},{6,7},{7,6},{8,9},{9,8},{10,11... | collective-permute-start | bytes 417800 | tf_op jit(solution)/shard_map/ppermute | solution.py:485
  23.4 5.4 %collective-permute-start.7 = (bf16[272,256]{1,0:T(8,128)(2,1)S(1)}, bf16[272,256]{1,0:T(8,128)(2,1)S(1)}, u32[]{:S(2)}, u32[]{:S(2)}) collective-permute-start(bf16[272,256]{1,0:T(8,128)(2,1)S(1)} %collective-permute-done.6.refs_2_), channel_id=1, source_target_pairs={{0,1},{1,0},{2,3},{3,2},{4,5},{5,4},{6,7},{7,6},{8,9},{9,8},{10,11... | collective-permute-start | bytes 417800 | tf_op jit(solution)/shard_map/ppermute | solution.py:485
  25.3 5.6 %collective-permute-start.12 = (bf16[272,256]{1,0:T(8,128)(2,1)S(1)}, bf16[272,256]{1,0:T(8,128)(2,1)S(1)}, u32[]{:S(2)}, u32[]{:S(2)}) collective-permute-start(bf16[272,256]{1,0:T(8,128)(2,1)S(1)} %collective-permute-done.11.refs_0_), channel_id=1, source_target_pairs={{0,1},{1,0},{2,3},{3,2},{4,5},{5,4},{6,7},{7,6},{8,9},{9,8},{10,11... | collective-permute-start | bytes 417800 | tf_op jit(solution)/shard_map/ppermute | solution.py:485
  25.6 6.5 %collective-permute-start.14 = (bf16[272,256]{1,0:T(8,128)(2,1)S(1)}, bf16[272,256]{1,0:T(8,128)(2,1)S(1)}, u32[]{:S(2)}, u32[]{:S(2)}) collective-permute-start(bf16[272,256]{1,0:T(8,128)(2,1)S(1)} %collective-permute-done.13.refs_0_), channel_id=1, source_target_pairs={{0,1},{1,0},{2,3},{3,2},{4,5},{5,4},{6,7},{7,6},{8,9},{9,8},{10,11... | collective-permute-start | bytes 417800 | tf_op jit(solution)/shard_map/ppermute | solution.py:485
  32.0 1.9 %copy-start = (f32[256,768]{1,0:T(8,128)S(1)}, f32[256,768]{1,0:T(8,128)}, u32[]{:S(2)}) copy-start(f32[256,768]{1,0:T(8,128)} %distances_ref.1) | copy-start | bytes 2359300
  32.1 1.9 %copy-start.1 = (s32[256,768]{1,0:T(8,128)S(1)}, s32[256,768]{1,0:T(8,128)}, u32[]{:S(2)}) copy-start(s32[256,768]{1,0:T(8,128)} %mask_ref.1) | copy-start | bytes 2359300
  32.1 1.9 %copy-start.7 = (f32[16,256]{1,0:T(8,128)S(1)}, f32[16,256]{1,0:T(8,128)}, u32[]{:S(2)}) copy-start(f32[16,256]{1,0:T(8,128)} %filter_ref.3) | copy-start | bytes 49156
  33.6 3.5 %collective-permute-start.15 = (bf16[256,256]{1,0:T(8,128)(2,1)S(1)}, bf16[256,256]{1,0:T(8,128)(2,1)S(1)}, u32[]{:S(2)}, u32[]{:S(2)}) collective-permute-start(bf16[256,256]{1,0:T(8,128)(2,1)S(1)} %get-tuple-element.20), channel_id=1, source_target_pairs={{0,1},{1,0},{2,3},{3,2},{4,5},{5,4},{6,7},{7,6},{8,9},{9,8},{10,11... | collective-permute-start | bytes 393224 | tf_op jit(solution)/shard_map/ppermute | solution.py:528
  36.2 0.9 %copy-start.3 = (bf16[256,256]{1,0:T(8,128)(2,1)S(1)}, bf16[256,256]{1,0:T(8,128)(2,1)}, u32[]{:S(2)}) copy-start(bf16[256,256]{1,0:T(8,128)(2,1)} %features_ref.1) | copy-start | bytes 393220
  36.2 1.0 %copy-start.4 = (bf16[256,256]{1,0:T(8,128)(2,1)S(1)}, bf16[256,256]{1,0:T(8,128)(2,1)}, u32[]{:S(2)}) copy-start(bf16[256,256]{1,0:T(8,128)(2,1)} %w_inner_ref.1) | copy-start | bytes 393220
  36.2 1.0 %copy-start.5 = (bf16[256,256]{1,0:T(8,128)(2,1)S(1)}, bf16[256,256]{1,0:T(8,128)(2,1)}, u32[]{:S(2)}) copy-start(bf16[256,256]{1,0:T(8,128)(2,1)} %w_outer_ref.1) | copy-start | bytes 393220
  36.3 1.0 %copy-start.9 = (f32[256]{0:T(256)S(1)}, f32[256]{0:T(256)}, u32[]{:S(2)}) copy-start(f32[256]{0:T(256)} %param.21) | copy-start | bytes 3076

commit v2 on v1

--- a/solution.py
+++ b/solution.py
@@ -14,12 +14,7 @@
 gather_limit = 8
 extra_rows = 16
 
-sin_terms = (
-    2.641753992459813,
-    -1.08637674632807,
-    0.134005627536115,
-    -0.007739884914760742,
-)
+sin_terms = (2.641737538071335, -1.0859062893731768, 0.13047468843565363)
 
 
 def padded(block, sides, width):
@@ -146,31 +141,32 @@
     return 1.0 - half_sin * half_sin, half_sin * half_cos
 
 
-def fill_phases(phase_ref, column, wave_ref, point_rows, step=64):
+def add_sums(sums_in, sums_ref, chunks, wave_ref, phase_ref, turned_ref=None, block=128, step=64):
+    rows = chunks[0].shape[0] - extra_rows
     wave_count = wave_ref.shape[0]
-    width = point_rows.shape[1]
-    for low in range(0, wave_count, step):
-        turns = jnp.dot(
-            wave_ref[low : low + step, :], point_rows, preferred_element_type=jnp.float32
-        )
-        cosine, sine = phases(turns)
-        phase_ref[low : low + step, column : column + width] = cosine.astype(jnp.bfloat16)
-        phase_ref[wave_count + low : wave_count + low + step, column : column + width] = (
-            sine.astype(jnp.bfloat16)
-        )
-
-
-def add_sums(sums, chunks, wave_ref, phase_ref):
-    rows = chunks[0].shape[0] - extra_rows
-    for i in range(len(chunks) // 2):
-        first, second = chunks[2 * i], chunks[2 * i + 1]
-        slot = phase_ref.at[i % 2]
-        fill_phases(slot, 0, wave_ref, first[rows:, :])
-        fill_phases(slot, rows, wave_ref, second[rows:, :])
-        block_values = jnp.concatenate([first[:rows, :], second[:rows, :]], axis=0)
+    block_values = [chunk[:rows, :] for chunk in chunks]
+    block_values = jnp.concatenate(block_values, axis=0) if len(chunks) > 1 else block_values[0]
+    for index, start in enumerate(range(0, wave_count, block)):
+        slot = phase_ref.at[index % 2]
+        for i, chunk in enumerate(chunks):
+            part = slice(i * rows, (i + 1) * rows)
+            for low in range(0, block, step):
+                turns = jnp.dot(
+                    wave_ref[start + low : start + low + step, :],
+                    chunk[rows:, :],
+                    preferred_element_type=jnp.float32,
+                )
+                cosine, sine = phases(turns)
+                slot[low : low + step, part] = cosine.astype(jnp.bfloat16)
+                slot[block + low : block + low + step, part] = sine.astype(jnp.bfloat16)
         found = jnp.dot(slot[...], block_values, preferred_element_type=jnp.float32)
-        sums = found if sums is None else sums + found
-    return sums
+        for first, rank in ((start, 0), (wave_count + start, block)):
+            value = found[rank : rank + block, :]
+            if sums_in is not None:
+                value = sums_in[first : first + block, :] + value
+            sums_ref[first : first + block, :] = value
+            if turned_ref is not None:
+                turned_ref[:, first : first + block] = slot[rank : rank + block, :rows].T
 
 
 def fetch(sources, targets, semaphores):
@@ -214,10 +210,9 @@
 
 
 def waves_kernel(
-    scale, wave_hbm, filter_long_hbm, waves_ref, weights_ref, wave_ref, filter_long_ref, sems
-):
-    fetch((wave_hbm, filter_long_hbm), (wave_ref, filter_long_ref), sems)
-    waves = wave_ref[...].astype(jnp.float32)
+    scale, own_wave_ref, other_wave_ref, filter_long_ref, waves_ref, weights_ref
+):
+    waves = jnp.concatenate([own_wave_ref[...], other_wave_ref[...]], axis=1).astype(jnp.float32)
     spare = jnp.zeros((extra_rows - 9, waves.shape[1]), jnp.float32)
     waves_ref[...] = jnp.concatenate([waves, waves, waves, spare], axis=0).T.astype(jnp.bfloat16)
     radial_count = filter_long_ref.shape[0]
@@ -236,14 +231,18 @@
     )
 
 
-def own_kernel(wave_ref, first_ref, second_ref, sums_ref, turned_ref, phase_ref):
-    sums_ref[...] = add_sums(None, (first_ref, second_ref), wave_ref, phase_ref)
-    turned_ref[...] = phase_ref[0].T
-
-
-def more_kernel(wave_ref, sums_in_ref, *refs):
-    chunks, (sums_ref, phase_ref) = refs[:-2], refs[-2:]
-    sums_ref[...] = add_sums(sums_in_ref[...], chunks, wave_ref, phase_ref)
+def first_kernel(wave_ref, *refs):
+    chunks, (sums_ref, turned_ref, phase_ref) = refs[:-3], refs[-3:]
+    add_sums(None, sums_ref, chunks, wave_ref, phase_ref, turned_ref)
+
+
+def last_kernel(wave_ref, sums_in_ref, weights_ref, *refs):
+    chunks, (shared_ref, phase_ref, sums_ref) = refs[:-3], refs[-3:]
+    add_sums(sums_in_ref, sums_ref, chunks, wave_ref, phase_ref)
+    wave_count = wave_ref.shape[0]
+    for start in (0, wave_count):
+        part = slice(start, start + wave_count)
+        shared_ref[part, :] = (sums_ref[part, :] * weights_ref[...]).astype(jnp.bfloat16)
 
 
 def weighted(products, rows, filter_ref):
@@ -263,7 +262,6 @@
     mask_ref,
     filter_ref,
     own_ref,
-    sibling_ref,
     near_ref,
     far_tiles_ref,
     tiles_ref,
@@ -297,7 +295,7 @@
             value = value * back
             put(k, value.astype(jnp.bfloat16))
 
-    block_values = jnp.concatenate([own_ref[:rows, :], sibling_ref[:rows, :]], axis=0)
+    block_values = own_ref[:rows, :]
 
     def products(i):
         found = jnp.dot(tiles_ref[i % 2], block_values, preferred_element_type=jnp.float32)
@@ -307,102 +305,97 @@
         for low in range(i * step, (i + 1) * step, part):
             inner = low - i * step
 
-            def put(column):
+            def put(k, value):
+                at = k * step + inner
+                tiles_ref[i % 2, at : at + part, :] = value
+
+            def put_far(column):
                 def store(k, value):
-                    at = k * step + inner
-                    tiles_ref[i % 2, at : at + part, column : column + rows] = value
+                    at = k * rows + low
+                    far_tiles_ref[at : at + part, column : column + rows] = value
 
                 return store
 
-            def put_far(k, value):
-                at = k * rows + low
-                far_tiles_ref[at : at + part, :] = value
-
-            make(low, 1, put(0))
-            make(low, sibling, put(rows))
-            make(low, 2 - sibling, put_far)
+            make(low, 1, put)
+            make(low, sibling, put_far(0))
+            make(low, 2 - sibling, put_far(rows))
         if i:
             products(i - 1)
     products(rows // step - 1)
 
 
-def beyond_kernel(nearby, near_in_ref, far_tiles_ref, filter_ref, *refs):
-    near_chunks, (near_ref, side_ref) = refs[:nearby], refs[nearby:]
-    rows = near_ref.shape[0]
+def near_masks(blocks):
+    return sorted({a ^ ((a + 1) % blocks) for a in range(blocks)})
+
+
+def pick_kernel(*refs):
+    own_ref, chunks, out_ref = refs[0], refs[1:-1], refs[-1]
+    rows = out_ref.shape[0] // 2
+    out_ref[:rows, :] = own_ref[:rows, :]
     blocks, block = lax.axis_size("atoms"), lax.axis_index("atoms")
-    side = lax.rem(block + 2 * lax.axis_index("waves") - 1 + blocks, blocks)
-    for mask, chunk in zip(near_masks(blocks), near_chunks):
+    side = lax.rem(block + 1 - 2 * lax.axis_index("waves") + blocks, blocks)
+    for mask, chunk in zip(near_masks(blocks), chunks):
 
         @pl.when((block ^ side) == mask)
         def _():
-            side_ref[...] = chunk[:rows, :]
-
+            out_ref[rows:, :] = chunk[:rows, :]
+
+
+def beyond_kernel(
+    scale,
+    near_in_ref,
+    far_tiles_ref,
+    filter_ref,
+    side_ref,
+    features_ref,
+    turned_ref,
+    shared_ref,
+    combined_ref,
+):
+    rows = near_in_ref.shape[0]
     found = jnp.dot(far_tiles_ref[...], side_ref[...], preferred_element_type=jnp.float32)
-    near_ref[...] = near_in_ref[...] + weighted(found, rows, filter_ref)
-
-
-def near_masks(blocks):
-    return sorted({a ^ ((a + 1) % blocks) for a in range(blocks)})
-
-
-def last_kernel(
-    wave_ref,
-    sums_in_ref,
-    weights_ref,
-    turned_ref,
-    *refs,
-):
-    chunks, (own_far_ref, message_ref, phase_ref) = refs[:-3], refs[-3:]
-    rows = own_far_ref.shape[0]
-    wave_count = wave_ref.shape[0]
-    sums = add_sums(sums_in_ref[...], chunks, wave_ref, phase_ref)
-    weights = weights_ref[...]
-    filtered = jnp.concatenate(
-        [
-            (sums[:wave_count, :] * weights).astype(jnp.bfloat16),
-            (sums[wave_count:, :] * weights).astype(jnp.bfloat16),
-        ],
-        axis=0,
-    )
-    far = jnp.dot(turned_ref[...], filtered, preferred_element_type=jnp.float32)
-    own_far_ref[...] = far[:rows, :]
-    message_ref[...] = far[rows:, :].astype(jnp.bfloat16)
+    far = jnp.dot(turned_ref[...], shared_ref[...], preferred_element_type=jnp.float32)
+    combined_ref[...] = (
+        features_ref[...].astype(jnp.float32)
+        + near_in_ref[...]
+        + weighted(found, rows, filter_ref)
+        + far * scale
+    )
 
 
 def update_kernel(
     scale,
-    count_hbm,
-    features_ref,
-    near_ref,
-    own_far_ref,
-    message_ref,
+    count_ref,
+    combined_ref,
+    received_ref,
+    turned_ref,
     gain_ref,
     w_inner_ref,
     w_outer_ref,
     out_ref,
-    count_ref,
-    sem,
-):
-    copy = pltpu.make_async_copy(count_hbm, count_ref, sem)
-    copy.start()
-    far = (own_far_ref[...] + message_ref[...].astype(jnp.float32)) * scale
-    combined = features_ref[...].astype(jnp.float32) + near_ref[...] + far
+):
+    quarter = received_ref.shape[0] // 4
+    received = jnp.concatenate(
+        [received_ref[i * quarter : (i + 1) * quarter, :] for i in (1, 0, 3, 2)], axis=0
+    )
+    far = jnp.dot(turned_ref[...], received, preferred_element_type=jnp.float32)
+    combined = combined_ref[...] + far * scale
     spread = lax.rsqrt(jnp.mean(combined * combined, axis=-1, keepdims=True) + 1e-06)
     normed = (combined * spread * gain_ref[...]).astype(jnp.bfloat16)
     inner = jnp.dot(normed, w_inner_ref[...], preferred_element_type=jnp.float32)
     inner = (inner / (1.0 + jnp.exp(-inner))).astype(jnp.bfloat16)
     result = jnp.dot(inner, w_outer_ref[...], preferred_element_type=jnp.float32)
     row = lax.broadcasted_iota(jnp.int32, result.shape, 0)
-    copy.wait()
-    out_ref[...] = jnp.where(row < count_ref[0], result, 0.0).astype(jnp.bfloat16)
+    out_ref[...] = jnp.where(row < count_ref[...].reshape(1, 1), result, 0.0).astype(jnp.bfloat16)
 
 
 hbm = pl.BlockSpec(memory_space=pltpu.HBM)
 vmem = pl.BlockSpec(memory_space=pltpu.VMEM)
 
 
-def call(kernel, specs, outs, scratch=(), micros=1.0, mib=8):
-    shapes = tuple(jax.ShapeDtypeStruct(shape, dtype) for shape, dtype in outs)
+def call(kernel, specs, outs, scratch=(), micros=1.0, mib=8, final=False):
+    make = jax.ShapeDtypeStruct if final else pltpu.VMEM
+    shapes = tuple(make(shape, dtype) for shape, dtype in outs)
     return pl.pallas_call(
         kernel,
         in_specs=specs,
@@ -455,93 +448,81 @@
             pltpu.SMEM(counts.shape, counts.dtype),
             pltpu.SemaphoreType.DMA((4,)),
         ],
-        micros=1.0,
+        micros=6.0,
         mib=60,
     )(features, w_value, positions, counts)
+
+    def move(value, mask):
+        return lax.ppermute(value, both, across(mask))
+
+    def swap(value):
+        return lax.ppermute(value, both, over)
+
+    starts, passed = move_masks(blocks)
+    got = {0: chunk, **{mask: move(chunk, mask) for mask in starts}}
+    for mask in passed:
+        got[mask] = lax.ppermute(got[starts[0]], both, across(starts[0] ^ mask))
+    other_waves = swap(wave_index)
+
+    wave_total = wave_count * cores
+    sums_shape = ((2 * wave_total, width), f32)
     waves, wave_weights = call(
         functools.partial(waves_kernel, float(rows * blocks * cores) ** -0.5),
-        [hbm, hbm],
-        [((wave_count, extra_rows), bf16), ((wave_count, width), f32)],
-        [
-            pltpu.VMEM(wave_index.shape, wave_index.dtype),
-            pltpu.VMEM(filter_long.shape, filter_long.dtype),
-            pltpu.SemaphoreType.DMA((2,)),
-        ],
-        micros=1.3,
-    )(wave_index, filter_long)
-
-    half = blocks // 2
-
-    def move(value, mask):
-        return lax.ppermute(value, both, across(mask))
-
-    got = {0: chunk, half: move(chunk, half)}
-    for mask in range(half - 1, 0, -1):
-        got[mask] = move(chunk, mask)
-    for mask in range(half - 1, 0, -1):
-        got[half ^ mask] = move(got[half], mask)
-    other = {}
-    for mask, value in got.items():
-        other[mask] = lax.ppermute(value, both, over)
-
-    sums_shape = ((2 * wave_count, width), f32)
-    phase_shape = (2 * wave_count, 2 * rows)
-    sums, turned = call(
-        own_kernel,
         [vmem] * 3,
-        [sums_shape, (phase_shape[::-1], bf16)],
-        [pltpu.VMEM((1,) + phase_shape, bf16)],
+        [((wave_total, extra_rows), bf16), ((wave_total, width), f32)],
         micros=1.0,
-    )(waves, chunk, other[0])
-
+    )(wave_index, other_waves, filter_long)
     step = rows // 4
     near, far_tiles = call(
         functools.partial(near_kernel, step=step),
-        [vmem] * 5,
-        [((rows, width), f32), ((radial_count * rows, rows), bf16)],
-        [pltpu.VMEM((2, radial_count * step, 2 * rows), bf16)],
+        [vmem] * 4,
+        [((rows, width), f32), ((radial_count * rows, 2 * rows), bf16)],
+        [pltpu.VMEM((2, radial_count * step, rows), bf16)],
         micros=2.5,
         mib=16,
-    )(distances, pair_mask, filter_short, chunk, other[0])
-
-    def pairs(masks):
-        return [c for mask in masks for c in (got[mask], other[mask])]
-
-    groups = sum_groups(blocks)
-    for masks in groups[:-1]:
-        (sums,) = call(
-            more_kernel,
-            [vmem] * (2 + 2 * len(masks)),
-            [sums_shape],
-            [pltpu.VMEM((min(2, len(masks)),) + phase_shape, bf16)],
-            micros=0.8 * len(masks) + 0.3,
-            mib=12,
-        )(waves, sums, *pairs(masks))
-    own_far, message = call(
+    )(distances, pair_mask, filter_short, chunk)
+
+    first, last = sum_groups(blocks)
+    sums, turned = call(
+        first_kernel,
+        [vmem] * (1 + len(first)),
+        [sums_shape, ((rows, 2 * wave_total), bf16)],
+        [phase_scratch(len(first), rows)],
+        micros=0.9 * len(first),
+        mib=12,
+    )(waves, *(got[mask] for mask in first))
+    (side,) = call(
+        pick_kernel, [vmem] * (1 + len(near_masks(blocks))), [((2 * rows, width), bf16)], micros=0.3
+    )(chunk, *(got[mask] for mask in near_masks(blocks)))
+    side = swap(side)
+    (shared,) = call(
         last_kernel,
-        [vmem] * (4 + 2 * len(groups[-1])),
-        [((rows, width), f32), ((rows, width), bf16)],
-        [pltpu.VMEM((min(2, len(groups[-1])),) + phase_shape, bf16)],
+        [vmem] * (3 + len(last)),
+        [(sums_shape[0], bf16)],
+        [phase_scratch(len(last), rows), pltpu.VMEM(sums_shape[0], f32)],
+        micros=0.9 * len(last),
+        mib=12,
+    )(waves, sums, wave_weights, *(got[mask] for mask in last))
+    received = swap(shared)
+    scale = float(wave_total) ** -0.5
+    (combined,) = call(
+        functools.partial(beyond_kernel, scale),
+        [vmem] * 7,
+        [((rows, width), f32)],
         micros=1.5,
         mib=12,
-    )(waves, sums, wave_weights, turned, *pairs(groups[-1]))
-    message = lax.ppermute(message, both, over)
-    near_chunks = [other[m] for m in near_masks(blocks)]
-    (near,) = call(
-        functools.partial(beyond_kernel, len(near_chunks)),
-        [vmem] * (3 + len(near_chunks)),
-        [((rows, width), f32)],
-        [pltpu.VMEM((rows, width), bf16)],
+    )(near, far_tiles, filter_short, side, features, turned, shared)
+    return call(
+        functools.partial(update_kernel, scale),
+        [vmem] * 7,
+        [((rows, width), bf16)],
         micros=1.0,
-        mib=12,
-    )(near, far_tiles, filter_short, *near_chunks)
-    return call(
-        functools.partial(update_kernel, float(wave_count * cores) ** -0.5),
-        [hbm] + [vmem] * 7,
-        [((rows, width), bf16)],
-        [pltpu.SMEM(counts.shape, counts.dtype), pltpu.SemaphoreType.DMA],
-        micros=1.0,
-    )(counts, features, near, own_far, message, jnp.reshape(gain, (1, width)), w_inner, w_outer)[0]
+        final=True,
+    )(counts, combined, received, turned, jnp.reshape(gain, (1, width)), w_inner, w_outer)[0]
+
+
+def phase_scratch(chunks, rows, block=128):
+    return pltpu.VMEM((2, 2 * block, chunks * rows), jnp.bfloat16)
 
 
 def gathered_body(*args):
@@ -556,14 +537,12 @@
 
 def sum_groups(blocks):
     starts, passed = move_masks(blocks)
-    order = starts[:1] + passed
-    groups = [starts[1:], order[:2]] + [[mask] for mask in order[2:]]
-    return [group for group in groups if group]
+    return [0] + starts[1:] + starts[:1], passed
 
 
 def gathers(mesh):
     blocks, cores = mesh.shape["atoms"], mesh.shape["waves"]
-    return cores == 2 and 2 <= blocks <= gather_limit and blocks & (blocks - 1) == 0
+    return cores == 2 and 4 <= blocks <= gather_limit and blocks & (blocks - 1) == 0
 
 
 def solution(mesh):
@@ -581,10 +560,11 @@
         P(),
         P(),
     )
-    return jax.shard_map(
+    mapped = jax.shard_map(
         gathered_body if gathers(mesh) else summed_body,
         mesh=mesh,
         in_specs=placed,
         out_specs=P(("groups", "atoms", "waves"), None),
         check_vma=False,
     )
+    return mapped if gathers(mesh) else mapped

time: 38.8 us -> 32.2 us (0.83)
  waiting for transfers between devices: 9.88 us -> 5.38 us
  Pallas kernels: 15.9 us -> 14.1 us
    ppermute x7 -> x4, waiting for transfers between devices: 9.85 us -> 2.98 us  [move(): return lax.ppermute(value, both, across(mask))]
    ppermute x7 -> x4, starting transfers between devices: 10.6 us -> 7.62 us  [move(): return lax.ppermute(value, both, across(mask))]
    ppermute x9 -> x6, starting transfers between devices: 1.19 us -> 4.12 us  [the longest x3 3.49 us: gathered_parts(): got[mask] = lax.ppermute(got[starts[0]], both, across(starts[0] ^ mask))]
    ppermute x9 -> x6, waiting for transfers between devices: 0.02 us -> 2.4 us  [the longest x3 1.49 us: swap(): return lax.ppermute(value, both, over)]
    pallas_call x8 -> x6, Pallas kernels: 13.4 us -> 11.8 us  [the longest x1 3.97 us: gathered_parts(): call(first_kernel, [vmem] * (1 + len(first)), [sums_shape, ((rows, 2 * wa...]
    pallas_call x1, Pallas kernels: 1.85 us -> 1.21 us  [gathered_parts(): call(prepare_kernel, [hbm, hbm, hbm, hbm], [((chunk_rows, width), bf16)],...]
  transfers between devices with their start and end apart: 16 -> 10, of which waited for: 6 -> 5; matrix products, arithmetic and copies ran while one was open for 0% -> 0% of each run, Pallas kernels for 29% -> 27%
where the time goes in v2:
time: 32.2 us; the launch traced here: 32.1 us
  Pallas kernels  14.1 us (44%)
  starting transfers between devices  11.7 us (36%)
  waiting for transfers between devices  5.38 us (17%)
  between operations  0.81 us (3%)
    ppermute x4, starting transfers between devices, move(): return lax.ppermute(value, both, across(mask))  7.62 us
    pallas_call x1, Pallas kernels, gathered_parts(): call(first_kernel, [vmem] * (1 + len(first)), [sums_shape, ((rows, 2 * wa...  3.97 us
    ppermute x3, starting transfers between devices, gathered_parts(): got[mask] = lax.ppermute(got[starts[0]], both, across(starts[0] ^ mask))  3.49 us
    ppermute x4, waiting for transfers between devices, move(): return lax.ppermute(value, both, across(mask))  2.98 us
    pallas_call x1, Pallas kernels, gathered_parts(): call(last_kernel, [vmem] * (3 + len(last)), [(sums_shape[0], bf16)], [pha...  2.72 us
    pallas_call x1, Pallas kernels, gathered_parts(): call(functools.partial(near_kernel, step=step), [vmem] * 4, [((rows, widt...  1.86 us
    pallas_call x1, Pallas kernels, gathered_parts(): call(functools.partial(beyond_kernel, scale), [vmem] * 7, [((rows, width)...  1.54 us
    pallas_call x1, Pallas kernels, gathered_parts(): call(functools.partial(update_kernel, scale), [vmem] * 7, [((rows, width)...  1.51 us
  transfers between devices with their start and end apart: 10, of which 5 were waited for; matrix products, arithmetic and copies ran while one was open for 0% of the time, Pallas kernels for 27%

profile of v2, /device:TPU:0, one launch (start us, length us, event | category | flops | bytes accessed | tf_op | source)
XLA Modules:
  0.0 32.1 jit_solution(6282100089835701094)
XLA Ops:
  0.7 0.0 copy-start.7
  0.7 0.0 copy-start.6
  0.7 1.2 %shard_map.118.own_ref.refs_0_ = bf16[272,256]{1,0:T(8,128)(2,1)S(1)} custom-call(bf16[256,256]{1,0:T(8,128)(2,1)} %features_ref.1, bf16[256,256]{1,0:T(8,128)(2,1)} %w_value_hbm.1, f32[3,256]{1,0:T(4,128)} %positions_hbm.1, s32[1]{0:T(128)S(6)} %copy.13.count_hbm.count_ref), custom_call_target="tpu_custom_call" | custom-call | flops 6600000000 | bytes 6000000 | tf_op jit(solution)/shard_map/pallas_call | solution.py:440
  1.9 4.1 %collective-permute-start.2 = (bf16[272,256]{1,0:T(8,128)(2,1)S(1)}, bf16[272,256]{1,0:T(8,128)(2,1)S(1)}, u32[]{:S(2)}, u32[]{:S(2)}) collective-permute-start(bf16[272,256]{1,0:T(8,128)(2,1)S(1)} %shard_map.118.own_ref.refs_0_), channel_id=1, source_target_pairs={{0,8},{1,9},{2,10},{3,11},{4,12},{5,13},{6,14},{7,15},{8,0},{9,1},... | collective-permute-start | bytes 417800 | tf_op jit(solution)/shard_map/ppermute | solution.py:456
  6.0 1.5 %collective-permute-start = (bf16[272,256]{1,0:T(8,128)(2,1)S(1)}, bf16[272,256]{1,0:T(8,128)(2,1)S(1)}, u32[]{:S(2)}, u32[]{:S(2)}) collective-permute-start(bf16[272,256]{1,0:T(8,128)(2,1)S(1)} %shard_map.118.own_ref.refs_0_), channel_id=1, source_target_pairs={{0,2},{1,3},{2,0},{3,1},{4,6},{5,7},{6,4},{7,5},{8,10},{9,11},{10,... | collective-permute-start | bytes 417800 | tf_op jit(solution)/shard_map/ppermute | solution.py:456
  7.5 1.5 %collective-permute-start.1 = (bf16[272,256]{1,0:T(8,128)(2,1)S(1)}, bf16[272,256]{1,0:T(8,128)(2,1)S(1)}, u32[]{:S(2)}, u32[]{:S(2)}) collective-permute-start(bf16[272,256]{1,0:T(8,128)(2,1)S(1)} %shard_map.118.own_ref.refs_0_), channel_id=1, source_target_pairs={{0,6},{1,7},{2,4},{3,5},{4,2},{5,3},{6,0},{7,1},{8,14},{9,15},{10,... | collective-permute-start | bytes 417800 | tf_op jit(solution)/shard_map/ppermute | solution.py:456
  9.1 0.4 %collective-permute-start.6 = (bf16[272,256]{1,0:T(8,128)(2,1)S(1)}, bf16[272,256]{1,0:T(8,128)(2,1)S(1)}, u32[]{:S(2)}, u32[]{:S(2)}) collective-permute-start(bf16[272,256]{1,0:T(8,128)(2,1)S(1)} %shard_map.118.own_ref.refs_0_), channel_id=1, source_target_pairs={{0,4},{1,5},{2,6},{3,7},{4,0},{5,1},{6,2},{7,3},{8,12},{9,13},{10,... | collective-permute-start | bytes 417800 | tf_op jit(solution)/shard_map/ppermute | solution.py:456
  9.5 0.0 copy-done.7
  9.5 0.0 collective-permute-start.5
  9.5 1.2 %collective-permute-done.5.other_wave_ref = s32[3,512]{1,0:T(4,128)S(1)} collective-permute-done((s32[3,512]{1,0:T(4,128)S(1)}, s32[3,512]{1,0:T(4,128)S(1)}, u32[]{:S(2)}, u32[]{:S(2)}) %collective-permute-start.5) | collective-permute-done | bytes 6176 | tf_op jit(solution)/shard_map/ppermute | solution.py:459
  10.7 0.0 copy-done.6
  10.7 1.1 %shard_map.121 = (bf16[1024,16]{1,0:T(8,128)(2,1)S(1)}, f32[1024,256]{1,0:T(8,128)S(1)}) custom-call(s32[3,512]{1,0:T(4,128)S(1)} %copy-done.7, s32[3,512]{1,0:T(4,128)S(1)} %collective-permute-done.5.other_wave_ref, f32[16,256]{1,0:T(8,128)S(1)} %copy-done.6), custom_call_target="tpu_custom_call" | custom-call | flops 1100000000 | bytes 1000000 | tf_op jit(solution)/shard_map/pallas_call | solution.py:469
  11.8 1.0 %collective-permute-done.2.refs_4_ = bf16[272,256]{1,0:T(8,128)(2,1)S(1)} collective-permute-done((bf16[272,256]{1,0:T(8,128)(2,1)S(1)}, bf16[272,256]{1,0:T(8,128)(2,1)S(1)}, u32[]{:S(2)}, u32[]{:S(2)}) %collective-permute-start.2) | collective-permute-done | bytes 139296 | tf_op jit(solution)/shard_map/ppermute | solution.py:456
  12.8 1.6 %collective-permute-start.3 = (bf16[272,256]{1,0:T(8,128)(2,1)S(1)}, bf16[272,256]{1,0:T(8,128)(2,1)S(1)}, u32[]{:S(2)}, u32[]{:S(2)}) collective-permute-start(bf16[272,256]{1,0:T(8,128)(2,1)S(1)} %collective-permute-done.2.refs_4_), channel_id=1, source_target_pairs={{0,6},{1,7},{2,4},{3,5},{4,2},{5,3},{6,0},{7,1},{8,14},{9,15},{10,... | collective-permute-start | bytes 417800 | tf_op jit(solution)/shard_map/ppermute | solution.py:464
  14.4 1.4 %collective-permute-start.7 = (bf16[272,256]{1,0:T(8,128)(2,1)S(1)}, bf16[272,256]{1,0:T(8,128)(2,1)S(1)}, u32[]{:S(2)}, u32[]{:S(2)}) collective-permute-start(bf16[272,256]{1,0:T(8,128)(2,1)S(1)} %collective-permute-done.2.refs_4_), channel_id=1, source_target_pairs={{0,4},{1,5},{2,6},{3,7},{4,0},{5,1},{6,2},{7,3},{8,12},{9,13},{10,... | collective-permute-start | bytes 417800 | tf_op jit(solution)/shard_map/ppermute | solution.py:464
  15.8 0.0 collective-permute-done.refs_1_.refs_3_
  15.8 0.5 %collective-permute-start.8 = (bf16[272,256]{1,0:T(8,128)(2,1)S(1)}, bf16[272,256]{1,0:T(8,128)(2,1)S(1)}, u32[]{:S(2)}, u32[]{:S(2)}) collective-permute-start(bf16[272,256]{1,0:T(8,128)(2,1)S(1)} %collective-permute-done.2.refs_4_), channel_id=1, source_target_pairs={{0,2},{1,3},{2,0},{3,1},{4,6},{5,7},{6,4},{7,5},{8,10},{9,11},{10,... | collective-permute-start | bytes 417800 | tf_op jit(solution)/shard_map/ppermute | solution.py:464
  16.3 0.0 collective-permute-done.1.refs_2_.refs_1_
  16.3 1.9 %collective-permute-done.6.refs_2_ = bf16[272,256]{1,0:T(8,128)(2,1)S(1)} collective-permute-done((bf16[272,256]{1,0:T(8,128)(2,1)S(1)}, bf16[272,256]{1,0:T(8,128)(2,1)S(1)}, u32[]{:S(2)}, u32[]{:S(2)}) %collective-permute-start.6) | collective-permute-done | bytes 139296 | tf_op jit(solution)/shard_map/ppermute | solution.py:456
  18.2 4.0 %shard_map.122 = (f32[2048,256]{1,0:T(8,128)S(1)}, bf16[256,2048]{1,0:T(8,128)(2,1)S(1)}) custom-call(bf16[1024,16]{1,0:T(8,128)(2,1)S(1)} %get-tuple-element.13.wave_ref, bf16[272,256]{1,0:T(8,128)(2,1)S(1)} %shard_map.118.own_ref.refs_0_, bf16[272,256]{1,0:T(8,128)(2,1)S(1)} %collective-permute-done.1.refs_2_.refs_1_, ...), custom_call_target="tpu_custom_call" | custom-call | flops 4950000128 | bytes 4500000 | tf_op jit(solution)/shard_map/pallas_call | solution.py:486
  22.2 0.0 collective-permute-done.3.refs_3_.refs_0_
  22.2 0.9 %collective-permute-done.7.refs_1_ = bf16[272,256]{1,0:T(8,128)(2,1)S(1)} collective-permute-done((bf16[272,256]{1,0:T(8,128)(2,1)S(1)}, bf16[272,256]{1,0:T(8,128)(2,1)S(1)}, u32[]{:S(2)}, u32[]{:S(2)}) %collective-permute-start.7) | collective-permute-done | bytes 139296 | tf_op jit(solution)/shard_map/ppermute | solution.py:464
  23.1 0.0 collective-permute-done.8.refs_2_
  23.1 0.0 copy-start.1
  23.1 0.0 copy-start.2
  23.1 0.0 copy-start.3
  23.1 2.7 %shard_map.123.shared_ref = bf16[2048,256]{1,0:T(8,128)(2,1)S(1)} custom-call(bf16[1024,16]{1,0:T(8,128)(2,1)S(1)} %get-tuple-element.13.wave_ref, f32[2048,256]{1,0:T(8,128)S(1)} %get-tuple-element.15.sums_in_ref, f32[1024,256]{1,0:T(8,128)S(1)} %get-tuple-element.16.weights_ref, bf16[272,256]{1,0:T(8,128)(2,1)S(1)} %collective-permute-done.3.refs_3_.refs_0_, ...), custom_call_target="tpu_custom_call" | custom-call | flops 2969999872 | bytes 2700000 | tf_op jit(solution)/shard_map/pallas_call | solution.py:498
  25.9 0.1 collective-permute-start.9
  25.9 0.2 shard_map.120
  26.2 0.0 copy-start
  26.2 0.6 %collective-permute-start.4 = (bf16[512,256]{1,0:T(8,128)(2,1)S(1)}, bf16[512,256]{1,0:T(8,128)(2,1)S(1)}, u32[]{:S(2)}, u32[]{:S(2)}) collective-permute-start(bf16[512,256]{1,0:T(8,128)(2,1)S(1)} %shard_map.120), channel_id=1, source_target_pairs={{0,1},{1,0},{2,3},{3,2},{4,5},{5,4},{6,7},{7,6},{8,9},{9,8},{10,11... | collective-permute-start | bytes 786440 | tf_op jit(solution)/shard_map/ppermute | solution.py:459
  26.7 0.0 copy-done.1
  26.7 0.0 copy-done.2
  26.7 0.0 copy-done.3
  26.7 1.9 %shard_map.119 = (f32[256,256]{1,0:T(8,128)S(1)}, bf16[4096,512]{1,0:T(8,128)(2,1)S(1)}) custom-call(f32[256,768]{1,0:T(8,128)S(1)} %copy-done.2, s32[256,768]{1,0:T(8,128)S(1)} %copy-done.3, f32[16,256]{1,0:T(8,128)S(1)} %copy-done.1, bf16[272,256]{1,0:T(8,128)(2,1)S(1)} %shard_map.118.own_ref.refs_0_), custom_call_target="tpu_custom_call" | custom-call | flops 2750000128 | bytes 2500000 | tf_op jit(solution)/shard_map/pallas_call | solution.py:476
  28.6 0.0 copy-start.4
  28.6 0.0 copy-start.5
  28.6 0.0 copy-start.8
  28.6 0.3 collective-permute-done.4.side_ref
  29.0 0.0 copy-done
  29.0 1.5 %shard_map.124.combined_ref = f32[256,256]{1,0:T(8,128)S(1)} custom-call(f32[256,256]{1,0:T(8,128)S(1)} %get-tuple-element.11.near_in_ref, bf16[4096,512]{1,0:T(8,128)(2,1)S(1)} %get-tuple-element.12.far_tiles_ref, f32[16,256]{1,0:T(8,128)S(1)} %copy-done.1, bf16[512,256]{1,0:T(8,128)(2,1)S(1)} %collective-permute-done.4.side_ref, ...), custom_call_target="tpu_custom_call" | custom-call | flops 1650000000 | bytes 1500000 | tf_op jit(solution)/shard_map/pallas_call | solution.py:508
  30.5 0.0 collective-permute-done.9.received_ref
  30.5 0.0 copy-done.4
  30.5 0.0 copy-done.5
  30.5 0.0 copy-done.8
  30.6 1.5 %shard_map.125 = bf16[256,256]{1,0:T(8,128)(2,1)} custom-call(s32[1]{0:T(128)S(6)} %copy.13.count_hbm.count_ref, f32[256,256]{1,0:T(8,128)S(1)} %shard_map.124.combined_ref, bf16[2048,256]{1,0:T(8,128)(2,1)S(1)} %collective-permute-done.9.received_ref, bf16[256,2048]{1,0:T(8,128)(2,1)S(1)} %get-tuple-element.14.turned_ref, f32[1,256]{1,0:T(1,128)S(1)} %bitcast.1, ...), custom_call_target="tpu_custom_call" | custom-call | flops 1100000000 | bytes 1000000 | tf_op jit(solution)/shard_map/pallas_call | solution.py:515
Async XLA Ops:
  0.7 8.9 %copy-start.7 = (s32[3,512]{1,0:T(4,128)S(1)}, s32[3,512]{1,0:T(4,128)}, u32[]{:S(2)}) copy-start(s32[3,512]{1,0:T(4,128)} %own_wave_ref.1) | copy-start | bytes 18436
  0.7 10.0 %copy-start.6 = (f32[16,256]{1,0:T(8,128)S(1)}, f32[16,256]{1,0:T(8,128)}, u32[]{:S(2)}) copy-start(f32[16,256]{1,0:T(8,128)} %filter_long_ref.1) | copy-start | bytes 49156
  1.9 10.9 %collective-permute-start.2 = (bf16[272,256]{1,0:T(8,128)(2,1)S(1)}, bf16[272,256]{1,0:T(8,128)(2,1)S(1)}, u32[]{:S(2)}, u32[]{:S(2)}) collective-permute-start(bf16[272,256]{1,0:T(8,128)(2,1)S(1)} %shard_map.118.own_ref.refs_0_), channel_id=1, source_target_pairs={{0,8},{1,9},{2,10},{3,11},{4,12},{5,13},{6,14},{7,15},{8,0},{9,1},... | collective-permute-start | bytes 417800 | tf_op jit(solution)/shard_map/ppermute | solution.py:456
  6.0 9.8 %collective-permute-start = (bf16[272,256]{1,0:T(8,128)(2,1)S(1)}, bf16[272,256]{1,0:T(8,128)(2,1)S(1)}, u32[]{:S(2)}, u32[]{:S(2)}) collective-permute-start(bf16[272,256]{1,0:T(8,128)(2,1)S(1)} %shard_map.118.own_ref.refs_0_), channel_id=1, source_target_pairs={{0,2},{1,3},{2,0},{3,1},{4,6},{5,7},{6,4},{7,5},{8,10},{9,11},{10,... | collective-permute-start | bytes 417800 | tf_op jit(solution)/shard_map/ppermute | solution.py:456
  7.5 8.8 %collective-permute-start.1 = (bf16[272,256]{1,0:T(8,128)(2,1)S(1)}, bf16[272,256]{1,0:T(8,128)(2,1)S(1)}, u32[]{:S(2)}, u32[]{:S(2)}) collective-permute-start(bf16[272,256]{1,0:T(8,128)(2,1)S(1)} %shard_map.118.own_ref.refs_0_), channel_id=1, source_target_pairs={{0,6},{1,7},{2,4},{3,5},{4,2},{5,3},{6,0},{7,1},{8,14},{9,15},{10,... | collective-permute-start | bytes 417800 | tf_op jit(solution)/shard_map/ppermute | solution.py:456
  9.1 9.2 %collective-permute-start.6 = (bf16[272,256]{1,0:T(8,128)(2,1)S(1)}, bf16[272,256]{1,0:T(8,128)(2,1)S(1)}, u32[]{:S(2)}, u32[]{:S(2)}) collective-permute-start(bf16[272,256]{1,0:T(8,128)(2,1)S(1)} %shard_map.118.own_ref.refs_0_), channel_id=1, source_target_pairs={{0,4},{1,5},{2,6},{3,7},{4,0},{5,1},{6,2},{7,3},{8,12},{9,13},{10,... | collective-permute-start | bytes 417800 | tf_op jit(solution)/shard_map/ppermute | solution.py:456
  9.5 1.2 %collective-permute-start.5 = (s32[3,512]{1,0:T(4,128)S(1)}, s32[3,512]{1,0:T(4,128)S(1)}, u32[]{:S(2)}, u32[]{:S(2)}) collective-permute-start(s32[3,512]{1,0:T(4,128)S(1)} %copy-done.7), channel_id=1, source_target_pairs={{0,1},{1,0},{2,3},{3,2},{4,5},{5,4},{6,7},{7,6},{8,9},{9,8},{10,11... | collective-permute-start | bytes 18440 | tf_op jit(solution)/shard_map/ppermute | solution.py:459
  12.8 9.4 %collective-permute-start.3 = (bf16[272,256]{1,0:T(8,128)(2,1)S(1)}, bf16[272,256]{1,0:T(8,128)(2,1)S(1)}, u32[]{:S(2)}, u32[]{:S(2)}) collective-permute-start(bf16[272,256]{1,0:T(8,128)(2,1)S(1)} %collective-permute-done.2.refs_4_), channel_id=1, source_target_pairs={{0,6},{1,7},{2,4},{3,5},{4,2},{5,3},{6,0},{7,1},{8,14},{9,15},{10,... | collective-permute-start | bytes 417800 | tf_op jit(solution)/shard_map/ppermute | solution.py:464
  14.4 8.7 %collective-permute-start.7 = (bf16[272,256]{1,0:T(8,128)(2,1)S(1)}, bf16[272,256]{1,0:T(8,128)(2,1)S(1)}, u32[]{:S(2)}, u32[]{:S(2)}) collective-permute-start(bf16[272,256]{1,0:T(8,128)(2,1)S(1)} %collective-permute-done.2.refs_4_), channel_id=1, source_target_pairs={{0,4},{1,5},{2,6},{3,7},{4,0},{5,1},{6,2},{7,3},{8,12},{9,13},{10,... | collective-permute-start | bytes 417800 | tf_op jit(solution)/shard_map/ppermute | solution.py:464
  15.8 7.3 %collective-permute-start.8 = (bf16[272,256]{1,0:T(8,128)(2,1)S(1)}, bf16[272,256]{1,0:T(8,128)(2,1)S(1)}, u32[]{:S(2)}, u32[]{:S(2)}) collective-permute-start(bf16[272,256]{1,0:T(8,128)(2,1)S(1)} %collective-permute-done.2.refs_4_), channel_id=1, source_target_pairs={{0,2},{1,3},{2,0},{3,1},{4,6},{5,7},{6,4},{7,5},{8,10},{9,11},{10,... | collective-permute-start | bytes 417800 | tf_op jit(solution)/shard_map/ppermute | solution.py:464
  23.1 3.6 %copy-start.1 = (f32[16,256]{1,0:T(8,128)S(1)}, f32[16,256]{1,0:T(8,128)}, u32[]{:S(2)}) copy-start(f32[16,256]{1,0:T(8,128)} %filter_ref.3) | copy-start | bytes 49156
  23.1 3.6 %copy-start.2 = (f32[256,768]{1,0:T(8,128)S(1)}, f32[256,768]{1,0:T(8,128)}, u32[]{:S(2)}) copy-start(f32[256,768]{1,0:T(8,128)} %distances_ref.1) | copy-start | bytes 2359300
  23.1 3.6 %copy-start.3 = (s32[256,768]{1,0:T(8,128)S(1)}, s32[256,768]{1,0:T(8,128)}, u32[]{:S(2)}) copy-start(s32[256,768]{1,0:T(8,128)} %mask_ref.1) | copy-start | bytes 2359300
  25.9 4.7 %collective-permute-start.9 = (bf16[2048,256]{1,0:T(8,128)(2,1)S(1)}, bf16[2048,256]{1,0:T(8,128)(2,1)S(1)}, u32[]{:S(2)}, u32[]{:S(2)}) collective-permute-start(bf16[2048,256]{1,0:T(8,128)(2,1)S(1)} %shard_map.123.shared_ref), channel_id=1, source_target_pairs={{0,1},{1,0},{2,3},{3,2},{4,5},{5,4},{6,7},{7,6},{8,9},{9,8},{10,11... | collective-permute-start | bytes 3145736 | tf_op jit(solution)/shard_map/ppermute | solution.py:459
  26.2 2.8 %copy-start = (bf16[256,256]{1,0:T(8,128)(2,1)S(1)}, bf16[256,256]{1,0:T(8,128)(2,1)}, u32[]{:S(2)}) copy-start(bf16[256,256]{1,0:T(8,128)(2,1)} %features_ref.1) | copy-start | bytes 393220
  26.2 2.8 %collective-permute-start.4 = (bf16[512,256]{1,0:T(8,128)(2,1)S(1)}, bf16[512,256]{1,0:T(8,128)(2,1)S(1)}, u32[]{:S(2)}, u32[]{:S(2)}) collective-permute-start(bf16[512,256]{1,0:T(8,128)(2,1)S(1)} %shard_map.120), channel_id=1, source_target_pairs={{0,1},{1,0},{2,3},{3,2},{4,5},{5,4},{6,7},{7,6},{8,9},{9,8},{10,11... | collective-permute-start | bytes 786440 | tf_op jit(solution)/shard_map/ppermute | solution.py:459
  28.6 1.9 %copy-start.4 = (bf16[256,256]{1,0:T(8,128)(2,1)S(1)}, bf16[256,256]{1,0:T(8,128)(2,1)}, u32[]{:S(2)}) copy-start(bf16[256,256]{1,0:T(8,128)(2,1)} %w_inner_ref.1) | copy-start | bytes 393220
  28.6 1.9 %copy-start.5 = (bf16[256,256]{1,0:T(8,128)(2,1)S(1)}, bf16[256,256]{1,0:T(8,128)(2,1)}, u32[]{:S(2)}) copy-start(bf16[256,256]{1,0:T(8,128)(2,1)} %w_outer_ref.1) | copy-start | bytes 393220
  28.6 1.9 %copy-start.8 = (f32[256]{0:T(256)S(1)}, f32[256]{0:T(256)}, u32[]{:S(2)}) copy-start(f32[256]{0:T(256)} %param.21) | copy-start | bytes 3076

commit v3 on v2

--- a/solution.py
+++ b/solution.py
@@ -141,13 +141,14 @@
     return 1.0 - half_sin * half_sin, half_sin * half_cos
 
 
-def add_sums(sums_in, sums_ref, chunks, wave_ref, phase_ref, turned_ref=None, block=128, step=64):
+def add_sums(sums_in, sums_ref, chunks, wave_ref, phase_ref, turned_ref=None, step=64):
     rows = chunks[0].shape[0] - extra_rows
     wave_count = wave_ref.shape[0]
+    block = wave_count // phase_ref.shape[0]
     block_values = [chunk[:rows, :] for chunk in chunks]
     block_values = jnp.concatenate(block_values, axis=0) if len(chunks) > 1 else block_values[0]
     for index, start in enumerate(range(0, wave_count, block)):
-        slot = phase_ref.at[index % 2]
+        slot = phase_ref.at[index]
         for i, chunk in enumerate(chunks):
             part = slice(i * rows, (i + 1) * rows)
             for low in range(0, block, step):
@@ -180,6 +181,12 @@
         copy.wait()
 
 
+def pieces(value):
+    high = value.astype(jnp.bfloat16).astype(jnp.float32)
+    middle = (value - high).astype(jnp.bfloat16).astype(jnp.float32)
+    return high, middle, value - high - middle
+
+
 def prepare_kernel(
     features_hbm,
     w_value_hbm,
@@ -202,9 +209,7 @@
     row = lax.broadcasted_iota(jnp.int32, values.shape, 0)
     chunk_ref[:rows, :] = jnp.where(row < count_ref[0], values, 0.0).astype(jnp.bfloat16)
     points = positions[...]
-    high = points.astype(jnp.bfloat16).astype(jnp.float32)
-    middle = (points - high).astype(jnp.bfloat16).astype(jnp.float32)
-    low = points - high - middle
+    high, middle, low = pieces(points)
     spare = jnp.zeros((extra_rows - 9, rows), jnp.float32)
     chunk_ref[rows:, :] = jnp.concatenate([high, middle, low, spare], axis=0).astype(jnp.bfloat16)
 
@@ -223,10 +228,13 @@
     index = lax.broadcasted_iota(jnp.int32, (radial_count, waves.shape[1]), 0)
     offsets = magnitude / spacing - index.astype(jnp.float32)
     basis = jnp.exp(-0.5 * offsets * offsets)
+    high, middle, low = pieces(basis)
+    rows = jnp.concatenate([high, high, middle, high, low, middle], axis=0)
+    high, middle, low = pieces(filter_long_ref[...])
+    columns = jnp.concatenate([high, middle, high, low, high, middle], axis=0)
     weights_ref[...] = scale * jnp.dot(
-        basis.T,
-        filter_long_ref[...],
-        precision=lax.Precision.HIGHEST,
+        rows.T.astype(jnp.bfloat16),
+        columns.astype(jnp.bfloat16),
         preferred_element_type=jnp.float32,
     )
 
@@ -234,6 +242,11 @@
 def first_kernel(wave_ref, *refs):
     chunks, (sums_ref, turned_ref, phase_ref) = refs[:-3], refs[-3:]
     add_sums(None, sums_ref, chunks, wave_ref, phase_ref, turned_ref)
+
+
+def more_kernel(wave_ref, sums_in_ref, *refs):
+    chunks, (sums_ref, phase_ref) = refs[:-2], refs[-2:]
+    add_sums(sums_in_ref, sums_ref, chunks, wave_ref, phase_ref)
 
 
 def last_kernel(wave_ref, sums_in_ref, weights_ref, *refs):
@@ -482,12 +495,12 @@
         mib=16,
     )(distances, pair_mask, filter_short, chunk)
 
-    first, last = sum_groups(blocks)
+    first, *later, last = sum_groups(blocks)
     sums, turned = call(
         first_kernel,
         [vmem] * (1 + len(first)),
         [sums_shape, ((rows, 2 * wave_total), bf16)],
-        [phase_scratch(len(first), rows)],
+        [phase_scratch(len(first), rows, wave_total)],
         micros=0.9 * len(first),
         mib=12,
     )(waves, *(got[mask] for mask in first))
@@ -495,11 +508,20 @@
         pick_kernel, [vmem] * (1 + len(near_masks(blocks))), [((2 * rows, width), bf16)], micros=0.3
     )(chunk, *(got[mask] for mask in near_masks(blocks)))
     side = swap(side)
+    for masks in later:
+        (sums,) = call(
+            more_kernel,
+            [vmem] * (2 + len(masks)),
+            [sums_shape],
+            [phase_scratch(len(masks), rows, wave_total)],
+            micros=0.9 * len(masks),
+            mib=12,
+        )(waves, sums, *(got[mask] for mask in masks))
     (shared,) = call(
         last_kernel,
         [vmem] * (3 + len(last)),
         [(sums_shape[0], bf16)],
-        [phase_scratch(len(last), rows), pltpu.VMEM(sums_shape[0], f32)],
+        [phase_scratch(len(last), rows, wave_total), pltpu.VMEM(sums_shape[0], f32)],
         micros=0.9 * len(last),
         mib=12,
     )(waves, sums, wave_weights, *(got[mask] for mask in last))
@@ -521,8 +543,8 @@
     )(counts, combined, received, turned, jnp.reshape(gain, (1, width)), w_inner, w_outer)[0]
 
 
-def phase_scratch(chunks, rows, block=128):
-    return pltpu.VMEM((2, 2 * block, chunks * rows), jnp.bfloat16)
+def phase_scratch(chunks, rows, waves, blocks=2):
+    return pltpu.VMEM((blocks, 2 * waves // blocks, chunks * rows), jnp.bfloat16)
 
 
 def gathered_body(*args):
@@ -537,7 +559,8 @@
 
 def sum_groups(blocks):
     starts, passed = move_masks(blocks)
-    return [0] + starts[1:] + starts[:1], passed
+    groups = [[0] + starts[-1:] + starts[:1], starts[1:-1], passed[:1], passed[1:]]
+    return [group for group in groups if group]
 
 
 def gathers(mesh):

time: 32.2 us -> 33.7 us (1.047)
  waiting for transfers between devices: 5.38 us -> 7.23 us
  Pallas kernels: 14.1 us -> 13.7 us
    ppermute x3, waiting for transfers between devices: 0.91 us -> 3.94 us  [gathered_parts(): got[mask] = lax.ppermute(got[starts[0]], both, across(starts[0] ^ mask))]
    pallas_call x0 -> x2, Pallas kernels: none -> 2.75 us  [gathered_parts(): call(more_kernel, [vmem] * (2 + len(masks)), [sums_shape], [phase_scratch...]
    pallas_call x1, Pallas kernels: 3.97 us -> 2.46 us  [gathered_parts(): call(first_kernel, [vmem] * (1 + len(first)), [sums_shape, ((rows, 2 * wa...]
    ppermute x3, waiting for transfers between devices: 1.49 us -> 0.36 us  [swap(): return lax.ppermute(value, both, over)]
    pallas_call x1, Pallas kernels: 2.72 us -> 1.72 us  [gathered_parts(): call(last_kernel, [vmem] * (3 + len(last)), [(sums_shape[0], bf16)], [pha...]
    pallas_call x1, Pallas kernels: 1.06 us -> 0.38 us  [gathered_parts(): call(functools.partial(waves_kernel, float(rows * blocks * cores) ** (-0....]
  transfers between devices with their start and end apart: 10 -> 10, of which waited for: 5 -> 3; matrix products, arithmetic and copies ran while one was open for 0% -> 0% of each run, Pallas kernels for 27% -> 27%
where the time goes in v3:
time: 33.7 us; the launch traced here: 33.5 us
  Pallas kernels  13.7 us (41%)
  starting transfers between devices  11.7 us (35%)
  waiting for transfers between devices  7.23 us (21%)
  between operations  0.84 us (2%)
    ppermute x4, starting transfers between devices, move(): return lax.ppermute(value, both, across(mask))  7.62 us
    ppermute x3, waiting for transfers between devices, gathered_parts(): got[mask] = lax.ppermute(got[starts[0]], both, across(starts[0] ^ mask))  3.94 us
    ppermute x3, starting transfers between devices, gathered_parts(): got[mask] = lax.ppermute(got[starts[0]], both, across(starts[0] ^ mask))  3.49 us
    ppermute x4, waiting for transfers between devices, move(): return lax.ppermute(value, both, across(mask))  2.92 us
    pallas_call x2, Pallas kernels, gathered_parts(): call(more_kernel, [vmem] * (2 + len(masks)), [sums_shape], [phase_scratch...  2.75 us
    pallas_call x1, Pallas kernels, gathered_parts(): call(first_kernel, [vmem] * (1 + len(first)), [sums_shape, ((rows, 2 * wa...  2.46 us
    pallas_call x1, Pallas kernels, gathered_parts(): call(functools.partial(near_kernel, step=step), [vmem] * 4, [((rows, widt...  1.86 us
    pallas_call x1, Pallas kernels, gathered_parts(): call(last_kernel, [vmem] * (3 + len(last)), [(sums_shape[0], bf16)], [pha...  1.72 us
  transfers between devices with their start and end apart: 10, of which 3 were waited for; matrix products, arithmetic and copies ran while one was open for 0% of the time, Pallas kernels for 27%

profile of v3, /device:TPU:0, one launch (start us, length us, event | category | flops | bytes accessed | tf_op | source)
XLA Modules:
  0.0 33.5 jit_solution(2711521232507095900)
XLA Ops:
  0.7 0.0 copy-start.7
  0.7 0.0 copy-start.6
  0.7 1.2 %shard_map.118.own_ref.refs_0_ = bf16[272,256]{1,0:T(8,128)(2,1)S(1)} custom-call(bf16[256,256]{1,0:T(8,128)(2,1)} %features_ref.1, bf16[256,256]{1,0:T(8,128)(2,1)} %w_value_hbm.1, f32[3,256]{1,0:T(4,128)} %positions_hbm.1, s32[1]{0:T(128)S(6)} %copy.13.count_hbm.count_ref), custom_call_target="tpu_custom_call" | custom-call | flops 6600000000 | bytes 6000000 | tf_op jit(solution)/shard_map/pallas_call | solution.py:453
  1.9 4.1 %collective-permute-start.2 = (bf16[272,256]{1,0:T(8,128)(2,1)S(1)}, bf16[272,256]{1,0:T(8,128)(2,1)S(1)}, u32[]{:S(2)}, u32[]{:S(2)}) collective-permute-start(bf16[272,256]{1,0:T(8,128)(2,1)S(1)} %shard_map.118.own_ref.refs_0_), channel_id=1, source_target_pairs={{0,8},{1,9},{2,10},{3,11},{4,12},{5,13},{6,14},{7,15},{8,0},{9,1},... | collective-permute-start | bytes 417800 | tf_op jit(solution)/shard_map/ppermute | solution.py:469
  6.0 1.5 %collective-permute-start = (bf16[272,256]{1,0:T(8,128)(2,1)S(1)}, bf16[272,256]{1,0:T(8,128)(2,1)S(1)}, u32[]{:S(2)}, u32[]{:S(2)}) collective-permute-start(bf16[272,256]{1,0:T(8,128)(2,1)S(1)} %shard_map.118.own_ref.refs_0_), channel_id=1, source_target_pairs={{0,2},{1,3},{2,0},{3,1},{4,6},{5,7},{6,4},{7,5},{8,10},{9,11},{10,... | collective-permute-start | bytes 417800 | tf_op jit(solution)/shard_map/ppermute | solution.py:469
  7.5 0.0 copy-done.7
  7.5 0.0 collective-permute-start.5
  7.5 1.6 %collective-permute-start.6 = (bf16[272,256]{1,0:T(8,128)(2,1)S(1)}, bf16[272,256]{1,0:T(8,128)(2,1)S(1)}, u32[]{:S(2)}, u32[]{:S(2)}) collective-permute-start(bf16[272,256]{1,0:T(8,128)(2,1)S(1)} %shard_map.118.own_ref.refs_0_), channel_id=1, source_target_pairs={{0,4},{1,5},{2,6},{3,7},{4,0},{5,1},{6,2},{7,3},{8,12},{9,13},{10,... | collective-permute-start | bytes 417800 | tf_op jit(solution)/shard_map/ppermute | solution.py:469
  9.1 0.4 %collective-permute-start.1 = (bf16[272,256]{1,0:T(8,128)(2,1)S(1)}, bf16[272,256]{1,0:T(8,128)(2,1)S(1)}, u32[]{:S(2)}, u32[]{:S(2)}) collective-permute-start(bf16[272,256]{1,0:T(8,128)(2,1)S(1)} %shard_map.118.own_ref.refs_0_), channel_id=1, source_target_pairs={{0,6},{1,7},{2,4},{3,5},{4,2},{5,3},{6,0},{7,1},{8,14},{9,15},{10,... | collective-permute-start | bytes 417800 | tf_op jit(solution)/shard_map/ppermute | solution.py:469
  9.5 0.0 collective-permute-done.5.other_wave_ref
  9.5 0.0 copy-done.6
  9.5 0.4 %shard_map.121 = (bf16[1024,16]{1,0:T(8,128)(2,1)S(1)}, f32[1024,256]{1,0:T(8,128)S(1)}) custom-call(s32[3,512]{1,0:T(4,128)S(1)} %copy-done.7, s32[3,512]{1,0:T(4,128)S(1)} %collective-permute-done.5.other_wave_ref, f32[16,256]{1,0:T(8,128)S(1)} %copy-done.6), custom_call_target="tpu_custom_call" | custom-call | flops 1100000000 | bytes 1000000 | tf_op jit(solution)/shard_map/pallas_call | solution.py:482
  9.9 2.9 %collective-permute-done.2.refs_2_ = bf16[272,256]{1,0:T(8,128)(2,1)S(1)} collective-permute-done((bf16[272,256]{1,0:T(8,128)(2,1)S(1)}, bf16[272,256]{1,0:T(8,128)(2,1)S(1)}, u32[]{:S(2)}, u32[]{:S(2)}) %collective-permute-start.2) | collective-permute-done | bytes 139296 | tf_op jit(solution)/shard_map/ppermute | solution.py:469
  12.8 1.5 %collective-permute-start.8 = (bf16[272,256]{1,0:T(8,128)(2,1)S(1)}, bf16[272,256]{1,0:T(8,128)(2,1)S(1)}, u32[]{:S(2)}, u32[]{:S(2)}) collective-permute-start(bf16[272,256]{1,0:T(8,128)(2,1)S(1)} %collective-permute-done.2.refs_2_), channel_id=1, source_target_pairs={{0,2},{1,3},{2,0},{3,1},{4,6},{5,7},{6,4},{7,5},{8,10},{9,11},{10,... | collective-permute-start | bytes 417800 | tf_op jit(solution)/shard_map/ppermute | solution.py:477
  14.3 0.6 %collective-permute-start.7 = (bf16[272,256]{1,0:T(8,128)(2,1)S(1)}, bf16[272,256]{1,0:T(8,128)(2,1)S(1)}, u32[]{:S(2)}, u32[]{:S(2)}) collective-permute-start(bf16[272,256]{1,0:T(8,128)(2,1)S(1)} %collective-permute-done.2.refs_2_), channel_id=1, source_target_pairs={{0,4},{1,5},{2,6},{3,7},{4,0},{5,1},{6,2},{7,3},{8,12},{9,13},{10,... | collective-permute-start | bytes 417800 | tf_op jit(solution)/shard_map/ppermute | solution.py:477
  14.9 0.0 collective-permute-done.refs_1_
  14.9 1.3 %collective-permute-start.3 = (bf16[272,256]{1,0:T(8,128)(2,1)S(1)}, bf16[272,256]{1,0:T(8,128)(2,1)S(1)}, u32[]{:S(2)}, u32[]{:S(2)}) collective-permute-start(bf16[272,256]{1,0:T(8,128)(2,1)S(1)} %collective-permute-done.2.refs_2_), channel_id=1, source_target_pairs={{0,6},{1,7},{2,4},{3,5},{4,2},{5,3},{6,0},{7,1},{8,14},{9,15},{10,... | collective-permute-start | bytes 417800 | tf_op jit(solution)/shard_map/ppermute | solution.py:477
  16.3 2.5 %shard_map.122 = (f32[2048,256]{1,0:T(8,128)S(1)}, bf16[256,2048]{1,0:T(8,128)(2,1)S(1)}) custom-call(bf16[1024,16]{1,0:T(8,128)(2,1)S(1)} %get-tuple-element.13.wave_ref, bf16[272,256]{1,0:T(8,128)(2,1)S(1)} %shard_map.118.own_ref.refs_0_, bf16[272,256]{1,0:T(8,128)(2,1)S(1)} %collective-permute-done.refs_1_, ...), custom_call_target="tpu_custom_call" | custom-call | flops 2969999872 | bytes 2700000 | tf_op jit(solution)/shard_map/pallas_call | solution.py:499
  18.7 0.0 collective-permute-done.6.refs_1_
  18.7 0.0 collective-permute-done.1.refs_2_.refs_0_
  18.8 1.7 %shard_map.123.sums_in_ref = f32[2048,256]{1,0:T(8,128)S(1)} custom-call(bf16[1024,16]{1,0:T(8,128)(2,1)S(1)} %get-tuple-element.13.wave_ref, f32[2048,256]{1,0:T(8,128)S(1)} %get-tuple-element.15.sums_in_ref, bf16[272,256]{1,0:T(8,128)(2,1)S(1)} %collective-permute-done.1.refs_2_.refs_0_, bf16[272,256]{1,0:T(8,128)(2,1)S(1)} %collective-permute-done.6.refs_1_), custom_call_target="tpu_custom_call" | custom-call | flops 1980000000 | bytes 1800000 | tf_op jit(solution)/shard_map/pallas_call | solution.py:512
  20.5 3.9 %collective-permute-done.3.refs_3_.refs_0_ = bf16[272,256]{1,0:T(8,128)(2,1)S(1)} collective-permute-done((bf16[272,256]{1,0:T(8,128)(2,1)S(1)}, bf16[272,256]{1,0:T(8,128)(2,1)S(1)}, u32[]{:S(2)}, u32[]{:S(2)}) %collective-permute-start.3) | collective-permute-done | bytes 139296 | tf_op jit(solution)/shard_map/ppermute | solution.py:477
  24.4 1.0 %shard_map.124.sums_in_ref = f32[2048,256]{1,0:T(8,128)S(1)} custom-call(bf16[1024,16]{1,0:T(8,128)(2,1)S(1)} %get-tuple-element.13.wave_ref, f32[2048,256]{1,0:T(8,128)S(1)} %shard_map.123.sums_in_ref, bf16[272,256]{1,0:T(8,128)(2,1)S(1)} %collective-permute-done.3.refs_3_.refs_0_), custom_call_target="tpu_custom_call" | custom-call | flops 990000000 | bytes 900000 | tf_op jit(solution)/shard_map/pallas_call | solution.py:512
  25.5 0.0 collective-permute-done.8.refs_1_
  25.5 0.0 collective-permute-done.7.refs_0_
  25.5 0.0 copy-start.1
  25.5 0.0 copy-start.2
  25.5 0.0 copy-start.3
  25.6 1.7 %shard_map.125.shared_ref = bf16[2048,256]{1,0:T(8,128)(2,1)S(1)} custom-call(bf16[1024,16]{1,0:T(8,128)(2,1)S(1)} %get-tuple-element.13.wave_ref, f32[2048,256]{1,0:T(8,128)S(1)} %shard_map.124.sums_in_ref, f32[1024,256]{1,0:T(8,128)S(1)} %get-tuple-element.16.weights_ref, bf16[272,256]{1,0:T(8,128)(2,1)S(1)} %collective-permute-done.7.refs_0_, ...), custom_call_target="tpu_custom_call" | custom-call | flops 1980000000 | bytes 1800000 | tf_op jit(solution)/shard_map/pallas_call | solution.py:520
  27.3 0.1 collective-permute-start.9
  27.4 0.2 shard_map.120
  27.6 0.0 copy-start
  27.6 0.6 %collective-permute-start.4 = (bf16[512,256]{1,0:T(8,128)(2,1)S(1)}, bf16[512,256]{1,0:T(8,128)(2,1)S(1)}, u32[]{:S(2)}, u32[]{:S(2)}) collective-permute-start(bf16[512,256]{1,0:T(8,128)(2,1)S(1)} %shard_map.120), channel_id=1, source_target_pairs={{0,1},{1,0},{2,3},{3,2},{4,5},{5,4},{6,7},{7,6},{8,9},{9,8},{10,11... | collective-permute-start | bytes 786440 | tf_op jit(solution)/shard_map/ppermute | solution.py:472
  28.2 0.0 copy-done.1
  28.2 0.0 copy-done.2
  28.2 0.0 copy-done.3
  28.2 1.9 %shard_map.119 = (f32[256,256]{1,0:T(8,128)S(1)}, bf16[4096,512]{1,0:T(8,128)(2,1)S(1)}) custom-call(f32[256,768]{1,0:T(8,128)S(1)} %copy-done.2, s32[256,768]{1,0:T(8,128)S(1)} %copy-done.3, f32[16,256]{1,0:T(8,128)S(1)} %copy-done.1, bf16[272,256]{1,0:T(8,128)(2,1)S(1)} %shard_map.118.own_ref.refs_0_), custom_call_target="tpu_custom_call" | custom-call | flops 2750000128 | bytes 2500000 | tf_op jit(solution)/shard_map/pallas_call | solution.py:489
  30.0 0.4 %collective-permute-done.4.side_ref = bf16[512,256]{1,0:T(8,128)(2,1)S(1)} collective-permute-done((bf16[512,256]{1,0:T(8,128)(2,1)S(1)}, bf16[512,256]{1,0:T(8,128)(2,1)S(1)}, u32[]{:S(2)}, u32[]{:S(2)}) %collective-permute-start.4) | collective-permute-done | bytes 262176 | tf_op jit(solution)/shard_map/ppermute | solution.py:472
  30.4 0.0 copy-done
  30.4 0.0 copy-start.4
  30.4 0.0 copy-start.5
  30.4 0.0 copy-start.8
  30.4 1.5 %shard_map.126.combined_ref = f32[256,256]{1,0:T(8,128)S(1)} custom-call(f32[256,256]{1,0:T(8,128)S(1)} %get-tuple-element.11.near_in_ref, bf16[4096,512]{1,0:T(8,128)(2,1)S(1)} %get-tuple-element.12.far_tiles_ref, f32[16,256]{1,0:T(8,128)S(1)} %copy-done.1, bf16[512,256]{1,0:T(8,128)(2,1)S(1)} %collective-permute-done.4.side_ref, ...), custom_call_target="tpu_custom_call" | custom-call | flops 1650000000 | bytes 1500000 | tf_op jit(solution)/shard_map/pallas_call | solution.py:530
  31.9 0.0 collective-permute-done.9.received_ref
  32.0 0.0 copy-done.4
  32.0 0.0 copy-done.5
  32.0 0.0 copy-done.8
  32.0 1.5 %shard_map.127 = bf16[256,256]{1,0:T(8,128)(2,1)} custom-call(s32[1]{0:T(128)S(6)} %copy.13.count_hbm.count_ref, f32[256,256]{1,0:T(8,128)S(1)} %shard_map.126.combined_ref, bf16[2048,256]{1,0:T(8,128)(2,1)S(1)} %collective-permute-done.9.received_ref, bf16[256,2048]{1,0:T(8,128)(2,1)S(1)} %get-tuple-element.14.turned_ref, f32[1,256]{1,0:T(1,128)S(1)} %bitcast.1, ...), custom_call_target="tpu_custom_call" | custom-call | flops 1100000000 | bytes 1000000 | tf_op jit(solution)/shard_map/pallas_call | solution.py:537
Async XLA Ops:
  0.7 6.9 %copy-start.7 = (s32[3,512]{1,0:T(4,128)S(1)}, s32[3,512]{1,0:T(4,128)}, u32[]{:S(2)}) copy-start(s32[3,512]{1,0:T(4,128)} %own_wave_ref.1) | copy-start | bytes 18436
  0.7 8.9 %copy-start.6 = (f32[16,256]{1,0:T(8,128)S(1)}, f32[16,256]{1,0:T(8,128)}, u32[]{:S(2)}) copy-start(f32[16,256]{1,0:T(8,128)} %filter_long_ref.1) | copy-start | bytes 49156
  1.9 10.9 %collective-permute-start.2 = (bf16[272,256]{1,0:T(8,128)(2,1)S(1)}, bf16[272,256]{1,0:T(8,128)(2,1)S(1)}, u32[]{:S(2)}, u32[]{:S(2)}) collective-permute-start(bf16[272,256]{1,0:T(8,128)(2,1)S(1)} %shard_map.118.own_ref.refs_0_), channel_id=1, source_target_pairs={{0,8},{1,9},{2,10},{3,11},{4,12},{5,13},{6,14},{7,15},{8,0},{9,1},... | collective-permute-start | bytes 417800 | tf_op jit(solution)/shard_map/ppermute | solution.py:469
  6.0 8.9 %collective-permute-start = (bf16[272,256]{1,0:T(8,128)(2,1)S(1)}, bf16[272,256]{1,0:T(8,128)(2,1)S(1)}, u32[]{:S(2)}, u32[]{:S(2)}) collective-permute-start(bf16[272,256]{1,0:T(8,128)(2,1)S(1)} %shard_map.118.own_ref.refs_0_), channel_id=1, source_target_pairs={{0,2},{1,3},{2,0},{3,1},{4,6},{5,7},{6,4},{7,5},{8,10},{9,11},{10,... | collective-permute-start | bytes 417800 | tf_op jit(solution)/shard_map/ppermute | solution.py:469
  7.5 2.0 %collective-permute-start.5 = (s32[3,512]{1,0:T(4,128)S(1)}, s32[3,512]{1,0:T(4,128)S(1)}, u32[]{:S(2)}, u32[]{:S(2)}) collective-permute-start(s32[3,512]{1,0:T(4,128)S(1)} %copy-done.7), channel_id=1, source_target_pairs={{0,1},{1,0},{2,3},{3,2},{4,5},{5,4},{6,7},{7,6},{8,9},{9,8},{10,11... | collective-permute-start | bytes 18440 | tf_op jit(solution)/shard_map/ppermute | solution.py:472
  7.5 11.2 %collective-permute-start.6 = (bf16[272,256]{1,0:T(8,128)(2,1)S(1)}, bf16[272,256]{1,0:T(8,128)(2,1)S(1)}, u32[]{:S(2)}, u32[]{:S(2)}) collective-permute-start(bf16[272,256]{1,0:T(8,128)(2,1)S(1)} %shard_map.118.own_ref.refs_0_), channel_id=1, source_target_pairs={{0,4},{1,5},{2,6},{3,7},{4,0},{5,1},{6,2},{7,3},{8,12},{9,13},{10,... | collective-permute-start | bytes 417800 | tf_op jit(solution)/shard_map/ppermute | solution.py:469
  9.1 9.7 %collective-permute-start.1 = (bf16[272,256]{1,0:T(8,128)(2,1)S(1)}, bf16[272,256]{1,0:T(8,128)(2,1)S(1)}, u32[]{:S(2)}, u32[]{:S(2)}) collective-permute-start(bf16[272,256]{1,0:T(8,128)(2,1)S(1)} %shard_map.118.own_ref.refs_0_), channel_id=1, source_target_pairs={{0,6},{1,7},{2,4},{3,5},{4,2},{5,3},{6,0},{7,1},{8,14},{9,15},{10,... | collective-permute-start | bytes 417800 | tf_op jit(solution)/shard_map/ppermute | solution.py:469
  12.8 12.7 %collective-permute-start.8 = (bf16[272,256]{1,0:T(8,128)(2,1)S(1)}, bf16[272,256]{1,0:T(8,128)(2,1)S(1)}, u32[]{:S(2)}, u32[]{:S(2)}) collective-permute-start(bf16[272,256]{1,0:T(8,128)(2,1)S(1)} %collective-permute-done.2.refs_2_), channel_id=1, source_target_pairs={{0,2},{1,3},{2,0},{3,1},{4,6},{5,7},{6,4},{7,5},{8,10},{9,11},{10,... | collective-permute-start | bytes 417800 | tf_op jit(solution)/shard_map/ppermute | solution.py:477
  14.3 11.2 %collective-permute-start.7 = (bf16[272,256]{1,0:T(8,128)(2,1)S(1)}, bf16[272,256]{1,0:T(8,128)(2,1)S(1)}, u32[]{:S(2)}, u32[]{:S(2)}) collective-permute-start(bf16[272,256]{1,0:T(8,128)(2,1)S(1)} %collective-permute-done.2.refs_2_), channel_id=1, source_target_pairs={{0,4},{1,5},{2,6},{3,7},{4,0},{5,1},{6,2},{7,3},{8,12},{9,13},{10,... | collective-permute-start | bytes 417800 | tf_op jit(solution)/shard_map/ppermute | solution.py:477
  14.9 9.5 %collective-permute-start.3 = (bf16[272,256]{1,0:T(8,128)(2,1)S(1)}, bf16[272,256]{1,0:T(8,128)(2,1)S(1)}, u32[]{:S(2)}, u32[]{:S(2)}) collective-permute-start(bf16[272,256]{1,0:T(8,128)(2,1)S(1)} %collective-permute-done.2.refs_2_), channel_id=1, source_target_pairs={{0,6},{1,7},{2,4},{3,5},{4,2},{5,3},{6,0},{7,1},{8,14},{9,15},{10,... | collective-permute-start | bytes 417800 | tf_op jit(solution)/shard_map/ppermute | solution.py:477
  25.5 2.6 %copy-start.1 = (f32[16,256]{1,0:T(8,128)S(1)}, f32[16,256]{1,0:T(8,128)}, u32[]{:S(2)}) copy-start(f32[16,256]{1,0:T(8,128)} %filter_ref.3) | copy-start | bytes 49156
  25.5 2.6 %copy-start.2 = (f32[256,768]{1,0:T(8,128)S(1)}, f32[256,768]{1,0:T(8,128)}, u32[]{:S(2)}) copy-start(f32[256,768]{1,0:T(8,128)} %distances_ref.1) | copy-start | bytes 2359300
  25.5 2.6 %copy-start.3 = (s32[256,768]{1,0:T(8,128)S(1)}, s32[256,768]{1,0:T(8,128)}, u32[]{:S(2)}) copy-start(s32[256,768]{1,0:T(8,128)} %mask_ref.1) | copy-start | bytes 2359300
  27.3 4.7 %collective-permute-start.9 = (bf16[2048,256]{1,0:T(8,128)(2,1)S(1)}, bf16[2048,256]{1,0:T(8,128)(2,1)S(1)}, u32[]{:S(2)}, u32[]{:S(2)}) collective-permute-start(bf16[2048,256]{1,0:T(8,128)(2,1)S(1)} %shard_map.125.shared_ref), channel_id=1, source_target_pairs={{0,1},{1,0},{2,3},{3,2},{4,5},{5,4},{6,7},{7,6},{8,9},{9,8},{10,11... | collective-permute-start | bytes 3145736 | tf_op jit(solution)/shard_map/ppermute | solution.py:472
  27.6 2.8 %copy-start = (bf16[256,256]{1,0:T(8,128)(2,1)S(1)}, bf16[256,256]{1,0:T(8,128)(2,1)}, u32[]{:S(2)}) copy-start(bf16[256,256]{1,0:T(8,128)(2,1)} %features_ref.1) | copy-start | bytes 393220
  27.6 2.8 %collective-permute-start.4 = (bf16[512,256]{1,0:T(8,128)(2,1)S(1)}, bf16[512,256]{1,0:T(8,128)(2,1)S(1)}, u32[]{:S(2)}, u32[]{:S(2)}) collective-permute-start(bf16[512,256]{1,0:T(8,128)(2,1)S(1)} %shard_map.120), channel_id=1, source_target_pairs={{0,1},{1,0},{2,3},{3,2},{4,5},{5,4},{6,7},{7,6},{8,9},{9,8},{10,11... | collective-permute-start | bytes 786440 | tf_op jit(solution)/shard_map/ppermute | solution.py:472
  30.4 1.6 %copy-start.4 = (bf16[256,256]{1,0:T(8,128)(2,1)S(1)}, bf16[256,256]{1,0:T(8,128)(2,1)}, u32[]{:S(2)}) copy-start(bf16[256,256]{1,0:T(8,128)(2,1)} %w_inner_ref.1) | copy-start | bytes 393220
  30.4 1.6 %copy-start.5 = (bf16[256,256]{1,0:T(8,128)(2,1)S(1)}, bf16[256,256]{1,0:T(8,128)(2,1)}, u32[]{:S(2)}) copy-start(bf16[256,256]{1,0:T(8,128)(2,1)} %w_outer_ref.1) | copy-start | bytes 393220
  30.4 1.6 %copy-start.8 = (f32[256]{0:T(256)S(1)}, f32[256]{0:T(256)}, u32[]{:S(2)}) copy-start(f32[256]{0:T(256)} %param.21) | copy-start | bytes 3076

commit v4 on v3

--- a/solution.py
+++ b/solution.py
@@ -170,44 +170,25 @@
                 turned_ref[:, first : first + block] = slot[rank : rank + block, :rows].T
 
 
-def fetch(sources, targets, semaphores):
-    copies = [
-        pltpu.make_async_copy(source, target, semaphores.at[i])
-        for i, (source, target) in enumerate(zip(sources, targets))
-    ]
-    for copy in copies:
-        copy.start()
-    for copy in copies:
-        copy.wait()
-
-
 def pieces(value):
     high = value.astype(jnp.bfloat16).astype(jnp.float32)
     middle = (value - high).astype(jnp.bfloat16).astype(jnp.float32)
     return high, middle, value - high - middle
 
 
-def prepare_kernel(
-    features_hbm,
-    w_value_hbm,
-    positions_hbm,
-    count_hbm,
-    chunk_ref,
-    features,
-    w_value,
-    positions,
-    count_ref,
-    sems,
-):
-    fetch(
-        (features_hbm, w_value_hbm, positions_hbm, count_hbm),
-        (features, w_value, positions, count_ref),
-        sems,
-    )
+def blank_kernel(blank_ref):
+    blank_ref[...] = jnp.zeros(blank_ref.shape, blank_ref.dtype)
+
+
+def count_kernel(count_ref, blank_ref, held_ref):
+    held_ref[...] = blank_ref[...] + count_ref[0]
+
+
+def prepare_kernel(count_ref, features, w_value, positions, chunk_ref):
     rows = features.shape[0]
     values = jnp.dot(features[...], w_value[...], preferred_element_type=jnp.float32)
     row = lax.broadcasted_iota(jnp.int32, values.shape, 0)
-    chunk_ref[:rows, :] = jnp.where(row < count_ref[0], values, 0.0).astype(jnp.bfloat16)
+    chunk_ref[:rows, :] = jnp.where(row < count_ref[:1, :1], values, 0.0).astype(jnp.bfloat16)
     points = positions[...]
     high, middle, low = pieces(points)
     spare = jnp.zeros((extra_rows - 9, rows), jnp.float32)
@@ -399,10 +380,10 @@
     inner = (inner / (1.0 + jnp.exp(-inner))).astype(jnp.bfloat16)
     result = jnp.dot(inner, w_outer_ref[...], preferred_element_type=jnp.float32)
     row = lax.broadcasted_iota(jnp.int32, result.shape, 0)
-    out_ref[...] = jnp.where(row < count_ref[...].reshape(1, 1), result, 0.0).astype(jnp.bfloat16)
-
-
-hbm = pl.BlockSpec(memory_space=pltpu.HBM)
+    out_ref[...] = jnp.where(row < count_ref[:1, :1], result, 0.0).astype(jnp.bfloat16)
+
+
+smem = pl.BlockSpec(memory_space=pltpu.SMEM)
 vmem = pl.BlockSpec(memory_space=pltpu.VMEM)
 
 
@@ -450,20 +431,12 @@
     over = [(a * cores + c, a * cores + 1 - c) for a in range(blocks) for c in range(cores)]
 
     chunk_rows = rows + extra_rows
+    (blank,) = call(blank_kernel, [], [((8, 128), jnp.int32)], micros=6.0)()
+    counts, blank = lax.optimization_barrier((counts, blank))
+    (held,) = call(count_kernel, [smem, vmem], [((8, 128), jnp.int32)])(counts, blank)
     (chunk,) = call(
-        prepare_kernel,
-        [hbm, hbm, hbm, hbm],
-        [((chunk_rows, width), bf16)],
-        [
-            pltpu.VMEM(features.shape, features.dtype),
-            pltpu.VMEM(w_value.shape, w_value.dtype),
-            pltpu.VMEM(positions.shape, positions.dtype),
-            pltpu.SMEM(counts.shape, counts.dtype),
-            pltpu.SemaphoreType.DMA((4,)),
-        ],
-        micros=6.0,
-        mib=60,
-    )(features, w_value, positions, counts)
+        prepare_kernel, [vmem] * 4, [((chunk_rows, width), bf16)], micros=0.3
+    )(held, features, w_value, positions)
 
     def move(value, mask):
         return lax.ppermute(value, both, across(mask))
@@ -540,7 +513,7 @@
         [((rows, width), bf16)],
         micros=1.0,
         final=True,
-    )(counts, combined, received, turned, jnp.reshape(gain, (1, width)), w_inner, w_outer)[0]
+    )(held, combined, received, turned, jnp.reshape(gain, (1, width)), w_inner, w_outer)[0]
 
 
 def phase_scratch(chunks, rows, waves, blocks=2):

time: 33.7 us -> 32.9 us (0.976)
  Pallas kernels: 13.7 us -> 12.6 us
    pallas_call x1 -> x3, Pallas kernels: 1.21 us -> 0.2 us  [the longest x1 0.2 us: gathered_parts(): call(prepare_kernel, [vmem] * 4, [((chunk_rows, width), bf16)], micros=0.3)]
  transfers between devices with their start and end apart: 10 -> 10, of which waited for: 3 -> 3; matrix products, arithmetic and copies ran while one was open for 0% -> 0% of each run, Pallas kernels for 27% -> 28%
where the time goes in v4:
time: 32.9 us; the launch traced here: 32.8 us
  Pallas kernels  12.6 us (38%)
  starting transfers between devices  11.7 us (36%)
  waiting for transfers between devices  7.23 us (22%)
  between operations  0.88 us (3%)
    ppermute x4, starting transfers between devices, move(): return lax.ppermute(value, both, across(mask))  7.62 us
    ppermute x3, waiting for transfers between devices, gathered_parts(): got[mask] = lax.ppermute(got[starts[0]], both, across(starts[0] ^ mask))  3.95 us
    ppermute x3, starting transfers between devices, gathered_parts(): got[mask] = lax.ppermute(got[starts[0]], both, across(starts[0] ^ mask))  3.49 us
    ppermute x4, waiting for transfers between devices, move(): return lax.ppermute(value, both, across(mask))  2.91 us
    pallas_call x2, Pallas kernels, gathered_parts(): call(more_kernel, [vmem] * (2 + len(masks)), [sums_shape], [phase_scratch...  2.74 us
    pallas_call x1, Pallas kernels, gathered_parts(): call(first_kernel, [vmem] * (1 + len(first)), [sums_shape, ((rows, 2 * wa...  2.46 us
    pallas_call x1, Pallas kernels, gathered_parts(): call(functools.partial(near_kernel, step=step), [vmem] * 4, [((rows, widt...  1.86 us
    pallas_call x1, Pallas kernels, gathered_parts(): call(last_kernel, [vmem] * (3 + len(last)), [(sums_shape[0], bf16)], [pha...  1.72 us
  transfers between devices with their start and end apart: 10, of which 3 were waited for; matrix products, arithmetic and copies ran while one was open for 0% of the time, Pallas kernels for 28%

profile of v4, /device:TPU:0, one launch (start us, length us, event | category | flops | bytes accessed | tf_op | source)
XLA Modules:
  0.0 32.8 jit_solution(11624941089313024734)
XLA Ops:
  0.0 0.0 copy-start
  0.0 0.0 copy-start.4
  0.7 0.0 copy-start.8
  0.7 0.0 copy-start.7
  0.7 0.2 copy-done
  0.9 0.1 copy-done.4
  1.0 0.0 copy-done.9
  1.0 0.2 shard_map.120.own_ref.refs_0_
  1.2 4.1 %collective-permute-start.2 = (bf16[272,256]{1,0:T(8,128)(2,1)S(1)}, bf16[272,256]{1,0:T(8,128)(2,1)S(1)}, u32[]{:S(2)}, u32[]{:S(2)}) collective-permute-start(bf16[272,256]{1,0:T(8,128)(2,1)S(1)} %shard_map.120.own_ref.refs_0_), channel_id=1, source_target_pairs={{0,8},{1,9},{2,10},{3,11},{4,12},{5,13},{6,14},{7,15},{8,0},{9,1},... | collective-permute-start | bytes 417800 | tf_op jit(solution)/shard_map/ppermute | solution.py:442
  5.3 1.5 %collective-permute-start = (bf16[272,256]{1,0:T(8,128)(2,1)S(1)}, bf16[272,256]{1,0:T(8,128)(2,1)S(1)}, u32[]{:S(2)}, u32[]{:S(2)}) collective-permute-start(bf16[272,256]{1,0:T(8,128)(2,1)S(1)} %shard_map.120.own_ref.refs_0_), channel_id=1, source_target_pairs={{0,2},{1,3},{2,0},{3,1},{4,6},{5,7},{6,4},{7,5},{8,10},{9,11},{10,... | collective-permute-start | bytes 417800 | tf_op jit(solution)/shard_map/ppermute | solution.py:442
  6.8 0.0 copy-done.8
  6.8 0.0 collective-permute-start.5
  6.8 1.6 %collective-permute-start.6 = (bf16[272,256]{1,0:T(8,128)(2,1)S(1)}, bf16[272,256]{1,0:T(8,128)(2,1)S(1)}, u32[]{:S(2)}, u32[]{:S(2)}) collective-permute-start(bf16[272,256]{1,0:T(8,128)(2,1)S(1)} %shard_map.120.own_ref.refs_0_), channel_id=1, source_target_pairs={{0,4},{1,5},{2,6},{3,7},{4,0},{5,1},{6,2},{7,3},{8,12},{9,13},{10,... | collective-permute-start | bytes 417800 | tf_op jit(solution)/shard_map/ppermute | solution.py:442
  8.4 0.4 %collective-permute-start.1 = (bf16[272,256]{1,0:T(8,128)(2,1)S(1)}, bf16[272,256]{1,0:T(8,128)(2,1)S(1)}, u32[]{:S(2)}, u32[]{:S(2)}) collective-permute-start(bf16[272,256]{1,0:T(8,128)(2,1)S(1)} %shard_map.120.own_ref.refs_0_), channel_id=1, source_target_pairs={{0,6},{1,7},{2,4},{3,5},{4,2},{5,3},{6,0},{7,1},{8,14},{9,15},{10,... | collective-permute-start | bytes 417800 | tf_op jit(solution)/shard_map/ppermute | solution.py:442
  8.8 0.0 collective-permute-done.5.other_wave_ref
  8.8 0.0 copy-done.7
  8.8 0.4 %shard_map.123 = (bf16[1024,16]{1,0:T(8,128)(2,1)S(1)}, f32[1024,256]{1,0:T(8,128)S(1)}) custom-call(s32[3,512]{1,0:T(4,128)S(1)} %copy-done.8, s32[3,512]{1,0:T(4,128)S(1)} %collective-permute-done.5.other_wave_ref, f32[16,256]{1,0:T(8,128)S(1)} %copy-done.7), custom_call_target="tpu_custom_call" | custom-call | flops 1100000000 | bytes 1000000 | tf_op jit(solution)/shard_map/pallas_call | solution.py:455
  9.2 2.9 %collective-permute-done.2.refs_2_ = bf16[272,256]{1,0:T(8,128)(2,1)S(1)} collective-permute-done((bf16[272,256]{1,0:T(8,128)(2,1)S(1)}, bf16[272,256]{1,0:T(8,128)(2,1)S(1)}, u32[]{:S(2)}, u32[]{:S(2)}) %collective-permute-start.2) | collective-permute-done | bytes 139296 | tf_op jit(solution)/shard_map/ppermute | solution.py:442
  12.1 1.5 %collective-permute-start.8 = (bf16[272,256]{1,0:T(8,128)(2,1)S(1)}, bf16[272,256]{1,0:T(8,128)(2,1)S(1)}, u32[]{:S(2)}, u32[]{:S(2)}) collective-permute-start(bf16[272,256]{1,0:T(8,128)(2,1)S(1)} %collective-permute-done.2.refs_2_), channel_id=1, source_target_pairs={{0,2},{1,3},{2,0},{3,1},{4,6},{5,7},{6,4},{7,5},{8,10},{9,11},{10,... | collective-permute-start | bytes 417800 | tf_op jit(solution)/shard_map/ppermute | solution.py:450
  13.6 0.6 %collective-permute-start.7 = (bf16[272,256]{1,0:T(8,128)(2,1)S(1)}, bf16[272,256]{1,0:T(8,128)(2,1)S(1)}, u32[]{:S(2)}, u32[]{:S(2)}) collective-permute-start(bf16[272,256]{1,0:T(8,128)(2,1)S(1)} %collective-permute-done.2.refs_2_), channel_id=1, source_target_pairs={{0,4},{1,5},{2,6},{3,7},{4,0},{5,1},{6,2},{7,3},{8,12},{9,13},{10,... | collective-permute-start | bytes 417800 | tf_op jit(solution)/shard_map/ppermute | solution.py:450
  14.2 0.0 collective-permute-done.refs_1_
  14.2 1.3 %collective-permute-start.3 = (bf16[272,256]{1,0:T(8,128)(2,1)S(1)}, bf16[272,256]{1,0:T(8,128)(2,1)S(1)}, u32[]{:S(2)}, u32[]{:S(2)}) collective-permute-start(bf16[272,256]{1,0:T(8,128)(2,1)S(1)} %collective-permute-done.2.refs_2_), channel_id=1, source_target_pairs={{0,6},{1,7},{2,4},{3,5},{4,2},{5,3},{6,0},{7,1},{8,14},{9,15},{10,... | collective-permute-start | bytes 417800 | tf_op jit(solution)/shard_map/ppermute | solution.py:450
  15.6 2.5 %shard_map.124 = (f32[2048,256]{1,0:T(8,128)S(1)}, bf16[256,2048]{1,0:T(8,128)(2,1)S(1)}) custom-call(bf16[1024,16]{1,0:T(8,128)(2,1)S(1)} %get-tuple-element.17.wave_ref, bf16[272,256]{1,0:T(8,128)(2,1)S(1)} %shard_map.120.own_ref.refs_0_, bf16[272,256]{1,0:T(8,128)(2,1)S(1)} %collective-permute-done.refs_1_, ...), custom_call_target="tpu_custom_call" | custom-call | flops 2969999872 | bytes 2700000 | tf_op jit(solution)/shard_map/pallas_call | solution.py:472
  18.0 0.0 collective-permute-done.6.refs_1_
  18.0 0.0 collective-permute-done.1.refs_2_.refs_0_
  18.1 1.7 %shard_map.125.sums_in_ref = f32[2048,256]{1,0:T(8,128)S(1)} custom-call(bf16[1024,16]{1,0:T(8,128)(2,1)S(1)} %get-tuple-element.17.wave_ref, f32[2048,256]{1,0:T(8,128)S(1)} %get-tuple-element.19.sums_in_ref, bf16[272,256]{1,0:T(8,128)(2,1)S(1)} %collective-permute-done.1.refs_2_.refs_0_, bf16[272,256]{1,0:T(8,128)(2,1)S(1)} %collective-permute-done.6.refs_1_), custom_call_target="tpu_custom_call" | custom-call | flops 1980000000 | bytes 1800000 | tf_op jit(solution)/shard_map/pallas_call | solution.py:485
  19.8 3.9 %collective-permute-done.3.refs_3_.refs_0_ = bf16[272,256]{1,0:T(8,128)(2,1)S(1)} collective-permute-done((bf16[272,256]{1,0:T(8,128)(2,1)S(1)}, bf16[272,256]{1,0:T(8,128)(2,1)S(1)}, u32[]{:S(2)}, u32[]{:S(2)}) %collective-permute-start.3) | collective-permute-done | bytes 139296 | tf_op jit(solution)/shard_map/ppermute | solution.py:450
  23.7 1.0 %shard_map.126.sums_in_ref = f32[2048,256]{1,0:T(8,128)S(1)} custom-call(bf16[1024,16]{1,0:T(8,128)(2,1)S(1)} %get-tuple-element.17.wave_ref, f32[2048,256]{1,0:T(8,128)S(1)} %shard_map.125.sums_in_ref, bf16[272,256]{1,0:T(8,128)(2,1)S(1)} %collective-permute-done.3.refs_3_.refs_0_), custom_call_target="tpu_custom_call" | custom-call | flops 990000000 | bytes 900000 | tf_op jit(solution)/shard_map/pallas_call | solution.py:485
  24.8 0.0 collective-permute-done.8.refs_1_
  24.8 0.0 collective-permute-done.7.refs_0_
  24.8 0.0 copy-start.1
  24.8 0.0 copy-start.2
  24.8 0.0 copy-start.3
  24.8 1.7 %shard_map.127.shared_ref = bf16[2048,256]{1,0:T(8,128)(2,1)S(1)} custom-call(bf16[1024,16]{1,0:T(8,128)(2,1)S(1)} %get-tuple-element.17.wave_ref, f32[2048,256]{1,0:T(8,128)S(1)} %shard_map.126.sums_in_ref, f32[1024,256]{1,0:T(8,128)S(1)} %get-tuple-element.20.weights_ref, bf16[272,256]{1,0:T(8,128)(2,1)S(1)} %collective-permute-done.7.refs_0_, ...), custom_call_target="tpu_custom_call" | custom-call | flops 1980000000 | bytes 1800000 | tf_op jit(solution)/shard_map/pallas_call | solution.py:493
  26.6 0.1 collective-permute-start.9
  26.6 0.2 shard_map.122
  26.9 0.6 %collective-permute-start.4 = (bf16[512,256]{1,0:T(8,128)(2,1)S(1)}, bf16[512,256]{1,0:T(8,128)(2,1)S(1)}, u32[]{:S(2)}, u32[]{:S(2)}) collective-permute-start(bf16[512,256]{1,0:T(8,128)(2,1)S(1)} %shard_map.122), channel_id=1, source_target_pairs={{0,1},{1,0},{2,3},{3,2},{4,5},{5,4},{6,7},{7,6},{8,9},{9,8},{10,11... | collective-permute-start | bytes 786440 | tf_op jit(solution)/shard_map/ppermute | solution.py:445
  27.4 0.0 copy-done.1
  27.4 0.0 copy-done.2
  27.4 0.0 copy-done.3
  27.4 1.9 %shard_map.121 = (f32[256,256]{1,0:T(8,128)S(1)}, bf16[4096,512]{1,0:T(8,128)(2,1)S(1)}) custom-call(f32[256,768]{1,0:T(8,128)S(1)} %copy-done.2, s32[256,768]{1,0:T(8,128)S(1)} %copy-done.3, f32[16,256]{1,0:T(8,128)S(1)} %copy-done.1, bf16[272,256]{1,0:T(8,128)(2,1)S(1)} %shard_map.120.own_ref.refs_0_), custom_call_target="tpu_custom_call" | custom-call | flops 2750000128 | bytes 2500000 | tf_op jit(solution)/shard_map/pallas_call | solution.py:462
  29.3 0.4 %collective-permute-done.4.side_ref = bf16[512,256]{1,0:T(8,128)(2,1)S(1)} collective-permute-done((bf16[512,256]{1,0:T(8,128)(2,1)S(1)}, bf16[512,256]{1,0:T(8,128)(2,1)S(1)}, u32[]{:S(2)}, u32[]{:S(2)}) %collective-permute-start.4) | collective-permute-done | bytes 262176 | tf_op jit(solution)/shard_map/ppermute | solution.py:445
  29.7 1.5 %shard_map.128.combined_ref = f32[256,256]{1,0:T(8,128)S(1)} custom-call(f32[256,256]{1,0:T(8,128)S(1)} %get-tuple-element.15.near_in_ref, bf16[4096,512]{1,0:T(8,128)(2,1)S(1)} %get-tuple-element.16.far_tiles_ref, f32[16,256]{1,0:T(8,128)S(1)} %copy-done.1, bf16[512,256]{1,0:T(8,128)(2,1)S(1)} %collective-permute-done.4.side_ref, ...), custom_call_target="tpu_custom_call" | custom-call | flops 1650000000 | bytes 1500000 | tf_op jit(solution)/shard_map/pallas_call | solution.py:503
  31.2 0.0 collective-permute-done.9.received_ref
  31.2 0.0 copy-done.5
  31.2 0.0 copy-done.6
  31.3 0.0 copy-done.10
  31.3 1.5 %shard_map.129 = bf16[256,256]{1,0:T(8,128)(2,1)} custom-call(s32[8,128]{1,0:T(8,128)S(1)} %shard_map.119.count_ref, f32[256,256]{1,0:T(8,128)S(1)} %shard_map.128.combined_ref, bf16[2048,256]{1,0:T(8,128)(2,1)S(1)} %collective-permute-done.9.received_ref, bf16[256,2048]{1,0:T(8,128)(2,1)S(1)} %get-tuple-element.18.turned_ref, f32[1,256]{1,0:T(1,128)S(1)} %bitcast.1, ...), custom_call_target="tpu_custom_call" | custom-call | flops 1100000000 | bytes 1000000 | tf_op jit(solution)/shard_map/pallas_call | solution.py:510
  (6 shorter events, 0.0 us)
Async XLA Ops:
  0.0 0.9 %copy-start = (bf16[256,256]{1,0:T(8,128)(2,1)S(1)}, bf16[256,256]{1,0:T(8,128)(2,1)}, u32[]{:S(2)}) copy-start(bf16[256,256]{1,0:T(8,128)(2,1)} %features_ref.1) | copy-start | bytes 393220
  0.0 1.0 %copy-start.4 = (bf16[256,256]{1,0:T(8,128)(2,1)S(1)}, bf16[256,256]{1,0:T(8,128)(2,1)}, u32[]{:S(2)}) copy-start(bf16[256,256]{1,0:T(8,128)(2,1)} %w_value.1) | copy-start | bytes 393220
  0.0 1.0 %copy-start.9 = (f32[3,256]{1,0:T(4,128)S(1)}, f32[3,256]{1,0:T(4,128)}, u32[]{:S(2)}) copy-start(f32[3,256]{1,0:T(4,128)} %positions.1) | copy-start | bytes 9220
  0.7 6.1 %copy-start.8 = (s32[3,512]{1,0:T(4,128)S(1)}, s32[3,512]{1,0:T(4,128)}, u32[]{:S(2)}) copy-start(s32[3,512]{1,0:T(4,128)} %own_wave_ref.1) | copy-start | bytes 18436
  0.7 8.1 %copy-start.7 = (f32[16,256]{1,0:T(8,128)S(1)}, f32[16,256]{1,0:T(8,128)}, u32[]{:S(2)}) copy-start(f32[16,256]{1,0:T(8,128)} %filter_long_ref.1) | copy-start | bytes 49156
  1.2 10.9 %collective-permute-start.2 = (bf16[272,256]{1,0:T(8,128)(2,1)S(1)}, bf16[272,256]{1,0:T(8,128)(2,1)S(1)}, u32[]{:S(2)}, u32[]{:S(2)}) collective-permute-start(bf16[272,256]{1,0:T(8,128)(2,1)S(1)} %shard_map.120.own_ref.refs_0_), channel_id=1, source_target_pairs={{0,8},{1,9},{2,10},{3,11},{4,12},{5,13},{6,14},{7,15},{8,0},{9,1},... | collective-permute-start | bytes 417800 | tf_op jit(solution)/shard_map/ppermute | solution.py:442
  5.3 8.9 %collective-permute-start = (bf16[272,256]{1,0:T(8,128)(2,1)S(1)}, bf16[272,256]{1,0:T(8,128)(2,1)S(1)}, u32[]{:S(2)}, u32[]{:S(2)}) collective-permute-start(bf16[272,256]{1,0:T(8,128)(2,1)S(1)} %shard_map.120.own_ref.refs_0_), channel_id=1, source_target_pairs={{0,2},{1,3},{2,0},{3,1},{4,6},{5,7},{6,4},{7,5},{8,10},{9,11},{10,... | collective-permute-start | bytes 417800 | tf_op jit(solution)/shard_map/ppermute | solution.py:442
  6.8 2.0 %collective-permute-start.5 = (s32[3,512]{1,0:T(4,128)S(1)}, s32[3,512]{1,0:T(4,128)S(1)}, u32[]{:S(2)}, u32[]{:S(2)}) collective-permute-start(s32[3,512]{1,0:T(4,128)S(1)} %copy-done.8), channel_id=1, source_target_pairs={{0,1},{1,0},{2,3},{3,2},{4,5},{5,4},{6,7},{7,6},{8,9},{9,8},{10,11... | collective-permute-start | bytes 18440 | tf_op jit(solution)/shard_map/ppermute | solution.py:445
  6.8 11.2 %collective-permute-start.6 = (bf16[272,256]{1,0:T(8,128)(2,1)S(1)}, bf16[272,256]{1,0:T(8,128)(2,1)S(1)}, u32[]{:S(2)}, u32[]{:S(2)}) collective-permute-start(bf16[272,256]{1,0:T(8,128)(2,1)S(1)} %shard_map.120.own_ref.refs_0_), channel_id=1, source_target_pairs={{0,4},{1,5},{2,6},{3,7},{4,0},{5,1},{6,2},{7,3},{8,12},{9,13},{10,... | collective-permute-start | bytes 417800 | tf_op jit(solution)/shard_map/ppermute | solution.py:442
  8.4 9.7 %collective-permute-start.1 = (bf16[272,256]{1,0:T(8,128)(2,1)S(1)}, bf16[272,256]{1,0:T(8,128)(2,1)S(1)}, u32[]{:S(2)}, u32[]{:S(2)}) collective-permute-start(bf16[272,256]{1,0:T(8,128)(2,1)S(1)} %shard_map.120.own_ref.refs_0_), channel_id=1, source_target_pairs={{0,6},{1,7},{2,4},{3,5},{4,2},{5,3},{6,0},{7,1},{8,14},{9,15},{10,... | collective-permute-start | bytes 417800 | tf_op jit(solution)/shard_map/ppermute | solution.py:442
  12.1 12.7 %collective-permute-start.8 = (bf16[272,256]{1,0:T(8,128)(2,1)S(1)}, bf16[272,256]{1,0:T(8,128)(2,1)S(1)}, u32[]{:S(2)}, u32[]{:S(2)}) collective-permute-start(bf16[272,256]{1,0:T(8,128)(2,1)S(1)} %collective-permute-done.2.refs_2_), channel_id=1, source_target_pairs={{0,2},{1,3},{2,0},{3,1},{4,6},{5,7},{6,4},{7,5},{8,10},{9,11},{10,... | collective-permute-start | bytes 417800 | tf_op jit(solution)/shard_map/ppermute | solution.py:450
  13.6 11.2 %collective-permute-start.7 = (bf16[272,256]{1,0:T(8,128)(2,1)S(1)}, bf16[272,256]{1,0:T(8,128)(2,1)S(1)}, u32[]{:S(2)}, u32[]{:S(2)}) collective-permute-start(bf16[272,256]{1,0:T(8,128)(2,1)S(1)} %collective-permute-done.2.refs_2_), channel_id=1, source_target_pairs={{0,4},{1,5},{2,6},{3,7},{4,0},{5,1},{6,2},{7,3},{8,12},{9,13},{10,... | collective-permute-start | bytes 417800 | tf_op jit(solution)/shard_map/ppermute | solution.py:450
  14.2 9.5 %collective-permute-start.3 = (bf16[272,256]{1,0:T(8,128)(2,1)S(1)}, bf16[272,256]{1,0:T(8,128)(2,1)S(1)}, u32[]{:S(2)}, u32[]{:S(2)}) collective-permute-start(bf16[272,256]{1,0:T(8,128)(2,1)S(1)} %collective-permute-done.2.refs_2_), channel_id=1, source_target_pairs={{0,6},{1,7},{2,4},{3,5},{4,2},{5,3},{6,0},{7,1},{8,14},{9,15},{10,... | collective-permute-start | bytes 417800 | tf_op jit(solution)/shard_map/ppermute | solution.py:450
  24.8 2.6 %copy-start.1 = (f32[16,256]{1,0:T(8,128)S(1)}, f32[16,256]{1,0:T(8,128)}, u32[]{:S(2)}) copy-start(f32[16,256]{1,0:T(8,128)} %filter_ref.3) | copy-start | bytes 49156
  24.8 2.6 %copy-start.2 = (f32[256,768]{1,0:T(8,128)S(1)}, f32[256,768]{1,0:T(8,128)}, u32[]{:S(2)}) copy-start(f32[256,768]{1,0:T(8,128)} %distances_ref.1) | copy-start | bytes 2359300
  24.8 2.6 %copy-start.3 = (s32[256,768]{1,0:T(8,128)S(1)}, s32[256,768]{1,0:T(8,128)}, u32[]{:S(2)}) copy-start(s32[256,768]{1,0:T(8,128)} %mask_ref.1) | copy-start | bytes 2359300
  26.6 4.7 %collective-permute-start.9 = (bf16[2048,256]{1,0:T(8,128)(2,1)S(1)}, bf16[2048,256]{1,0:T(8,128)(2,1)S(1)}, u32[]{:S(2)}, u32[]{:S(2)}) collective-permute-start(bf16[2048,256]{1,0:T(8,128)(2,1)S(1)} %shard_map.127.shared_ref), channel_id=1, source_target_pairs={{0,1},{1,0},{2,3},{3,2},{4,5},{5,4},{6,7},{7,6},{8,9},{9,8},{10,11... | collective-permute-start | bytes 3145736 | tf_op jit(solution)/shard_map/ppermute | solution.py:445
  26.9 2.8 %collective-permute-start.4 = (bf16[512,256]{1,0:T(8,128)(2,1)S(1)}, bf16[512,256]{1,0:T(8,128)(2,1)S(1)}, u32[]{:S(2)}, u32[]{:S(2)}) collective-permute-start(bf16[512,256]{1,0:T(8,128)(2,1)S(1)} %shard_map.122), channel_id=1, source_target_pairs={{0,1},{1,0},{2,3},{3,2},{4,5},{5,4},{6,7},{7,6},{8,9},{9,8},{10,11... | collective-permute-start | bytes 786440 | tf_op jit(solution)/shard_map/ppermute | solution.py:445
  29.7 1.6 %copy-start.5 = (bf16[256,256]{1,0:T(8,128)(2,1)S(1)}, bf16[256,256]{1,0:T(8,128)(2,1)}, u32[]{:S(2)}) copy-start(bf16[256,256]{1,0:T(8,128)(2,1)} %w_inner_ref.1) | copy-start | bytes 393220
  29.7 1.6 %copy-start.6 = (bf16[256,256]{1,0:T(8,128)(2,1)S(1)}, bf16[256,256]{1,0:T(8,128)(2,1)}, u32[]{:S(2)}) copy-start(bf16[256,256]{1,0:T(8,128)(2,1)} %w_outer_ref.1) | copy-start | bytes 393220
  29.7 1.6 %copy-start.10 = (f32[256]{0:T(256)S(1)}, f32[256]{0:T(256)}, u32[]{:S(2)}) copy-start(f32[256]{0:T(256)} %param.21) | copy-start | bytes 3076

commit v5 on v4

--- a/solution.py
+++ b/solution.py
@@ -230,13 +230,17 @@
     add_sums(sums_in_ref, sums_ref, chunks, wave_ref, phase_ref)
 
 
-def last_kernel(wave_ref, sums_in_ref, weights_ref, *refs):
+def last_kernel(half, wave_ref, sums_in_ref, weights_ref, *refs):
     chunks, (shared_ref, phase_ref, sums_ref) = refs[:-3], refs[-3:]
-    add_sums(sums_in_ref, sums_ref, chunks, wave_ref, phase_ref)
-    wave_count = wave_ref.shape[0]
-    for start in (0, wave_count):
-        part = slice(start, start + wave_count)
-        shared_ref[part, :] = (sums_ref[part, :] * weights_ref[...]).astype(jnp.bfloat16)
+    block = shared_ref.shape[0] // 2
+    waves = wave_ref.at[half * block : (half + 1) * block]
+    add_sums(None, sums_ref, chunks, waves, phase_ref)
+    for rank in range(2):
+        part = slice(rank * block, (rank + 1) * block)
+        first = (2 * rank + half) * block
+        total = sums_in_ref[first : first + block, :] + sums_ref[part, :]
+        weights = weights_ref[half * block : (half + 1) * block, :]
+        shared_ref[part, :] = (total * weights).astype(jnp.bfloat16)
 
 
 def weighted(products, rows, filter_ref):
@@ -335,6 +339,12 @@
             out_ref[rows:, :] = chunk[:rows, :]
 
 
+def joined(mine_ref, others_ref):
+    block = mine_ref.shape[0] // 2
+    parts = [ref[i * block : (i + 1) * block, :] for i in range(2) for ref in (mine_ref, others_ref)]
+    return jnp.concatenate(parts, axis=0)
+
+
 def beyond_kernel(
     scale,
     near_in_ref,
@@ -343,12 +353,14 @@
     side_ref,
     features_ref,
     turned_ref,
-    shared_ref,
+    mine_ref,
+    others_ref,
     combined_ref,
 ):
     rows = near_in_ref.shape[0]
     found = jnp.dot(far_tiles_ref[...], side_ref[...], preferred_element_type=jnp.float32)
-    far = jnp.dot(turned_ref[...], shared_ref[...], preferred_element_type=jnp.float32)
+    shared = joined(mine_ref, others_ref)
+    far = jnp.dot(turned_ref[...], shared, preferred_element_type=jnp.float32)
     combined_ref[...] = (
         features_ref[...].astype(jnp.float32)
         + near_in_ref[...]
@@ -361,17 +373,15 @@
     scale,
     count_ref,
     combined_ref,
-    received_ref,
+    mine_ref,
+    others_ref,
     turned_ref,
     gain_ref,
     w_inner_ref,
     w_outer_ref,
     out_ref,
 ):
-    quarter = received_ref.shape[0] // 4
-    received = jnp.concatenate(
-        [received_ref[i * quarter : (i + 1) * quarter, :] for i in (1, 0, 3, 2)], axis=0
-    )
+    received = joined(mine_ref, others_ref)
     far = jnp.dot(turned_ref[...], received, preferred_element_type=jnp.float32)
     combined = combined_ref[...] + far * scale
     spread = lax.rsqrt(jnp.mean(combined * combined, axis=-1, keepdims=True) + 1e-06)
@@ -490,30 +500,33 @@
             micros=0.9 * len(masks),
             mib=12,
         )(waves, sums, *(got[mask] for mask in masks))
-    (shared,) = call(
-        last_kernel,
-        [vmem] * (3 + len(last)),
-        [(sums_shape[0], bf16)],
-        [phase_scratch(len(last), rows, wave_total), pltpu.VMEM(sums_shape[0], f32)],
-        micros=0.9 * len(last),
-        mib=12,
-    )(waves, sums, wave_weights, *(got[mask] for mask in last))
-    received = swap(shared)
+    shared, received = [], []
+    half_shape = (sums_shape[0][0] // 2, width)
+    for half in range(2):
+        shared += call(
+            functools.partial(last_kernel, half),
+            [vmem] * (3 + len(last)),
+            [(half_shape, bf16)],
+            [phase_scratch(len(last), rows, wave_total // 2), pltpu.VMEM(half_shape, f32)],
+            micros=0.5 * len(last),
+            mib=12,
+        )(waves, sums, wave_weights, *(got[mask] for mask in last))
+        received.append(swap(shared[half]))
     scale = float(wave_total) ** -0.5
     (combined,) = call(
         functools.partial(beyond_kernel, scale),
-        [vmem] * 7,
+        [vmem] * 8,
         [((rows, width), f32)],
         micros=1.5,
         mib=12,
-    )(near, far_tiles, filter_short, side, features, turned, shared)
+    )(near, far_tiles, filter_short, side, features, turned, *shared)
     return call(
         functools.partial(update_kernel, scale),
-        [vmem] * 7,
+        [vmem] * 8,
         [((rows, width), bf16)],
         micros=1.0,
         final=True,
-    )(held, combined, received, turned, jnp.reshape(gain, (1, width)), w_inner, w_outer)[0]
+    )(held, combined, *received[::-1], turned, jnp.reshape(gain, (1, width)), w_inner, w_outer)[0]
 
 
 def phase_scratch(chunks, rows, waves, blocks=2):

time: 32.9 us -> 31.8 us (0.967)
  waiting for transfers between devices: 7.23 us -> 5.64 us
  Pallas kernels: 12.6 us -> 13 us
    ppermute x3, waiting for transfers between devices: 3.95 us -> 2.75 us  [gathered_parts(): got[mask] = lax.ppermute(got[starts[0]], both, across(starts[0] ^ mask))]
    ppermute x3 -> x4, waiting for transfers between devices: 0.37 us -> 0.01 us  [swap(): return lax.ppermute(value, both, over)]
    pallas_call x3 -> x4, Pallas kernels: 4.77 us -> 5.1 us  [the longest x2 2.01 us: gathered_parts(): call(functools.partial(last_kernel, half), [vmem] * (3 + len(last)), [(ha...]
    ppermute x3 -> x4, starting transfers between devices: 0.63 us -> 0.72 us  [swap(): return lax.ppermute(value, both, over)]
  transfers between devices with their start and end apart: 10 -> 11, of which waited for: 3 -> 3; matrix products, arithmetic and copies ran while one was open for 0% -> 0% of each run, Pallas kernels for 28% -> 32%
where the time goes in v5:
time: 31.8 us; the launch traced here: 31.7 us
  Pallas kernels  13 us (41%)
  starting transfers between devices  11.8 us (37%)
  waiting for transfers between devices  5.64 us (18%)
  between operations  0.94 us (3%)
    ppermute x4, starting transfers between devices, move(): return lax.ppermute(value, both, across(mask))  7.62 us
    ppermute x3, starting transfers between devices, gathered_parts(): got[mask] = lax.ppermute(got[starts[0]], both, across(starts[0] ^ mask))  3.49 us
    ppermute x4, waiting for transfers between devices, move(): return lax.ppermute(value, both, across(mask))  2.87 us
    ppermute x3, waiting for transfers between devices, gathered_parts(): got[mask] = lax.ppermute(got[starts[0]], both, across(starts[0] ^ mask))  2.75 us
    pallas_call x2, Pallas kernels, gathered_parts(): call(more_kernel, [vmem] * (2 + len(masks)), [sums_shape], [phase_scratch...  2.75 us
    pallas_call x1, Pallas kernels, gathered_parts(): call(first_kernel, [vmem] * (1 + len(first)), [sums_shape, ((rows, 2 * wa...  2.46 us
    pallas_call x2, Pallas kernels, gathered_parts(): call(functools.partial(last_kernel, half), [vmem] * (3 + len(last)), [(ha...  2.01 us
    pallas_call x1, Pallas kernels, gathered_parts(): call(functools.partial(near_kernel, step=step), [vmem] * 4, [((rows, widt...  1.86 us
  transfers between devices with their start and end apart: 11, of which 3 were waited for; matrix products, arithmetic and copies ran while one was open for 0% of the time, Pallas kernels for 32%

profile of v5, /device:TPU:0, one launch (start us, length us, event | category | flops | bytes accessed | tf_op | source)
XLA Modules:
  0.0 31.7 jit_solution(15166363803079733164)
XLA Ops:
  0.7 0.0 copy-start.8
  0.7 0.0 copy-start.7
  0.7 0.2 copy-done
  0.9 0.1 copy-done.4
  1.0 0.0 copy-done.9
  1.0 0.2 shard_map.120.own_ref.refs_0_
  1.2 4.1 %collective-permute-start.2 = (bf16[272,256]{1,0:T(8,128)(2,1)S(1)}, bf16[272,256]{1,0:T(8,128)(2,1)S(1)}, u32[]{:S(2)}, u32[]{:S(2)}) collective-permute-start(bf16[272,256]{1,0:T(8,128)(2,1)S(1)} %shard_map.120.own_ref.refs_0_), channel_id=1, source_target_pairs={{0,8},{1,9},{2,10},{3,11},{4,12},{5,13},{6,14},{7,15},{8,0},{9,1},... | collective-permute-start | bytes 417800 | tf_op jit(solution)/shard_map/ppermute | solution.py:452
  5.3 1.5 %collective-permute-start = (bf16[272,256]{1,0:T(8,128)(2,1)S(1)}, bf16[272,256]{1,0:T(8,128)(2,1)S(1)}, u32[]{:S(2)}, u32[]{:S(2)}) collective-permute-start(bf16[272,256]{1,0:T(8,128)(2,1)S(1)} %shard_map.120.own_ref.refs_0_), channel_id=1, source_target_pairs={{0,2},{1,3},{2,0},{3,1},{4,6},{5,7},{6,4},{7,5},{8,10},{9,11},{10,... | collective-permute-start | bytes 417800 | tf_op jit(solution)/shard_map/ppermute | solution.py:452
  6.8 0.0 copy-done.8
  6.8 0.0 collective-permute-start.5
  6.8 1.5 %collective-permute-start.1 = (bf16[272,256]{1,0:T(8,128)(2,1)S(1)}, bf16[272,256]{1,0:T(8,128)(2,1)S(1)}, u32[]{:S(2)}, u32[]{:S(2)}) collective-permute-start(bf16[272,256]{1,0:T(8,128)(2,1)S(1)} %shard_map.120.own_ref.refs_0_), channel_id=1, source_target_pairs={{0,6},{1,7},{2,4},{3,5},{4,2},{5,3},{6,0},{7,1},{8,14},{9,15},{10,... | collective-permute-start | bytes 417800 | tf_op jit(solution)/shard_map/ppermute | solution.py:452
  8.4 0.5 %collective-permute-start.6 = (bf16[272,256]{1,0:T(8,128)(2,1)S(1)}, bf16[272,256]{1,0:T(8,128)(2,1)S(1)}, u32[]{:S(2)}, u32[]{:S(2)}) collective-permute-start(bf16[272,256]{1,0:T(8,128)(2,1)S(1)} %shard_map.120.own_ref.refs_0_), channel_id=1, source_target_pairs={{0,4},{1,5},{2,6},{3,7},{4,0},{5,1},{6,2},{7,3},{8,12},{9,13},{10,... | collective-permute-start | bytes 417800 | tf_op jit(solution)/shard_map/ppermute | solution.py:452
  8.8 0.0 collective-permute-done.5.other_wave_ref
  8.8 0.0 copy-done.7
  8.8 0.4 %shard_map.123 = (bf16[1024,16]{1,0:T(8,128)(2,1)S(1)}, f32[1024,256]{1,0:T(8,128)S(1)}) custom-call(s32[3,512]{1,0:T(4,128)S(1)} %copy-done.8, s32[3,512]{1,0:T(4,128)S(1)} %collective-permute-done.5.other_wave_ref, f32[16,256]{1,0:T(8,128)S(1)} %copy-done.7), custom_call_target="tpu_custom_call" | custom-call | flops 1100000000 | bytes 1000000 | tf_op jit(solution)/shard_map/pallas_call | solution.py:465
  9.2 2.9 %collective-permute-done.2.refs_2_ = bf16[272,256]{1,0:T(8,128)(2,1)S(1)} collective-permute-done((bf16[272,256]{1,0:T(8,128)(2,1)S(1)}, bf16[272,256]{1,0:T(8,128)(2,1)S(1)}, u32[]{:S(2)}, u32[]{:S(2)}) %collective-permute-start.2) | collective-permute-done | bytes 139296 | tf_op jit(solution)/shard_map/ppermute | solution.py:452
  12.1 1.6 %collective-permute-start.3 = (bf16[272,256]{1,0:T(8,128)(2,1)S(1)}, bf16[272,256]{1,0:T(8,128)(2,1)S(1)}, u32[]{:S(2)}, u32[]{:S(2)}) collective-permute-start(bf16[272,256]{1,0:T(8,128)(2,1)S(1)} %collective-permute-done.2.refs_2_), channel_id=1, source_target_pairs={{0,6},{1,7},{2,4},{3,5},{4,2},{5,3},{6,0},{7,1},{8,14},{9,15},{10,... | collective-permute-start | bytes 417800 | tf_op jit(solution)/shard_map/ppermute | solution.py:460
  13.7 1.4 %collective-permute-start.7 = (bf16[272,256]{1,0:T(8,128)(2,1)S(1)}, bf16[272,256]{1,0:T(8,128)(2,1)S(1)}, u32[]{:S(2)}, u32[]{:S(2)}) collective-permute-start(bf16[272,256]{1,0:T(8,128)(2,1)S(1)} %collective-permute-done.2.refs_2_), channel_id=1, source_target_pairs={{0,4},{1,5},{2,6},{3,7},{4,0},{5,1},{6,2},{7,3},{8,12},{9,13},{10,... | collective-permute-start | bytes 417800 | tf_op jit(solution)/shard_map/ppermute | solution.py:460
  15.1 0.0 collective-permute-done.refs_1_
  15.1 0.5 %collective-permute-start.8 = (bf16[272,256]{1,0:T(8,128)(2,1)S(1)}, bf16[272,256]{1,0:T(8,128)(2,1)S(1)}, u32[]{:S(2)}, u32[]{:S(2)}) collective-permute-start(bf16[272,256]{1,0:T(8,128)(2,1)S(1)} %collective-permute-done.2.refs_2_), channel_id=1, source_target_pairs={{0,2},{1,3},{2,0},{3,1},{4,6},{5,7},{6,4},{7,5},{8,10},{9,11},{10,... | collective-permute-start | bytes 417800 | tf_op jit(solution)/shard_map/ppermute | solution.py:460
  15.6 2.5 %shard_map.124 = (f32[2048,256]{1,0:T(8,128)S(1)}, bf16[256,2048]{1,0:T(8,128)(2,1)S(1)}) custom-call(bf16[1024,16]{1,0:T(8,128)(2,1)S(1)} %get-tuple-element.17.wave_ref, bf16[272,256]{1,0:T(8,128)(2,1)S(1)} %shard_map.120.own_ref.refs_0_, bf16[272,256]{1,0:T(8,128)(2,1)S(1)} %collective-permute-done.refs_1_, ...), custom_call_target="tpu_custom_call" | custom-call | flops 2969999872 | bytes 2700000 | tf_op jit(solution)/shard_map/pallas_call | solution.py:482
  18.0 0.0 collective-permute-done.1.refs_2_.refs_0_
  18.0 0.0 collective-permute-done.6.refs_1_
  18.1 1.7 %shard_map.125.sums_in_ref = f32[2048,256]{1,0:T(8,128)S(1)} custom-call(bf16[1024,16]{1,0:T(8,128)(2,1)S(1)} %get-tuple-element.17.wave_ref, f32[2048,256]{1,0:T(8,128)S(1)} %get-tuple-element.19.sums_in_ref, bf16[272,256]{1,0:T(8,128)(2,1)S(1)} %collective-permute-done.1.refs_2_.refs_0_, bf16[272,256]{1,0:T(8,128)(2,1)S(1)} %collective-permute-done.6.refs_1_), custom_call_target="tpu_custom_call" | custom-call | flops 1980000000 | bytes 1800000 | tf_op jit(solution)/shard_map/pallas_call | solution.py:495
  19.8 2.1 %collective-permute-done.3.refs_3_.refs_0_ = bf16[272,256]{1,0:T(8,128)(2,1)S(1)} collective-permute-done((bf16[272,256]{1,0:T(8,128)(2,1)S(1)}, bf16[272,256]{1,0:T(8,128)(2,1)S(1)}, u32[]{:S(2)}, u32[]{:S(2)}) %collective-permute-start.3) | collective-permute-done | bytes 139296 | tf_op jit(solution)/shard_map/ppermute | solution.py:460
  21.9 1.0 %shard_map.126.sums_in_ref = f32[2048,256]{1,0:T(8,128)S(1)} custom-call(bf16[1024,16]{1,0:T(8,128)(2,1)S(1)} %get-tuple-element.17.wave_ref, f32[2048,256]{1,0:T(8,128)S(1)} %shard_map.125.sums_in_ref, bf16[272,256]{1,0:T(8,128)(2,1)S(1)} %collective-permute-done.3.refs_3_.refs_0_), custom_call_target="tpu_custom_call" | custom-call | flops 990000000 | bytes 900000 | tf_op jit(solution)/shard_map/pallas_call | solution.py:495
  22.9 0.7 %collective-permute-done.7.refs_0_ = bf16[272,256]{1,0:T(8,128)(2,1)S(1)} collective-permute-done((bf16[272,256]{1,0:T(8,128)(2,1)S(1)}, bf16[272,256]{1,0:T(8,128)(2,1)S(1)}, u32[]{:S(2)}, u32[]{:S(2)}) %collective-permute-start.7) | collective-permute-done | bytes 139296 | tf_op jit(solution)/shard_map/ppermute | solution.py:460
  23.6 0.0 collective-permute-done.8.refs_1_
  23.6 1.0 %shard_map.128.others_ref = bf16[1024,256]{1,0:T(8,128)(2,1)S(1)} custom-call(bf16[1024,16]{1,0:T(8,128)(2,1)S(1)} %get-tuple-element.17.wave_ref, f32[2048,256]{1,0:T(8,128)S(1)} %shard_map.126.sums_in_ref, f32[1024,256]{1,0:T(8,128)S(1)} %get-tuple-element.20.weights_ref, bf16[272,256]{1,0:T(8,128)(2,1)S(1)} %collective-permute-done.7.refs_0_, ...), custom_call_target="tpu_custom_call" | custom-call | flops 1100000000 | bytes 1000000 | tf_op jit(solution)/shard_map/pallas_call | solution.py:506
  24.6 0.0 copy-start.1
  24.6 0.0 copy-start.2
  24.6 0.0 copy-start.3
  24.6 0.1 collective-permute-start.9
  24.7 1.0 %shard_map.127.mine_ref = bf16[1024,256]{1,0:T(8,128)(2,1)S(1)} custom-call(bf16[1024,16]{1,0:T(8,128)(2,1)S(1)} %get-tuple-element.17.wave_ref, f32[2048,256]{1,0:T(8,128)S(1)} %shard_map.126.sums_in_ref, f32[1024,256]{1,0:T(8,128)S(1)} %get-tuple-element.20.weights_ref, bf16[272,256]{1,0:T(8,128)(2,1)S(1)} %collective-permute-done.7.refs_0_, ...), custom_call_target="tpu_custom_call" | custom-call | flops 1100000000 | bytes 1000000 | tf_op jit(solution)/shard_map/pallas_call | solution.py:506
  25.7 0.6 %collective-permute-start.10 = (bf16[1024,256]{1,0:T(8,128)(2,1)S(1)}, bf16[1024,256]{1,0:T(8,128)(2,1)S(1)}, u32[]{:S(2)}, u32[]{:S(2)}) collective-permute-start(bf16[1024,256]{1,0:T(8,128)(2,1)S(1)} %shard_map.127.mine_ref), channel_id=1, source_target_pairs={{0,1},{1,0},{2,3},{3,2},{4,5},{5,4},{6,7},{7,6},{8,9},{9,8},{10,11... | collective-permute-start | bytes 1572872 | tf_op jit(solution)/shard_map/ppermute | solution.py:455
  26.3 0.2 shard_map.122
  26.5 0.1 collective-permute-start.4
  26.6 0.0 copy-done.1
  26.6 0.0 copy-done.2
  26.6 1.9 %shard_map.121 = (f32[256,256]{1,0:T(8,128)S(1)}, bf16[4096,512]{1,0:T(8,128)(2,1)S(1)}) custom-call(f32[256,768]{1,0:T(8,128)S(1)} %copy-done.2, s32[256,768]{1,0:T(8,128)S(1)} %copy-done.3, f32[16,256]{1,0:T(8,128)S(1)} %copy-done.1, bf16[272,256]{1,0:T(8,128)(2,1)S(1)} %shard_map.120.own_ref.refs_0_), custom_call_target="tpu_custom_call" | custom-call | flops 2750000128 | bytes 2500000 | tf_op jit(solution)/shard_map/pallas_call | solution.py:472
  28.5 0.0 collective-permute-done.4.side_ref
  28.5 0.0 copy-start.5
  28.5 0.0 copy-start.6
  28.5 0.0 copy-start.10
  28.5 1.5 %shard_map.129.combined_ref = f32[256,256]{1,0:T(8,128)S(1)} custom-call(f32[256,256]{1,0:T(8,128)S(1)} %get-tuple-element.15.near_in_ref, bf16[4096,512]{1,0:T(8,128)(2,1)S(1)} %get-tuple-element.16.far_tiles_ref, f32[16,256]{1,0:T(8,128)S(1)} %copy-done.1, bf16[512,256]{1,0:T(8,128)(2,1)S(1)} %collective-permute-done.4.side_ref, ...), custom_call_target="tpu_custom_call" | custom-call | flops 1650000000 | bytes 1500000 | tf_op jit(solution)/shard_map/pallas_call | solution.py:516
  30.1 0.0 collective-permute-done.9.mine_ref
  30.1 0.0 collective-permute-done.10.others_ref
  30.1 1.5 %shard_map.130 = bf16[256,256]{1,0:T(8,128)(2,1)} custom-call(s32[8,128]{1,0:T(8,128)S(1)} %shard_map.119.count_ref, f32[256,256]{1,0:T(8,128)S(1)} %shard_map.129.combined_ref, bf16[1024,256]{1,0:T(8,128)(2,1)S(1)} %collective-permute-done.9.mine_ref, bf16[1024,256]{1,0:T(8,128)(2,1)S(1)} %collective-permute-done.10.others_ref, ...), custom_call_target="tpu_custom_call" | custom-call | flops 1100000000 | bytes 1000000 | tf_op jit(solution)/shard_map/pallas_call | solution.py:523
  (9 shorter events, 0.0 us)
Async XLA Ops:
  0.0 0.9 %copy-start = (bf16[256,256]{1,0:T(8,128)(2,1)S(1)}, bf16[256,256]{1,0:T(8,128)(2,1)}, u32[]{:S(2)}) copy-start(bf16[256,256]{1,0:T(8,128)(2,1)} %features_ref.1) | copy-start | bytes 393220
  0.0 1.0 %copy-start.4 = (bf16[256,256]{1,0:T(8,128)(2,1)S(1)}, bf16[256,256]{1,0:T(8,128)(2,1)}, u32[]{:S(2)}) copy-start(bf16[256,256]{1,0:T(8,128)(2,1)} %w_value.1) | copy-start | bytes 393220
  0.0 1.0 %copy-start.9 = (f32[3,256]{1,0:T(4,128)S(1)}, f32[3,256]{1,0:T(4,128)}, u32[]{:S(2)}) copy-start(f32[3,256]{1,0:T(4,128)} %positions.1) | copy-start | bytes 9220
  0.7 6.1 %copy-start.8 = (s32[3,512]{1,0:T(4,128)S(1)}, s32[3,512]{1,0:T(4,128)}, u32[]{:S(2)}) copy-start(s32[3,512]{1,0:T(4,128)} %own_wave_ref.1) | copy-start | bytes 18436
  0.7 8.1 %copy-start.7 = (f32[16,256]{1,0:T(8,128)S(1)}, f32[16,256]{1,0:T(8,128)}, u32[]{:S(2)}) copy-start(f32[16,256]{1,0:T(8,128)} %filter_long_ref.1) | copy-start | bytes 49156
  1.2 10.9 %collective-permute-start.2 = (bf16[272,256]{1,0:T(8,128)(2,1)S(1)}, bf16[272,256]{1,0:T(8,128)(2,1)S(1)}, u32[]{:S(2)}, u32[]{:S(2)}) collective-permute-start(bf16[272,256]{1,0:T(8,128)(2,1)S(1)} %shard_map.120.own_ref.refs_0_), channel_id=1, source_target_pairs={{0,8},{1,9},{2,10},{3,11},{4,12},{5,13},{6,14},{7,15},{8,0},{9,1},... | collective-permute-start | bytes 417800 | tf_op jit(solution)/shard_map/ppermute | solution.py:452
  5.3 9.8 %collective-permute-start = (bf16[272,256]{1,0:T(8,128)(2,1)S(1)}, bf16[272,256]{1,0:T(8,128)(2,1)S(1)}, u32[]{:S(2)}, u32[]{:S(2)}) collective-permute-start(bf16[272,256]{1,0:T(8,128)(2,1)S(1)} %shard_map.120.own_ref.refs_0_), channel_id=1, source_target_pairs={{0,2},{1,3},{2,0},{3,1},{4,6},{5,7},{6,4},{7,5},{8,10},{9,11},{10,... | collective-permute-start | bytes 417800 | tf_op jit(solution)/shard_map/ppermute | solution.py:452
  6.8 2.0 %collective-permute-start.5 = (s32[3,512]{1,0:T(4,128)S(1)}, s32[3,512]{1,0:T(4,128)S(1)}, u32[]{:S(2)}, u32[]{:S(2)}) collective-permute-start(s32[3,512]{1,0:T(4,128)S(1)} %copy-done.8), channel_id=1, source_target_pairs={{0,1},{1,0},{2,3},{3,2},{4,5},{5,4},{6,7},{7,6},{8,9},{9,8},{10,11... | collective-permute-start | bytes 18440 | tf_op jit(solution)/shard_map/ppermute | solution.py:455
  6.8 11.2 %collective-permute-start.1 = (bf16[272,256]{1,0:T(8,128)(2,1)S(1)}, bf16[272,256]{1,0:T(8,128)(2,1)S(1)}, u32[]{:S(2)}, u32[]{:S(2)}) collective-permute-start(bf16[272,256]{1,0:T(8,128)(2,1)S(1)} %shard_map.120.own_ref.refs_0_), channel_id=1, source_target_pairs={{0,6},{1,7},{2,4},{3,5},{4,2},{5,3},{6,0},{7,1},{8,14},{9,15},{10,... | collective-permute-start | bytes 417800 | tf_op jit(solution)/shard_map/ppermute | solution.py:452
  8.4 9.7 %collective-permute-start.6 = (bf16[272,256]{1,0:T(8,128)(2,1)S(1)}, bf16[272,256]{1,0:T(8,128)(2,1)S(1)}, u32[]{:S(2)}, u32[]{:S(2)}) collective-permute-start(bf16[272,256]{1,0:T(8,128)(2,1)S(1)} %shard_map.120.own_ref.refs_0_), channel_id=1, source_target_pairs={{0,4},{1,5},{2,6},{3,7},{4,0},{5,1},{6,2},{7,3},{8,12},{9,13},{10,... | collective-permute-start | bytes 417800 | tf_op jit(solution)/shard_map/ppermute | solution.py:452
  12.1 9.8 %collective-permute-start.3 = (bf16[272,256]{1,0:T(8,128)(2,1)S(1)}, bf16[272,256]{1,0:T(8,128)(2,1)S(1)}, u32[]{:S(2)}, u32[]{:S(2)}) collective-permute-start(bf16[272,256]{1,0:T(8,128)(2,1)S(1)} %collective-permute-done.2.refs_2_), channel_id=1, source_target_pairs={{0,6},{1,7},{2,4},{3,5},{4,2},{5,3},{6,0},{7,1},{8,14},{9,15},{10,... | collective-permute-start | bytes 417800 | tf_op jit(solution)/shard_map/ppermute | solution.py:460
  13.7 9.9 %collective-permute-start.7 = (bf16[272,256]{1,0:T(8,128)(2,1)S(1)}, bf16[272,256]{1,0:T(8,128)(2,1)S(1)}, u32[]{:S(2)}, u32[]{:S(2)}) collective-permute-start(bf16[272,256]{1,0:T(8,128)(2,1)S(1)} %collective-permute-done.2.refs_2_), channel_id=1, source_target_pairs={{0,4},{1,5},{2,6},{3,7},{4,0},{5,1},{6,2},{7,3},{8,12},{9,13},{10,... | collective-permute-start | bytes 417800 | tf_op jit(solution)/shard_map/ppermute | solution.py:460
  15.1 8.5 %collective-permute-start.8 = (bf16[272,256]{1,0:T(8,128)(2,1)S(1)}, bf16[272,256]{1,0:T(8,128)(2,1)S(1)}, u32[]{:S(2)}, u32[]{:S(2)}) collective-permute-start(bf16[272,256]{1,0:T(8,128)(2,1)S(1)} %collective-permute-done.2.refs_2_), channel_id=1, source_target_pairs={{0,2},{1,3},{2,0},{3,1},{4,6},{5,7},{6,4},{7,5},{8,10},{9,11},{10,... | collective-permute-start | bytes 417800 | tf_op jit(solution)/shard_map/ppermute | solution.py:460
  24.6 2.0 %copy-start.1 = (f32[16,256]{1,0:T(8,128)S(1)}, f32[16,256]{1,0:T(8,128)}, u32[]{:S(2)}) copy-start(f32[16,256]{1,0:T(8,128)} %filter_ref.3) | copy-start | bytes 49156
  24.6 2.0 %copy-start.2 = (f32[256,768]{1,0:T(8,128)S(1)}, f32[256,768]{1,0:T(8,128)}, u32[]{:S(2)}) copy-start(f32[256,768]{1,0:T(8,128)} %distances_ref.1) | copy-start | bytes 2359300
  24.6 2.0 %copy-start.3 = (s32[256,768]{1,0:T(8,128)S(1)}, s32[256,768]{1,0:T(8,128)}, u32[]{:S(2)}) copy-start(s32[256,768]{1,0:T(8,128)} %mask_ref.1) | copy-start | bytes 2359300
  24.6 5.5 %collective-permute-start.9 = (bf16[1024,256]{1,0:T(8,128)(2,1)S(1)}, bf16[1024,256]{1,0:T(8,128)(2,1)S(1)}, u32[]{:S(2)}, u32[]{:S(2)}) collective-permute-start(bf16[1024,256]{1,0:T(8,128)(2,1)S(1)} %shard_map.128.others_ref), channel_id=1, source_target_pairs={{0,1},{1,0},{2,3},{3,2},{4,5},{5,4},{6,7},{7,6},{8,9},{9,8},{10,11... | collective-permute-start | bytes 1572872 | tf_op jit(solution)/shard_map/ppermute | solution.py:455
  25.7 4.4 %collective-permute-start.10 = (bf16[1024,256]{1,0:T(8,128)(2,1)S(1)}, bf16[1024,256]{1,0:T(8,128)(2,1)S(1)}, u32[]{:S(2)}, u32[]{:S(2)}) collective-permute-start(bf16[1024,256]{1,0:T(8,128)(2,1)S(1)} %shard_map.127.mine_ref), channel_id=1, source_target_pairs={{0,1},{1,0},{2,3},{3,2},{4,5},{5,4},{6,7},{7,6},{8,9},{9,8},{10,11... | collective-permute-start | bytes 1572872 | tf_op jit(solution)/shard_map/ppermute | solution.py:455
  26.5 2.0 %collective-permute-start.4 = (bf16[512,256]{1,0:T(8,128)(2,1)S(1)}, bf16[512,256]{1,0:T(8,128)(2,1)S(1)}, u32[]{:S(2)}, u32[]{:S(2)}) collective-permute-start(bf16[512,256]{1,0:T(8,128)(2,1)S(1)} %shard_map.122), channel_id=1, source_target_pairs={{0,1},{1,0},{2,3},{3,2},{4,5},{5,4},{6,7},{7,6},{8,9},{9,8},{10,11... | collective-permute-start | bytes 786440 | tf_op jit(solution)/shard_map/ppermute | solution.py:455
  28.5 1.6 %copy-start.5 = (bf16[256,256]{1,0:T(8,128)(2,1)S(1)}, bf16[256,256]{1,0:T(8,128)(2,1)}, u32[]{:S(2)}) copy-start(bf16[256,256]{1,0:T(8,128)(2,1)} %w_inner_ref.1) | copy-start | bytes 393220
  28.5 1.6 %copy-start.6 = (bf16[256,256]{1,0:T(8,128)(2,1)S(1)}, bf16[256,256]{1,0:T(8,128)(2,1)}, u32[]{:S(2)}) copy-start(bf16[256,256]{1,0:T(8,128)(2,1)} %w_outer_ref.1) | copy-start | bytes 393220
  28.5 1.6 %copy-start.10 = (f32[256]{0:T(256)S(1)}, f32[256]{0:T(256)}, u32[]{:S(2)}) copy-start(f32[256]{0:T(256)} %param.21) | copy-start | bytes 3076
